TPU v7x, 32 devices: a whole 2x2x4 slice. The times are simulated.
32 devices in a mesh: fsdp: 4 (over y, x), context: 4 (over z), tensor: 2 (over core).
Axes of the slice: x: 2, y: 2, z: 4, core: 2. Of those that a mesh axis runs over, the one named last changes fastest.
Arguments:
- tokens: bfloat16 [4096, 1024], P(('fsdp', 'context')), may hold values from -6 to 6
- lengths: int32 [4, 4], P('fsdp'), may hold values from 1 to 896, 1024 in all within a row
- deal: int32 [4, 1024], P('fsdp', 'context'), may hold values from 0 to 1023, as said below
- attn_norm_gain: float32 [1024], replicated, may hold values from 0.5 to 1.5
- ff_norm_gain: float32 [1024], replicated, may hold values from 0.5 to 1.5
- w_query: bfloat16 [1024, 512], P('fsdp', 'tensor'), may hold values from -0.1875 to 0.1875
- w_key: bfloat16 [1024, 128], P('fsdp', 'tensor'), may hold values from -0.1875 to 0.1875
- w_value: bfloat16 [1024, 128], P('fsdp', 'tensor'), may hold values from -0.1875 to 0.1875
- w_attn_out: bfloat16 [1024, 512], P('fsdp', 'tensor'), may hold values from -2 to 2
- w_gate_z: bfloat16 [1024, 1536], P('fsdp', 'tensor'), may hold values from -0.1875 to 0.1875
- w_ssm_in: bfloat16 [1024, 1536], P('fsdp', 'tensor'), may hold values from -0.1875 to 0.1875
- w_bc: bfloat16 [1024, 256], P('fsdp'), may hold values from -0.1875 to 0.1875
- w_step: bfloat16 [1024, 24], P('fsdp', 'tensor'), may hold values from -0.1875 to 0.1875
- w_ssm_out: bfloat16 [1024, 1536], P('fsdp', 'tensor'), may hold values from -0.15625 to 0.15625
- conv_ssm: float32 [1536, 4], P('tensor'), may hold values from -3 to 3
- conv_bc: float32 [256, 4], replicated, may hold values from -3 to 3
- step_bias: float32 [24], P('tensor'), may hold values from -2 to 1
- decay_log: float32 [24], P('tensor'), may hold values from -8 to 0
- skip_gain: float32 [24], P('tensor'), may hold values from 0.5 to 1.5
- ssm_norm_gain: float32 [1536], P('tensor'), may hold values from 0.5 to 1.5
- w_gate: bfloat16 [1024, 2048], P('fsdp', 'tensor'), may hold values from -0.1875 to 0.1875
- w_up: bfloat16 [1024, 2048], P('fsdp', 'tensor'), may hold values from -0.1875 to 0.1875
- w_down: bfloat16 [1024, 2048], P('fsdp', 'tensor'), may hold values from -0.125 to 0.125
- cotangent: bfloat16 [4096, 1024], P(('fsdp', 'context')), may hold values from -6 to 6
Outputs:
- output: bfloat16 [4096, 1024], P(('fsdp', 'context'))
- input_grad: float32 [4096, 1024], P(('fsdp', 'context'))
- grad_attn_norm_gain: float32 [1024], replicated
- grad_ff_norm_gain: float32 [1024], replicated
- grad_w_query: float32 [1024, 512], P('fsdp', 'tensor')
- grad_w_key: float32 [1024, 128], P('fsdp', 'tensor')
- grad_w_value: float32 [1024, 128], P('fsdp', 'tensor')
- grad_w_attn_out: float32 [1024, 512], P('fsdp', 'tensor')
- grad_w_gate_z: float32 [1024, 1536], P('fsdp', 'tensor')
- grad_w_ssm_in: float32 [1024, 1536], P('fsdp', 'tensor')
- grad_w_bc: float32 [1024, 256], P('fsdp')
- grad_w_step: float32 [1024, 24], P('fsdp', 'tensor')
- grad_w_ssm_out: float32 [1024, 1536], P('fsdp', 'tensor')
- grad_conv_ssm: float32 [1536, 4], P('tensor')
- grad_conv_bc: float32 [256, 4], replicated
- grad_step_bias: float32 [24], P('tensor')
- grad_decay_log: float32 [24], P('tensor')
- grad_skip_gain: float32 [24], P('tensor')
- grad_ssm_norm_gain: float32 [1536], P('tensor')
- grad_w_gate: float32 [1024, 2048], P('fsdp', 'tensor')
- grad_w_up: float32 [1024, 2048], P('fsdp', 'tensor')
- grad_w_down: float32 [1024, 2048], P('fsdp', 'tensor')
- rms_stats: float32 [3], replicated
Inputs may be any that keep to these rules, and one draw needn't show every extreme that they name: Row g lists in order the lengths of the 4 sequences packed into token group g; each row sums to 1024 and its largest entry is 896. With P = 256 / 4 and one shift s of 0 to 4 - 1 for each group, row d * 256 + j * P + i of group g (j < 4, i < P) holds place j * 256 + ((d + s) mod 4) * P + i; each row of deal is a permutation of the group's places.
All inputs are finite; a program needn't handle non-finite values.
Results may differ from a plain program's by a relative error of at most 0.019.
Values may be sent and summed in bfloat16 or wider, within the bound.
A program may use at most 192 MiB of HBM per device.

v0:
```python
import jax
import jax.numpy as jnp
from jax import lax
from jax.sharding import PartitionSpec as P

D = 1024
QUERY_HEADS = 8
HEAD_WIDTH = 64
SPACE_HEADS = 24
SPACE_HEAD_WIDTH = 64
STATE_WIDTH = 128
KC = 4
DI = 1536


epsilon = 1e-06
rope_base = 100000000000.0
masked_value = -1e30
highest = lax.Precision.HIGHEST


def passed_along(block, axis, distance):
    devices = range(lax.axis_size(axis))
    route = [(i - distance, i) for i in devices if i - distance in devices]
    return lax.ppermute(block, axis, route)


def matmul_low(left, right):
    return jnp.dot(left, right, preferred_element_type=jnp.float32)


def matmul_tn(left, right):
    return lax.dot_general(
        left, right, (((0,), (0,)), ((), ())), preferred_element_type=jnp.float32
    )


def matmul_nt(left, right):
    return lax.dot_general(
        left, right, (((1,), (1,)), ((), ())), preferred_element_type=jnp.float32
    )


def segments_of(lengths_row, positions):
    ends = jnp.cumsum(lengths_row)
    seg_ids = jnp.sum((positions[:, None] >= ends[None, :]).astype(jnp.int32), axis=1)
    starts = jnp.max(jnp.where(ends[None, :] <= positions[:, None], ends[None, :], 0), axis=1)
    return (seg_ids, starts)


def apply_rotary(value_matrix, sequence_position, head_list, sign):
    half_width = value_matrix.shape[-1] // (2 * head_list)
    freqs = rope_base ** (-jnp.arange(half_width, dtype=jnp.float32) / half_width)
    angles = sequence_position.astype(jnp.float32)[:, None] * freqs[None, :]
    cosine = jnp.cos(angles)[:, None, :]
    sine_part = sign * jnp.sin(angles)[:, None, :]
    shaped = value_matrix.reshape(value_matrix.shape[0], head_list, 2 * half_width)
    first_part = shaped[..., :half_width]
    second_part = shaped[..., half_width:]
    turned = jnp.concatenate(
        [
            first_part * cosine - second_part * sine_part,
            second_part * cosine + first_part * sine_part,
        ],
        axis=-1,
    )
    return turned.reshape(value_matrix.shape)


def causal_conv(extended, conv_weight, seg_extended, segment_rows):
    count_of_rows = segment_rows.shape[0]
    summed = jnp.zeros((count_of_rows, extended.shape[1]), jnp.float32)
    for offset in range(conv_weight.shape[1]):
        window = extended[offset : offset + count_of_rows]
        keep_mask = (seg_extended[offset : offset + count_of_rows] == segment_rows).astype(
            jnp.float32
        )
        summed = summed + window * keep_mask[:, None] * conv_weight[:, offset][None, :]
    return jax.nn.silu(summed)


def ssd_local(
    scan_inputs,
    input_matrix,
    output_matrix,
    step_size,
    rate,
    skip_gain,
    segment_rows,
    segment_before,
):
    count_of_rows = segment_rows.shape[0]
    log_decay = step_size * rate[None, :]
    cumulative = jnp.cumsum(log_decay, axis=0)
    order = jnp.arange(count_of_rows, dtype=jnp.int32)
    joined = (segment_rows[:, None] == segment_rows[None, :]) & (order[:, None] >= order[None, :])
    differ = cumulative.T[:, :, None] - cumulative.T[:, None, :]
    within = jnp.exp(jnp.where(joined[None], differ, masked_value))
    intersection = jnp.dot(
        output_matrix, input_matrix.T, precision=highest, preferred_element_type=jnp.float32
    )
    scaled = scan_inputs * step_size[:, :, None]
    local_out = jnp.einsum("hts,shp->thp", within * intersection[None], scaled, precision=highest)
    fresh = (segment_rows == segment_before).astype(jnp.float32)
    carry_gain = fresh[:, None] * jnp.exp(cumulative)
    tail = (segment_rows == segment_rows[count_of_rows - 1]).astype(jnp.float32)[:, None] * jnp.exp(
        cumulative[count_of_rows - 1][None, :] - cumulative
    )
    fresh_state = jnp.einsum("sh,shp,sn->hpn", tail, scaled, input_matrix, precision=highest)
    whole_decay = carry_gain[count_of_rows - 1]
    local_out = local_out + skip_gain[None, :, None] * scan_inputs
    return (local_out, carry_gain, whole_decay, fresh_state)


def mixer_local(
    extended,
    conv_weight,
    step_raw,
    step_bias,
    decay_log,
    skip_gain,
    seg_extended,
    segment_rows,
    segment_before,
    head_list,
):
    active_rows = causal_conv(extended, conv_weight, seg_extended, segment_rows)
    inner_width = head_list * SPACE_HEAD_WIDTH
    scan_inputs = active_rows[:, :inner_width].reshape(
        active_rows.shape[0], head_list, SPACE_HEAD_WIDTH
    )
    input_matrix = active_rows[:, inner_width : inner_width + STATE_WIDTH]
    output_matrix = active_rows[:, inner_width + STATE_WIDTH :]
    step_size = jax.nn.softplus(step_raw + step_bias[None, :])
    rate = -jnp.exp(decay_log)
    local_out, carry_gain, whole_decay, fresh_state = ssd_local(
        scan_inputs,
        input_matrix,
        output_matrix,
        step_size,
        rate,
        skip_gain,
        segment_rows,
        segment_before,
    )
    return (local_out, carry_gain, output_matrix, whole_decay, fresh_state)


def carry_states(decay, state_term, reverse):
    direction = -1 if reverse else 1

    def relay(step_index, incoming):
        outgoing = decay[:, None, None] * incoming + state_term
        return passed_along(outgoing, "context", direction)

    return lax.fori_loop(0, lax.axis_size("context") - 1, relay, jnp.zeros_like(state_term))


def over_tensor(value_matrix):
    return lax.psum(value_matrix, "tensor")


def per_device(
    tokens,
    lengths,
    deal,
    attn_norm_gain,
    ff_norm_gain,
    w_query,
    w_key,
    w_value,
    w_attn_out,
    w_gate_z,
    w_ssm_in,
    w_bc,
    w_step,
    w_ssm_out,
    conv_ssm,
    conv_bc,
    step_bias,
    decay_log,
    skip_gain,
    ssm_norm_gain,
    w_gate,
    w_up,
    w_down,
    cotangent,
):
    count_of_rows = tokens.shape[0]
    contexts = lax.axis_size("context")
    group_row_list = count_of_rows * contexts
    tensors = lax.axis_size("tensor")
    query_heads = QUERY_HEADS // tensors
    space_head_list = SPACE_HEADS // tensors
    inner_width_local = space_head_list * SPACE_HEAD_WIDTH
    score_scale = HEAD_WIDTH ** (-0.5)
    piece_rows = count_of_rows // contexts
    shift_amount = (deal[0, 0] // piece_rows - lax.axis_index("context")) % contexts
    dealt_tokens, dealt_cot = (
        lax.all_to_all(tokens, "context", split_axis=0, concat_axis=0, tiled=True),
        lax.all_to_all(cotangent, "context", split_axis=0, concat_axis=0, tiled=True),
    )
    tokens_placed = jnp.roll(
        dealt_tokens.reshape(contexts, piece_rows, D), shift_amount, axis=0
    ).reshape(count_of_rows, D)
    cot_placed = jnp.roll(dealt_cot.reshape(contexts, piece_rows, D), shift_amount, axis=0).reshape(
        count_of_rows, D
    )
    (
        full_query,
        full_key,
        full_value,
        full_attn_out,
        full_gate_z,
        full_ssm_in,
        full_bc,
        full_step,
        full_ssm_out,
        full_gate,
        full_up,
        full_down,
    ) = (
        lax.all_gather(w_query, "fsdp", axis=0, tiled=True),
        lax.all_gather(w_key, "fsdp", axis=0, tiled=True),
        lax.all_gather(w_value, "fsdp", axis=0, tiled=True),
        lax.all_gather(w_attn_out, "fsdp", axis=0, tiled=True),
        lax.all_gather(w_gate_z, "fsdp", axis=0, tiled=True),
        lax.all_gather(w_ssm_in, "fsdp", axis=0, tiled=True),
        lax.all_gather(w_bc, "fsdp", axis=0, tiled=True),
        lax.all_gather(w_step, "fsdp", axis=0, tiled=True),
        lax.all_gather(w_ssm_out, "fsdp", axis=0, tiled=True),
        lax.all_gather(w_gate, "fsdp", axis=0, tiled=True),
        lax.all_gather(w_up, "fsdp", axis=0, tiled=True),
        lax.all_gather(w_down, "fsdp", axis=0, tiled=True),
    )
    w_inputs = jnp.concatenate(
        [full_query, full_key, full_value, full_gate_z, full_ssm_in, full_bc, full_step], axis=1
    )
    query_end = query_heads * HEAD_WIDTH
    key_end = query_end + HEAD_WIDTH
    value_end = key_end + HEAD_WIDTH
    gate_end = value_end + inner_width_local
    ssm_end = gate_end + inner_width_local
    bc_end = ssm_end + 2 * STATE_WIDTH
    step_end = bc_end + space_head_list
    offset_rows = lax.axis_index("context") * count_of_rows
    positions = offset_rows + jnp.arange(count_of_rows, dtype=jnp.int32)
    lengths_row = lengths[0]
    segment_rows, starts = segments_of(lengths_row, positions)
    sequence_position = positions - starts
    ext_positions = offset_rows - (KC - 1) + jnp.arange(count_of_rows + KC - 1, dtype=jnp.int32)
    seg_extended, ext_starts = segments_of(lengths_row, ext_positions)
    segment_before = jnp.where(offset_rows > 0, seg_extended[KC - 2], -1)
    tokens_f = tokens_placed.astype(jnp.float32)
    inv_first = lax.rsqrt(jnp.mean(tokens_f * tokens_f, axis=-1, keepdims=True) + epsilon)
    scaled_first = tokens_f * inv_first
    normed = (scaled_first * attn_norm_gain).astype(jnp.bfloat16)
    projected = matmul_low(normed, w_inputs)
    query_pre = projected[:, :query_end]
    key_before_rotary = projected[:, query_end:key_end]
    value_low = projected[:, key_end:value_end].astype(jnp.bfloat16)
    gate_z = projected[:, value_end:gate_end]
    conv_in = projected[:, gate_end:bc_end].astype(jnp.bfloat16)
    step_raw = projected[:, bc_end:step_end]
    query_rot = apply_rotary(query_pre, sequence_position, query_heads, 1.0).astype(jnp.bfloat16)
    key_rot = apply_rotary(key_before_rotary, sequence_position, 1, 1.0).astype(jnp.bfloat16)
    key_value = lax.all_gather(
        jnp.concatenate([key_rot, value_low], axis=1), "context", axis=0, tiled=True
    )
    query_matrix = (
        query_rot.reshape(count_of_rows, query_heads, HEAD_WIDTH)
        .transpose(1, 0, 2)
        .reshape(query_heads * count_of_rows, HEAD_WIDTH)
    )
    query_pos = jnp.tile(positions, query_heads)
    query_start = jnp.tile(starts, query_heads)
    query_rows = query_heads * count_of_rows
    block_row_list = min(512, group_row_list)
    block_count = group_row_list // block_row_list
    block_ids = jnp.arange(block_count, dtype=jnp.int32)

    def block_scores(block_index):
        block_first_row = block_index * block_row_list
        kv_piece = lax.dynamic_slice_in_dim(key_value, block_first_row, block_row_list, 0)
        key_pos = block_first_row + jnp.arange(block_row_list, dtype=jnp.int32)
        allowed = (key_pos[None, :] <= query_pos[:, None]) & (
            key_pos[None, :] >= query_start[:, None]
        )
        raw_scores = matmul_nt(query_matrix, kv_piece[:, :HEAD_WIDTH]) * score_scale
        return (kv_piece, allowed, raw_scores)

    def needed(block_index):
        block_first_row = block_index * block_row_list
        return (block_first_row <= positions[count_of_rows - 1]) & (
            block_first_row + block_row_list - 1 >= starts[0]
        )

    def max_step(carry, block_index):

        def max_compute(state_pair):
            running_max, running_sum = state_pair
            kv_piece, allowed, raw_scores = block_scores(block_index)
            masked = jnp.where(allowed, raw_scores, masked_value)
            new_max = jnp.maximum(running_max, jnp.max(masked, axis=1))
            exps = jnp.where(allowed, jnp.exp(masked - new_max[:, None]), 0.0)
            return (new_max, running_sum * jnp.exp(running_max - new_max) + jnp.sum(exps, axis=1))

        return (
            lax.cond(needed(block_index), max_compute, lambda state_pair: state_pair, carry),
            None,
        )

    start_pair = (
        jnp.full((query_rows,), masked_value, jnp.float32),
        jnp.zeros((query_rows,), jnp.float32),
    )
    (running_max, running_sum), unused_max = lax.scan(max_step, start_pair, block_ids)
    log_sum = running_max + jnp.log(running_sum)

    def out_step(summed, block_index):

        def out_compute(partial_sum):
            kv_piece, allowed, raw_scores = block_scores(block_index)
            prob_values = jnp.where(allowed, jnp.exp(raw_scores - log_sum[:, None]), 0.0)
            return partial_sum + matmul_low(
                prob_values.astype(jnp.bfloat16), kv_piece[:, HEAD_WIDTH:]
            )

        return (
            lax.cond(needed(block_index), out_compute, lambda partial_sum: partial_sum, summed),
            None,
        )

    attn_rows, unused_out = lax.scan(
        out_step, jnp.zeros((query_rows, HEAD_WIDTH), jnp.float32), block_ids
    )
    attended = (
        attn_rows.reshape(query_heads, count_of_rows, HEAD_WIDTH)
        .transpose(1, 0, 2)
        .reshape(count_of_rows, query_end)
        .astype(jnp.bfloat16)
    )
    attn_part = matmul_nt(attended, full_attn_out)
    halo_rows = passed_along(conv_in[count_of_rows - (KC - 1) :], "context", 1)
    extended = jnp.concatenate([halo_rows, conv_in], axis=0).astype(jnp.float32)
    conv_weight = jnp.concatenate([conv_ssm, conv_bc], axis=0)

    def mixer_piece(ext_values, conv_values, raw_steps, bias_values, decay_values, skip_values):
        return mixer_local(
            ext_values,
            conv_values,
            raw_steps,
            bias_values,
            decay_values,
            skip_values,
            seg_extended,
            segment_rows,
            segment_before,
            space_head_list,
        )

    (local_out, carry_gain, output_matrix, whole_decay, fresh_state), pullback = jax.vjp(
        mixer_piece, extended, conv_weight, step_raw, step_bias, decay_log, skip_gain
    )
    state_in = carry_states(whole_decay, fresh_state, False)
    carried = jnp.einsum("hpn,tn->thp", state_in, output_matrix, precision=highest)
    ssm_y = (local_out + carry_gain[:, :, None] * carried).reshape(count_of_rows, inner_width_local)
    silu_gate_values = jax.nn.silu(gate_z)
    gated = ssm_y * silu_gate_values
    square_sum = over_tensor(jnp.sum(gated * gated, axis=1))
    gated_inv = lax.rsqrt(square_sum / DI + epsilon)
    gated_norm = gated * gated_inv[:, None]
    mixed = (gated_norm * ssm_norm_gain).astype(jnp.bfloat16)
    ssm_part = matmul_nt(mixed, full_ssm_out)
    mixer = over_tensor(attn_part + ssm_part)
    resid = tokens_f + mixer
    inv_second = lax.rsqrt(jnp.mean(resid * resid, axis=-1, keepdims=True) + epsilon)
    scaled_second = resid * inv_second
    normed_ff = (scaled_second * ff_norm_gain).astype(jnp.bfloat16)
    gate_v = matmul_low(normed_ff, full_gate)
    up_v = matmul_low(normed_ff, full_up)
    sig_gate = jax.nn.sigmoid(gate_v)
    silu_gate = gate_v * sig_gate
    hidden = (silu_gate * up_v).astype(jnp.bfloat16)
    ff_part = over_tensor(matmul_nt(hidden, full_down))
    final = resid + ff_part
    output = final.astype(jnp.bfloat16)
    grad_final = cot_placed.astype(jnp.float32)
    grad_ff = grad_final.astype(jnp.bfloat16)
    grad_hidden = matmul_low(grad_ff, full_down)
    grad_down = matmul_tn(grad_ff, hidden)
    grad_gate = (grad_hidden * up_v * sig_gate * (1.0 + gate_v * (1.0 - sig_gate))).astype(
        jnp.bfloat16
    )
    grad_up = (grad_hidden * silu_gate).astype(jnp.bfloat16)
    grad_normed_ff = over_tensor(matmul_nt(grad_gate, full_gate) + matmul_nt(grad_up, full_up))
    grad_weight_gate = matmul_tn(normed_ff, grad_gate)
    grad_weight_up = matmul_tn(normed_ff, grad_up)
    grad_ff_gain = jnp.sum(grad_normed_ff * scaled_second, axis=0)
    grad_second = grad_normed_ff * ff_norm_gain
    grad_resid = (
        grad_final
        + inv_second * grad_second
        - resid * inv_second**3 * jnp.mean(grad_second * resid, axis=-1, keepdims=True)
    )
    grad_mixer = grad_resid.astype(jnp.bfloat16)
    grad_attended = matmul_low(grad_mixer, full_attn_out).astype(jnp.bfloat16)
    grad_attn_out = matmul_tn(grad_mixer, attended)
    grad_mixed = matmul_low(grad_mixer, full_ssm_out)
    grad_ssm_out = matmul_tn(grad_mixer, mixed)
    grad_rows = (
        grad_attended.reshape(count_of_rows, query_heads, HEAD_WIDTH)
        .transpose(1, 0, 2)
        .reshape(query_rows, HEAD_WIDTH)
    )
    row_delta = jnp.sum(grad_rows.astype(jnp.float32) * attn_rows, axis=1)

    def back_step(grad_query, block_index):

        def back_compute(partial_grad):
            kv_piece, allowed, raw_scores = block_scores(block_index)
            prob_values = jnp.where(allowed, jnp.exp(raw_scores - log_sum[:, None]), 0.0)
            grad_probs = matmul_nt(grad_rows, kv_piece[:, HEAD_WIDTH:])
            grad_scores = (prob_values * (grad_probs - row_delta[:, None])).astype(jnp.bfloat16)
            partial_grad = (
                partial_grad + matmul_low(grad_scores, kv_piece[:, :HEAD_WIDTH]) * score_scale
            )
            grad_keys = matmul_tn(grad_scores, query_matrix) * score_scale
            grad_values = matmul_tn(prob_values.astype(jnp.bfloat16), grad_rows)
            return (partial_grad, jnp.concatenate([grad_keys, grad_values], axis=1))

        def skipped(partial_grad):
            return (partial_grad, jnp.zeros((block_row_list, 2 * HEAD_WIDTH), jnp.float32))

        return lax.cond(needed(block_index), back_compute, skipped, grad_query)

    grad_query_rows, grad_kv_blocks = lax.scan(
        back_step, jnp.zeros((query_rows, HEAD_WIDTH), jnp.float32), block_ids
    )
    grad_kv = lax.psum_scatter(
        grad_kv_blocks.reshape(group_row_list, 2 * HEAD_WIDTH).astype(jnp.bfloat16),
        "context",
        scatter_dimension=0,
        tiled=True,
    ).astype(jnp.float32)
    grad_query_rot = (
        grad_query_rows.reshape(query_heads, count_of_rows, HEAD_WIDTH)
        .transpose(1, 0, 2)
        .reshape(count_of_rows, query_end)
    )
    grad_query_pre = apply_rotary(grad_query_rot, sequence_position, query_heads, -1.0).astype(
        jnp.bfloat16
    )
    grad_key_pre = apply_rotary(grad_kv[:, :HEAD_WIDTH], sequence_position, 1, -1.0).astype(
        jnp.bfloat16
    )
    grad_value = grad_kv[:, HEAD_WIDTH:].astype(jnp.bfloat16)
    sig_z = jax.nn.sigmoid(gate_z)
    grad_norm_in = grad_mixed * ssm_norm_gain
    grad_ssm_gain = jnp.sum(grad_mixed * gated_norm, axis=0)
    inner_sum = over_tensor(jnp.sum(grad_norm_in * gated, axis=1))
    gated_gradient = (
        gated_inv[:, None] * grad_norm_in - gated * (gated_inv**3 * inner_sum / DI)[:, None]
    )
    output_gradient = (gated_gradient * silu_gate_values).reshape(
        count_of_rows, space_head_list, SPACE_HEAD_WIDTH
    )
    grad_z = (gated_gradient * ssm_y * sig_z * (1.0 + gate_z * (1.0 - sig_z))).astype(jnp.bfloat16)
    grad_carry_gain = jnp.sum(output_gradient * carried, axis=2)
    weighted = carry_gain[:, :, None] * output_gradient
    grad_cmat_extra = jnp.einsum("thp,hpn->tn", weighted, state_in, precision=highest)
    back_term = jnp.einsum("thp,tn->hpn", weighted, output_matrix, precision=highest)
    grad_state_out = carry_states(whole_decay, back_term, True)
    grad_decay = jnp.sum(grad_state_out * state_in, axis=(1, 2))
    grad_ext, grad_conv, grad_step_raw, grad_bias, grad_decay_log, grad_skip = pullback(
        (output_gradient, grad_carry_gain, grad_cmat_extra, grad_decay, grad_state_out)
    )
    ext_rows = count_of_rows + KC - 1
    packed = jnp.concatenate(
        [grad_ext[:, inner_width_local:], grad_conv[inner_width_local:].T], axis=0
    )
    summed_bc = over_tensor(packed)
    grad_ext_full = jnp.concatenate([grad_ext[:, :inner_width_local], summed_bc[:ext_rows]], axis=1)
    grad_conv_bc = summed_bc[ext_rows:].T
    halo_grads = passed_along(grad_ext_full[: KC - 1], "context", -1)
    grad_conv_in = grad_ext_full[KC - 1 :] + jnp.concatenate(
        [jnp.zeros((count_of_rows - (KC - 1), grad_ext_full.shape[1]), jnp.float32), halo_grads],
        axis=0,
    )
    grad_inputs = jnp.concatenate(
        [
            grad_query_pre,
            grad_key_pre,
            grad_value,
            grad_z,
            grad_conv_in.astype(jnp.bfloat16),
            grad_step_raw.astype(jnp.bfloat16),
        ],
        axis=1,
    )
    column_scale = jnp.concatenate(
        [
            jnp.ones((ssm_end,), jnp.bfloat16),
            jnp.full((2 * STATE_WIDTH,), 0.5, jnp.bfloat16),
            jnp.ones((space_head_list,), jnp.bfloat16),
        ]
    )
    w_back = w_inputs * column_scale[None, :]
    grad_normed = over_tensor(matmul_nt(grad_inputs, w_back))
    grad_inputs_weight = matmul_tn(normed, grad_inputs)
    grad_attn_gain = jnp.sum(grad_normed * scaled_first, axis=0)
    grad_first = grad_normed * attn_norm_gain
    input_grad = (
        grad_resid
        + inv_first * grad_first
        - tokens_f * inv_first**3 * jnp.mean(grad_first * tokens_f, axis=-1, keepdims=True)
    )
    stats_part = jnp.stack(
        [jnp.sum(final * final), jnp.sum(mixer * mixer), jnp.sum(ff_part * ff_part)]
    )
    (
        stats_sum,
        sum_attn_gain,
        sum_ff_gain,
        sum_conv_ssm,
        sum_conv_bc,
        sum_bias,
        sum_decay_log,
        sum_skip,
        sum_ssm_gain,
    ) = lax.psum(
        (
            stats_part,
            grad_attn_gain,
            grad_ff_gain,
            grad_conv[:inner_width_local],
            grad_conv_bc,
            grad_bias,
            grad_decay_log,
            grad_skip,
            grad_ssm_gain,
        ),
        ("fsdp", "context"),
    )
    token_count = group_row_list * lax.axis_size("fsdp")
    rms_stats = jnp.sqrt(stats_sum / (token_count * D))
    part_query = grad_inputs_weight[:, :query_end]
    part_key = grad_inputs_weight[:, query_end:key_end]
    part_value = grad_inputs_weight[:, key_end:value_end]
    part_gate_z = grad_inputs_weight[:, value_end:gate_end]
    part_ssm_in = grad_inputs_weight[:, gate_end:ssm_end]
    part_bc = grad_inputs_weight[:, ssm_end:bc_end]
    part_step = grad_inputs_weight[:, bc_end:step_end]
    (
        rows_query,
        rows_key,
        rows_value,
        rows_attn_out,
        rows_gate_z,
        rows_ssm_in,
        rows_bc,
        rows_step,
        rows_ssm_out,
        rows_gate,
        rows_up,
        rows_down,
    ) = (
        lax.psum_scatter(
            part_query.astype(jnp.bfloat16), "fsdp", scatter_dimension=0, tiled=True
        ).astype(jnp.float32),
        lax.psum_scatter(
            part_key.astype(jnp.bfloat16), "fsdp", scatter_dimension=0, tiled=True
        ).astype(jnp.float32),
        lax.psum_scatter(
            part_value.astype(jnp.bfloat16), "fsdp", scatter_dimension=0, tiled=True
        ).astype(jnp.float32),
        lax.psum_scatter(
            grad_attn_out.astype(jnp.bfloat16), "fsdp", scatter_dimension=0, tiled=True
        ).astype(jnp.float32),
        lax.psum_scatter(
            part_gate_z.astype(jnp.bfloat16), "fsdp", scatter_dimension=0, tiled=True
        ).astype(jnp.float32),
        lax.psum_scatter(
            part_ssm_in.astype(jnp.bfloat16), "fsdp", scatter_dimension=0, tiled=True
        ).astype(jnp.float32),
        lax.psum_scatter(
            part_bc.astype(jnp.bfloat16), "fsdp", scatter_dimension=0, tiled=True
        ).astype(jnp.float32),
        lax.psum_scatter(
            part_step.astype(jnp.bfloat16), "fsdp", scatter_dimension=0, tiled=True
        ).astype(jnp.float32),
        lax.psum_scatter(
            grad_ssm_out.astype(jnp.bfloat16), "fsdp", scatter_dimension=0, tiled=True
        ).astype(jnp.float32),
        lax.psum_scatter(
            grad_weight_gate.astype(jnp.bfloat16), "fsdp", scatter_dimension=0, tiled=True
        ).astype(jnp.float32),
        lax.psum_scatter(
            grad_weight_up.astype(jnp.bfloat16), "fsdp", scatter_dimension=0, tiled=True
        ).astype(jnp.float32),
        lax.psum_scatter(
            grad_down.astype(jnp.bfloat16), "fsdp", scatter_dimension=0, tiled=True
        ).astype(jnp.float32),
    )
    (
        final_query,
        final_key,
        final_value,
        final_attn_out,
        final_gate_z,
        final_ssm_in,
        final_bc,
        final_step,
        final_ssm_out,
        final_gate,
        final_up,
        final_down,
    ) = (
        lax.psum(rows_query.astype(jnp.bfloat16), "context").astype(jnp.float32),
        lax.psum(rows_key.astype(jnp.bfloat16), "context").astype(jnp.float32),
        lax.psum(rows_value.astype(jnp.bfloat16), "context").astype(jnp.float32),
        lax.psum(rows_attn_out.astype(jnp.bfloat16), "context").astype(jnp.float32),
        lax.psum(rows_gate_z.astype(jnp.bfloat16), "context").astype(jnp.float32),
        lax.psum(rows_ssm_in.astype(jnp.bfloat16), "context").astype(jnp.float32),
        lax.psum(rows_bc.astype(jnp.bfloat16), "context").astype(jnp.float32),
        lax.psum(rows_step.astype(jnp.bfloat16), "context").astype(jnp.float32),
        lax.psum(rows_ssm_out.astype(jnp.bfloat16), "context").astype(jnp.float32),
        lax.psum(rows_gate.astype(jnp.bfloat16), "context").astype(jnp.float32),
        lax.psum(rows_up.astype(jnp.bfloat16), "context").astype(jnp.float32),
        lax.psum(rows_down.astype(jnp.bfloat16), "context").astype(jnp.float32),
    )
    return (
        output,
        input_grad,
        sum_attn_gain,
        sum_ff_gain,
        final_query,
        final_key,
        final_value,
        final_attn_out,
        final_gate_z,
        final_ssm_in,
        final_bc,
        final_step,
        final_ssm_out,
        sum_conv_ssm,
        sum_conv_bc,
        sum_bias,
        sum_decay_log,
        sum_skip,
        sum_ssm_gain,
        final_gate,
        final_up,
        final_down,
        rms_stats,
    )


def solution(mesh):
    return jax.shard_map(
        per_device,
        mesh=mesh,
        in_specs=(
            P(("fsdp", "context"), None),
            P("fsdp", None),
            P("fsdp", "context"),
            P(),
            P(),
            P("fsdp", "tensor"),
            P("fsdp", "tensor"),
            P("fsdp", "tensor"),
            P("fsdp", "tensor"),
            P("fsdp", "tensor"),
            P("fsdp", "tensor"),
            P("fsdp", None),
            P("fsdp", "tensor"),
            P("fsdp", "tensor"),
            P("tensor", None),
            P(),
            P("tensor"),
            P("tensor"),
            P("tensor"),
            P("tensor"),
            P("fsdp", "tensor"),
            P("fsdp", "tensor"),
            P("fsdp", "tensor"),
            P(("fsdp", "context"), None),
        ),
        out_specs=(
            P(("fsdp", "context"), None),
            P(("fsdp", "context"), None),
            P(),
            P(),
            P("fsdp", "tensor"),
            P("fsdp", "tensor"),
            P("fsdp", "tensor"),
            P("fsdp", "tensor"),
            P("fsdp", "tensor"),
            P("fsdp", "tensor"),
            P("fsdp", None),
            P("fsdp", "tensor"),
            P("fsdp", "tensor"),
            P("tensor", None),
            P(),
            P("tensor"),
            P("tensor"),
            P("tensor"),
            P("tensor"),
            P("fsdp", "tensor"),
            P("fsdp", "tensor"),
            P("fsdp", "tensor"),
            P(),
        ),
        check_vma=False,
    )
```

profile of v0, /device:TPU:0, one launch (start us, length us, event | category | flops | bytes accessed | tf_op | source)
XLA Modules:
  0.0 1084.3 jit_solution(7012718670229462573)
XLA Ops:
  31.5 15.3 %all_gather.44 = bf16[1024,256]{1,0:T(8,128)(2,1)S(1)} all-gather(bf16[256,256]{1,0:T(8,128)(2,1)S(1)} %copy-done.82), channel_id=1, replica_groups=mesh['fsdp'=4,'context'=4,'tensor'=2] {'fsdp'}, dimensions={0}, use_global_device_ids=true | all-gather | bytes 655360 | tf_op jit(solution)/shard_map/all_gather | solution.py:229
  154.2 35.5 %while.78 = (s32[]{:T(128)}, f32[12,64,128]{2,1,0:T(8,128)S(1)}, f32[1,12]{1,0:T(1,128)}, f32[12,64,128]{2,1,0:T(8,128)S(1)}, s32[]{:T(128)}) while((s32[]{:T(128)}, f32[12,64,128]{2,1,0:T(8,128)S(1)}, f32[1,12]{1,0:T(1,128)}, f32[12,64,128]{2,1,0:T(8,128)S(1)}, s32[]{:T(128)}) %tuple.292), condition=%wide.region_18.20_spmd, body=%wide.region_17.19_spmd.sunk | while | flops 196610 | bytes 2752661 | solution.py:156
  209.5 18.7 %all_to_all.18 = bf16[4,64,1024]{2,1,0:T(8,128)(2,1)S(1)} all-to-all(bf16[4,64,1024]{2,1,0:T(8,128)(2,1)} %bitcast.308), channel_id=1, replica_groups=mesh['fsdp'=4,'context'=4,'tensor'=2] {'context'}, dimensions={0} | all-to-all | bytes 1048576 | tf_op jit(solution)/shard_map/all_to_all | solution.py:201
  236.4 29.4 %all-gather.13.cloned.1.call-done = bf16[1024,1024]{1,0:T(8,128)(2,1)} async-done(((bf16[256,1024]{1,0:T(8,128)(2,1)}), bf16[1024,1024]{1,0:T(8,128)(2,1)}) %all-gather.13.cloned.1.call-update) | async-done | bytes 2097168 | tf_op jit(solution)/shard_map/all_gather | solution.py:232
  269.2 33.6 %all-gather.15.cloned.1.call-done = bf16[1024,1024]{1,0:T(8,128)(2,1)} async-done(((bf16[256,1024]{1,0:T(8,128)(2,1)}), bf16[1024,1024]{1,0:T(8,128)(2,1)}) %all-gather.15.cloned.1.call-update) | async-done | bytes 2097168 | tf_op jit(solution)/shard_map/all_gather | solution.py:233
  313.2 20.5 %all-reduce.31.cloned.1.call-done = (f32[256,1024]{1,0:T(8,128)}, f32[256,1024]{1,0:T(8,128)}) async-done(((f32[256,1024]{1,0:T(8,128)}, f32[256,1024]{1,0:T(8,128)}), (f32[256,1024]{1,0:T(8,128)}, f32[256,1024]{1,0:T(8,128)})) %all-reduce.31.cloned.1.call-update) | async-done | bytes 2097168 | tf_op jit(solution)/shard_map/psum | solution.py:160
  352.1 42.4 %while.79 = (s32[]{:T(128)}, f32[12,64,128]{2,1,0:T(8,128)S(1)}, f32[1,12]{1,0:T(1,128)}, f32[12,64,128]{2,1,0:T(8,128)S(1)}, s32[]{:T(128)}) while((s32[]{:T(128)}, f32[12,64,128]{2,1,0:T(8,128)S(1)}, f32[1,12]{1,0:T(1,128)}, f32[12,64,128]{2,1,0:T(8,128)S(1)}, s32[]{:T(128)}) %tuple.298), condition=%wide.region_36.38_spmd, body=%wide.region_35.37_spmd.sunk | while | flops 196610 | bytes 2752661 | solution.py:156
  427.0 15.7 %while.82 = (s32[]{:T(128)}, f32[1024,64]{0,1:T(8,128)S(1)}, bf16[2,512,128]{1,2,0:T(8,128)(2,1)}, s32[2]{0:T(128)}, s32[256]{0:T(256)S(1)}, /*index=5*/s32[256]...) while((s32[]{:T(128)}, f32[1024,64]{0,1:T(8,128)S(1)}, ...), condition=%wide.region_30.32_spmd.clone.clone, body=%wide.region_27.31_spmd.clone.clone.sunk | while | flops 341246464 | bytes 13286321 | solution.py:437
  454.0 20.7 %reduce-scatter.14.cloned.1.call-done = bf16[256,128]{0,1:T(8,128)(2,1)} async-done(((bf16[1024,128]{0,1:T(8,128)(2,1)}), bf16[256,128]{0,1:T(8,128)(2,1)}) %reduce-scatter.14.cloned.1.call-update) | async-done | bytes 65552 | tf_op jit(solution)/shard_map/reduce_scatter | solution.py:440
  508.1 27.4 %reduce-scatter.18.cloned.1.call-done = bf16[256,64]{0,1:T(8,128)(2,1)} async-done(((bf16[1024,64]{0,1:T(8,128)(2,1)}), bf16[256,64]{0,1:T(8,128)(2,1)}) %reduce-scatter.18.cloned.1.call-update) | async-done | bytes 32784 | tf_op jit(solution)/shard_map/reduce_scatter | solution.py:571
  535.5 27.5 %reduce-scatter.20.cloned.1.call-done = bf16[256,64]{0,1:T(8,128)(2,1)} async-done(((bf16[1024,64]{0,1:T(8,128)(2,1)}), bf16[256,64]{0,1:T(8,128)(2,1)}) %reduce-scatter.20.cloned.1.call-update) | async-done | bytes 32784 | tf_op jit(solution)/shard_map/reduce_scatter | solution.py:574
  568.1 22.7 %reduce-scatter.22.cloned.1.call-done = bf16[256,256]{1,0:T(8,128)(2,1)} async-done(((bf16[1024,256]{1,0:T(8,128)(2,1)}), bf16[256,256]{1,0:T(8,128)(2,1)}) %reduce-scatter.22.cloned.1.call-update) | async-done | bytes 131088 | tf_op jit(solution)/shard_map/reduce_scatter | solution.py:577
  590.8 28.4 %reduce-scatter.16.cloned.1.call-done = bf16[256,256]{0,1:T(8,128)(2,1)} async-done(((bf16[1024,256]{0,1:T(8,128)(2,1)}), bf16[256,256]{0,1:T(8,128)(2,1)}) %reduce-scatter.16.cloned.1.call-update) | async-done | bytes 131088 | tf_op jit(solution)/shard_map/reduce_scatter | solution.py:568
  619.2 28.4 %reduce-scatter.28.cloned.1.call-done = bf16[256,256]{0,1:T(8,128)(2,1)} async-done(((bf16[1024,256]{0,1:T(8,128)(2,1)}), bf16[256,256]{0,1:T(8,128)(2,1)}) %reduce-scatter.28.cloned.1.call-update) | async-done | bytes 131088 | tf_op jit(solution)/shard_map/reduce_scatter | solution.py:586
  647.6 38.1 %reduce-scatter.34.cloned.1.call-done = bf16[256,1024]{1,0:T(8,128)(2,1)} async-done(((bf16[1024,1024]{1,0:T(8,128)(2,1)}), bf16[256,1024]{1,0:T(8,128)(2,1)}) %reduce-scatter.34.cloned.1.call-update) | async-done | bytes 524304 | tf_op jit(solution)/shard_map/reduce_scatter | solution.py:595
  685.6 38.0 %reduce-scatter.36.cloned.1.call-done = bf16[256,1024]{1,0:T(8,128)(2,1)} async-done(((bf16[1024,1024]{1,0:T(8,128)(2,1)}), bf16[256,1024]{1,0:T(8,128)(2,1)}) %reduce-scatter.36.cloned.1.call-update) | async-done | bytes 524304 | tf_op jit(solution)/shard_map/reduce_scatter | solution.py:598
  723.7 38.2 %reduce-scatter.38.cloned.1.call-done = bf16[256,1024]{1,0:T(8,128)(2,1)} async-done(((bf16[1024,1024]{1,0:T(8,128)(2,1)}), bf16[256,1024]{1,0:T(8,128)(2,1)}) %reduce-scatter.38.cloned.1.call-update) | async-done | bytes 524304 | tf_op jit(solution)/shard_map/reduce_scatter | solution.py:601
  761.8 34.0 %reduce-scatter.32.cloned.1.call-done = bf16[256,768]{1,0:T(8,128)(2,1)} async-done(((bf16[1024,768]{1,0:T(8,128)(2,1)}), bf16[256,768]{1,0:T(8,128)(2,1)}) %reduce-scatter.32.cloned.1.call-update) | async-done | bytes 393232 | tf_op jit(solution)/shard_map/reduce_scatter | solution.py:592
  795.8 34.2 %reduce-scatter.24.cloned.1.call-done = bf16[256,768]{0,1:T(8,128)(2,1)} async-done(((bf16[1024,768]{0,1:T(8,128)(2,1)}), bf16[256,768]{0,1:T(8,128)(2,1)}) %reduce-scatter.24.cloned.1.call-update) | async-done | bytes 393232 | tf_op jit(solution)/shard_map/reduce_scatter | solution.py:580
  830.0 34.1 %reduce-scatter.26.cloned.1.call-done = bf16[256,768]{0,1:T(8,128)(2,1)} async-done(((bf16[1024,768]{0,1:T(8,128)(2,1)}), bf16[256,768]{0,1:T(8,128)(2,1)}) %reduce-scatter.26.cloned.1.call-update) | async-done | bytes 393232 | tf_op jit(solution)/shard_map/reduce_scatter | solution.py:583
  867.6 33.5 %all-reduce.33.cloned.1.call-done = (bf16[256,64]{0,1:T(8,128)(2,1)}, bf16[256,64]{0,1:T(8,128)(2,1)}, bf16[256,12]{0,1:T(8,128)(2,1)}) async-done(((bf16[256,64]{0,1:T(8,128)(2,1)}, bf16[256,64]{0,1:T(8,128)(2,1)}, bf16[256,12]{0,1:T(8,128)(2,1)}), (bf16[256,64]{0,1:T(8,128)(2,1)}, bf16[256,64]{0,1:T(8,128)(2,1)}, bf16[256,12]{0,1:T(8,128)(2,1)})) %all-reduce.33.cloned.1.call-update) | async-done | bytes 71696 | tf_op jit(solution)/shard_map/psum | solution.py:620
  905.2 18.1 %all-reduce.29.cloned.1.call-done = f32[256,1024]{1,0:T(8,128)} async-done(((f32[256,1024]{1,0:T(8,128)}), f32[256,1024]{1,0:T(8,128)}) %all-reduce.29.cloned.1.call-update) | async-done | bytes 1048592 | tf_op jit(solution)/shard_map/psum | solution.py:160
  925.0 108.6 %all-reduce.14 = (f32[1024]{0:T(1024)}, f32[1024]{0:T(1024)}, f32[768,4]{1,0:T(8,128)S(1)}, f32[256,4]{1,0:T(8,128)S(1)}, f32[12]{0:T(128)}, /*index=5*/f32[12]{...) all-reduce(f32[1024]{0:T(1024)S(1)} %get-tuple-element.1242, ...), channel_id=1, replica_groups=mesh['fsdp'=4,'context'=4,'tensor'=2] {'fsdp','context'}, use_global_device_ids=true, to_apply=%region_53.55 | all-reduce | flops 6951 | bytes 55608 | tf_op jit(solution)/shard_map/psum | solution.py:531
  1036.8 29.9 %all-reduce.35.cloned.1.call-done = (bf16[256,256]{0,1:T(8,128)(2,1)}, bf16[256,768]{0,1:T(8,128)(2,1)}, bf16[256,768]{0,1:T(8,128)(2,1)}, bf16[256,256]{0,1:T(8...) async-done(((bf16[256,256]{0,1:T(8,128)(2,1)}, ...) | async-done | bytes 3145744 | tf_op jit(solution)/shard_map/psum | solution.py:619
  (620 shorter events, 398.3 us)
Async XLA Ops:
  7.2 84.4 %all-gather.7.cloned.1.call-start = ((), (), s32[]{:S(2)}) async-start(), calls=%async_computation.15 | async-start | bytes 1966080 | tf_op jit(solution)/shard_map/all_gather | solution.py:227
  8.0 83.7 %all-gather.9.cloned.1.call-start = ((), (), s32[]{:S(2)}) async-start(), calls=%async_computation.16 | async-start | bytes 1966080 | tf_op jit(solution)/shard_map/all_gather | solution.py:228
  8.7 195.9 %all-gather.11.cloned.1.call-start = ((), (), s32[]{:S(2)}) async-start(), calls=%async_computation.17 | async-start | bytes 1966080 | tf_op jit(solution)/shard_map/all_gather | solution.py:231
  9.5 81.4 %all-to-all-start = ((bf16[4,64,1024]{2,1,0:T(8,128)(2,1)}), bf16[4,64,1024]{2,1,0:T(8,128)(2,1)S(1)}, u32[]{:S(2)}, u32[]{:S(2)}) async-start(bf16[4,64,1024]{2,1,0:T(8,128)(2,1)} %bitcast.307), calls=%async_computation | async-start | bytes 1048576 | tf_op jit(solution)/shard_map/all_to_all | solution.py:200
  16.0 213.2 %all-gather.17.cloned.1.call-start = ((), (), s32[]{:S(2)}) async-start(), calls=%async_computation.21 | async-start | bytes 2621440 | tf_op jit(solution)/shard_map/all_gather | solution.py:234
  16.6 216.3 %all-reduce.25.cloned.1.call-start = ((), (), s32[]{:S(2)}) async-start(), calls=%async_computation.18 | async-start | bytes 2097152 | tf_op jit(solution)/shard_map/psum | solution.py:160
  208.1 57.6 %all-gather.13.cloned.1.call-start = ((), (), s32[]{:S(2)}) async-start(), calls=%async_computation.19 | async-start | bytes 2621440 | tf_op jit(solution)/shard_map/all_gather | solution.py:232
  208.7 94.1 %all-gather.15.cloned.1.call-start = ((), (), s32[]{:S(2)}) async-start(), calls=%async_computation.20 | async-start | bytes 2621440 | tf_op jit(solution)/shard_map/all_gather | solution.py:233
  209.4 124.2 %all-reduce.31.cloned.1.call-start = ((), (), s32[]{:S(2)}) async-start(), calls=%async_computation.37 | async-start | bytes 4194304 | tf_op jit(solution)/shard_map/psum | solution.py:160
  312.1 138.7 %all-reduce.27.cloned.1.call-start = ((), (), s32[]{:S(2)}) async-start(), calls=%async_computation.23 | async-start | bytes 786432 | tf_op jit(solution)/shard_map/psum | solution.py:160
  448.3 59.8 %reduce-scatter.30.cloned.1.call-start = ((), (), s32[]{:S(2)}) async-start(), calls=%async_computation.32 | async-start | bytes 40960 | tf_op jit(solution)/shard_map/reduce_scatter | solution.py:589
  488.4 74.6 %reduce-scatter.20.cloned.1.call-start = ((), (), s32[]{:S(2)}) async-start(), calls=%async_computation.27 | async-start | bytes 163840 | tf_op jit(solution)/shard_map/reduce_scatter | solution.py:574
  489.2 101.6 %reduce-scatter.22.cloned.1.call-start = ((), (), s32[]{:S(2)}) async-start(), calls=%async_computation.28 | async-start | bytes 655360 | tf_op jit(solution)/shard_map/reduce_scatter | solution.py:577
  490.5 128.7 %reduce-scatter.16.cloned.1.call-start = ((), (), s32[]{:S(2)}) async-start(), calls=%async_computation.25 | async-start | bytes 655360 | tf_op jit(solution)/shard_map/reduce_scatter | solution.py:568
  492.9 154.7 %reduce-scatter.28.cloned.1.call-start = ((), (), s32[]{:S(2)}) async-start(), calls=%async_computation.31 | async-start | bytes 655360 | tf_op jit(solution)/shard_map/reduce_scatter | solution.py:586
  493.5 192.2 %reduce-scatter.34.cloned.1.call-start = ((), (), s32[]{:S(2)}) async-start(), calls=%async_computation.34 | async-start | bytes 2621440 | tf_op jit(solution)/shard_map/reduce_scatter | solution.py:595
  495.7 228.0 %reduce-scatter.36.cloned.1.call-start = ((), (), s32[]{:S(2)}) async-start(), calls=%async_computation.35 | async-start | bytes 2621440 | tf_op jit(solution)/shard_map/reduce_scatter | solution.py:598
  499.0 262.9 %reduce-scatter.38.cloned.1.call-start = ((), (), s32[]{:S(2)}) async-start(), calls=%async_computation.36 | async-start | bytes 2621440 | tf_op jit(solution)/shard_map/reduce_scatter | solution.py:601
  501.1 294.7 %reduce-scatter.32.cloned.1.call-start = ((), (), s32[]{:S(2)}) async-start(), calls=%async_computation.33 | async-start | bytes 1966080 | tf_op jit(solution)/shard_map/reduce_scatter | solution.py:592
  503.1 326.9 %reduce-scatter.24.cloned.1.call-start = ((), (), s32[]{:S(2)}) async-start(), calls=%async_computation.29 | async-start | bytes 1966080 | tf_op jit(solution)/shard_map/reduce_scatter | solution.py:580
  507.0 357.1 %reduce-scatter.26.cloned.1.call-start = ((), (), s32[]{:S(2)}) async-start(), calls=%async_computation.30 | async-start | bytes 1966080 | tf_op jit(solution)/shard_map/reduce_scatter | solution.py:583
  507.8 393.3 %all-reduce.33.cloned.1.call-start = ((), (), s32[]{:S(2)}) async-start(), calls=%async_computation.38 | async-start | bytes 147456 | tf_op jit(solution)/shard_map/psum | solution.py:620
  563.0 360.3 %all-reduce.29.cloned.1.call-start = ((), (), s32[]{:S(2)}) async-start(), calls=%async_computation.24 | async-start | bytes 2097152 | tf_op jit(solution)/shard_map/psum | solution.py:160
  567.9 498.8 %all-reduce.35.cloned.1.call-start = ((), (), s32[]{:S(2)}) async-start(), calls=%async_computation.39 | async-start | bytes 6291456 | tf_op jit(solution)/shard_map/psum | solution.py:619
  (158 other events, 4242.7 us)
Sparse Core Ops, SparseCore 0:
  9.9 38.9 all-gather.6
  50.7 32.5 all-gather.8
  85.1 30.8 all-gather.10
  117.7 35.2 all-gather.16
  208.2 19.3 all-reduce.24
  229.3 36.3 all-gather.12
  267.6 35.1 all-gather.14
  312.2 21.3 all-reduce.30
  448.4 26.1 reduce-scatter.13
  486.8 21.2 reduce-scatter.29
  511.3 24.1 reduce-scatter.17
  538.8 24.1 reduce-scatter.19
  565.7 25.0 reduce-scatter.21
  594.1 25.0 reduce-scatter.15
  622.4 25.0 reduce-scatter.27
  650.4 35.1 reduce-scatter.33
  688.5 35.1 reduce-scatter.35
  726.6 35.1 reduce-scatter.37
  764.7 31.1 reduce-scatter.31
  798.8 31.1 reduce-scatter.23
  833.0 31.1 reduce-scatter.25
  866.7 34.3 all-reduce.32
  903.9 19.4 all-reduce.28
  926.4 140.2 all-reduce.34
  (1 shorter events, 18.5 us)
where the time goes:
time: 1090 us; the launch traced here: 1080 us
  waiting for transfers between devices  599 us (55%)
  blocking collectives  213 us (20%)
  matrix products  76.1 us (7%)
  other arithmetic  74.3 us (7%)
  local copies, waits for them, and re-layouts  60.1 us (6%)
  starting transfers between devices  27.5 us (3%)
  between operations  19.6 us (2%)
  loops' own time  14.9 us (1%)
    psum x1, blocking collectives, per_device(): lax.psum((stats_part, grad_attn_gain, grad_ff_gain, grad_conv[:inner_widt...  109 us
    ppermute x8, waiting for transfers between devices, passed_along(): return lax.ppermute(block, axis, route)  56.3 us
    psum x4, waiting for transfers between devices, over_tensor(): return lax.psum(value_matrix, 'tensor')  38.6 us
    reduce_scatter x1, waiting for transfers between devices, per_device(): lax.psum_scatter(grad_down.astype(jnp.bfloat16), 'fsdp', scatter_dimensio...  38.2 us
    reduce_scatter x1, waiting for transfers between devices, per_device(): lax.psum_scatter(grad_weight_gate.astype(jnp.bfloat16), 'fsdp', scatter_d...  38.1 us
    reduce_scatter x1, waiting for transfers between devices, per_device(): lax.psum_scatter(grad_weight_up.astype(jnp.bfloat16), 'fsdp', scatter_dim...  38 us
    reduce_scatter x1, waiting for transfers between devices, per_device(): lax.psum_scatter(part_gate_z.astype(jnp.bfloat16), 'fsdp', scatter_dimens...  34.2 us
    reduce_scatter x1, waiting for transfers between devices, per_device(): lax.psum_scatter(part_ssm_in.astype(jnp.bfloat16), 'fsdp', scatter_dimens...  34.1 us
  transfers between devices with their start and end apart: 34, of which 25 were waited for; matrix products, arithmetic and copies ran while one was open for 12% of the time, Pallas kernels for 0%

commit v1 on v0

--- a/solution.py
+++ b/solution.py
@@ -146,18 +146,171 @@
     return (local_out, carry_gain, output_matrix, whole_decay, fresh_state)
 
 
+def swap(block, axis, bit):
+    route = [(i, i ^ bit) for i in range(lax.axis_size(axis))]
+    return lax.ppermute(block, axis, route)
+
+
+def over_tensor(block):
+    return block + swap(block, "tensor", 1)
+
+
+def relative(block, shard, axis):
+    width = D // 4
+    parts = [lax.slice_in_dim(block, k * width, (k + 1) * width, axis=axis) for k in range(4)]
+    odd = (shard & 1) == 1
+    parts = [jnp.where(odd, parts[k ^ 1], parts[k]) for k in range(4)]
+    high = (shard >> 1) == 1
+    parts = [jnp.where(high, parts[k ^ 2], parts[k]) for k in range(4)]
+    return jnp.concatenate(parts, axis=axis)
+
+
+def gather_shards(own):
+    half = own.shape[0] // 2
+    from_x = swap(own, "fsdp", 1)
+    from_y = swap(own, "fsdp", 2)
+    top = swap(from_x[:half], "fsdp", 2)
+    low = swap(from_y[half:], "fsdp", 1)
+    return jnp.concatenate([own, from_x, from_y, top, low], axis=0)
+
+
+def scatter_sum(blocks):
+    rows = blocks.shape[0] // 4
+    half = rows // 2
+    top = swap(blocks[3 * rows : 3 * rows + half], "fsdp", 2)
+    low = swap(blocks[3 * rows + half :], "fsdp", 1)
+    to_x = jnp.concatenate([plus(blocks[rows : rows + half], top), blocks[rows + half : 2 * rows]])
+    to_y = jnp.concatenate(
+        [blocks[2 * rows : 2 * rows + half], plus(blocks[2 * rows + half : 3 * rows], low)]
+    )
+    from_x = swap(to_x, "fsdp", 1)
+    from_y = swap(to_y, "fsdp", 2)
+    total = (
+        blocks[:rows].astype(jnp.float32)
+        + from_x.astype(jnp.float32)
+        + from_y.astype(jnp.float32)
+    )
+    return total.astype(jnp.bfloat16)
+
+
+def plus(left, right):
+    return (left.astype(jnp.float32) + right.astype(jnp.float32)).astype(jnp.bfloat16)
+
+
+def sum_context(block):
+    index = lax.axis_index("context")
+    bits = []
+    bit = 1
+    while bit < lax.axis_size("context"):
+        bits.append(bit)
+        half = block.shape[0] // 2
+        upper = (index & bit) != 0
+        low, top = block[:half], block[half:]
+        kept = jnp.where(upper, top, low)
+        sent = jnp.where(upper, low, top)
+        block = plus(kept, swap(sent, "context", bit))
+        bit *= 2
+    for bit in reversed(bits):
+        upper = (index & bit) != 0
+        other = swap(block, "context", bit)
+        block = jnp.concatenate(
+            [jnp.where(upper, other, block), jnp.where(upper, block, other)], axis=0
+        )
+    return block
+
+
+def sum_small(vector):
+    for axis in ("fsdp", "context"):
+        bit = 1
+        while bit < lax.axis_size(axis):
+            vector = vector + swap(vector, axis, bit)
+            bit *= 2
+    return vector
+
+
+def deal_rows(block, shift):
+    contexts = lax.axis_size("context")
+    pieces = block.reshape(contexts, block.shape[0] // contexts, block.shape[1])
+    if contexts > 4:
+        dealt = lax.all_to_all(pieces, "context", split_axis=0, concat_axis=0, tiled=True)
+        return jnp.roll(dealt, shift, axis=0).reshape(block.shape)
+    index = lax.axis_index("context")
+    got = []
+    for k in range(contexts):
+        piece = lax.dynamic_index_in_dim(pieces, index ^ k, 0, keepdims=False)
+        got.append(swap(piece, "context", k) if k else piece)
+    ordered = []
+    for q in range(contexts):
+        from_index = jnp.mod(q - shift, contexts) ^ index
+        chosen = got[0]
+        for k in range(1, contexts):
+            chosen = jnp.where(from_index == k, got[k], chosen)
+        ordered.append(chosen)
+    return jnp.concatenate(ordered, axis=0)
+
+
+def gather_earlier(block):
+    contexts = lax.axis_size("context")
+    if contexts > 4:
+        return lax.all_gather(block, "context", axis=0)
+    index = lax.axis_index("context")
+    got = [block] + [passed_along(block, "context", k) for k in range(1, contexts)]
+    ordered = []
+    for j in range(contexts):
+        chosen = block
+        for k in range(1, contexts):
+            chosen = jnp.where(index - j == k, got[k], chosen)
+        ordered.append(chosen)
+    return jnp.stack(ordered)
+
+
+def scatter_earlier(blocks):
+    contexts = lax.axis_size("context")
+    if contexts > 4:
+        return lax.psum_scatter(
+            blocks.astype(jnp.bfloat16), "context", scatter_dimension=0, tiled=False
+        ).astype(jnp.float32)
+    index = lax.axis_index("context")
+    total = lax.dynamic_index_in_dim(blocks, index, 0, keepdims=False)
+    low = blocks.astype(jnp.bfloat16)
+    for k in range(1, contexts):
+        sent = lax.dynamic_index_in_dim(low, jnp.maximum(index - k, 0), 0, keepdims=False)
+        total = total + passed_along(sent, "context", -k).astype(jnp.float32)
+    return total
+
+
 def carry_states(decay, state_term, reverse):
     direction = -1 if reverse else 1
-
-    def relay(step_index, incoming):
-        outgoing = decay[:, None, None] * incoming + state_term
-        return passed_along(outgoing, "context", direction)
-
-    return lax.fori_loop(0, lax.axis_size("context") - 1, relay, jnp.zeros_like(state_term))
-
-
-def over_tensor(value_matrix):
-    return lax.psum(value_matrix, "tensor")
+    heads, width, states = state_term.shape
+    state = state_term
+    gain = decay
+    entering = None
+    entering_gain = None
+    distance = 1
+    contexts = lax.axis_size("context")
+    while distance < contexts:
+        high = gain.astype(jnp.bfloat16)
+        rest = (gain - high.astype(jnp.float32)).astype(jnp.bfloat16)
+        gains = jnp.zeros((16, states), jnp.bfloat16)
+        gains = gains.at[0, :heads].set(high).at[1, :heads].set(rest)
+        packed = jnp.concatenate(
+            [state.astype(jnp.bfloat16).reshape(heads * width, states), gains], axis=0
+        )
+        got = passed_along(packed, "context", direction * distance)
+        got_gain = (
+            got[heads * width, :heads].astype(jnp.float32)
+            + got[heads * width + 1, :heads].astype(jnp.float32)
+        )
+        got_state = got[: heads * width].astype(jnp.float32).reshape(heads, width, states)
+        if entering is None:
+            entering, entering_gain = got_state, got_gain
+        else:
+            entering = entering + entering_gain[:, None, None] * got_state
+            entering_gain = entering_gain * got_gain
+        state = state + gain[:, None, None] * got_state
+        gain = gain * got_gain
+        distance *= 2
+    return entering
 
 
 def per_device(
@@ -196,46 +349,18 @@
     score_scale = HEAD_WIDTH ** (-0.5)
     piece_rows = count_of_rows // contexts
     shift_amount = (deal[0, 0] // piece_rows - lax.axis_index("context")) % contexts
-    dealt_tokens, dealt_cot = (
-        lax.all_to_all(tokens, "context", split_axis=0, concat_axis=0, tiled=True),
-        lax.all_to_all(cotangent, "context", split_axis=0, concat_axis=0, tiled=True),
-    )
-    tokens_placed = jnp.roll(
-        dealt_tokens.reshape(contexts, piece_rows, D), shift_amount, axis=0
-    ).reshape(count_of_rows, D)
-    cot_placed = jnp.roll(dealt_cot.reshape(contexts, piece_rows, D), shift_amount, axis=0).reshape(
-        count_of_rows, D
-    )
-    (
-        full_query,
-        full_key,
-        full_value,
-        full_attn_out,
-        full_gate_z,
-        full_ssm_in,
-        full_bc,
-        full_step,
-        full_ssm_out,
-        full_gate,
-        full_up,
-        full_down,
-    ) = (
-        lax.all_gather(w_query, "fsdp", axis=0, tiled=True),
-        lax.all_gather(w_key, "fsdp", axis=0, tiled=True),
-        lax.all_gather(w_value, "fsdp", axis=0, tiled=True),
-        lax.all_gather(w_attn_out, "fsdp", axis=0, tiled=True),
-        lax.all_gather(w_gate_z, "fsdp", axis=0, tiled=True),
-        lax.all_gather(w_ssm_in, "fsdp", axis=0, tiled=True),
-        lax.all_gather(w_bc, "fsdp", axis=0, tiled=True),
-        lax.all_gather(w_step, "fsdp", axis=0, tiled=True),
-        lax.all_gather(w_ssm_out, "fsdp", axis=0, tiled=True),
-        lax.all_gather(w_gate, "fsdp", axis=0, tiled=True),
-        lax.all_gather(w_up, "fsdp", axis=0, tiled=True),
-        lax.all_gather(w_down, "fsdp", axis=0, tiled=True),
-    )
-    w_inputs = jnp.concatenate(
-        [full_query, full_key, full_value, full_gate_z, full_ssm_in, full_bc, full_step], axis=1
-    )
+    shard = lax.axis_index("fsdp")
+    own_inputs = jnp.concatenate(
+        [w_query, w_key, w_value, w_gate_z, w_ssm_in, w_bc, w_step], axis=1
+    )
+    w_inputs = gather_shards(own_inputs)
+    tokens_placed = relative(deal_rows(tokens, shift_amount), shard, 1)
+    cot_placed = relative(deal_rows(cotangent, shift_amount), shard, 1)
+    full_out = gather_shards(jnp.concatenate([w_attn_out, w_ssm_out], axis=1))
+    full_gate_up = gather_shards(jnp.concatenate([w_gate, w_up], axis=1))
+    full_down = gather_shards(w_down)
+    attn_gain_rel = relative(attn_norm_gain, shard, 0)
+    ff_gain_rel = relative(ff_norm_gain, shard, 0)
     query_end = query_heads * HEAD_WIDTH
     key_end = query_end + HEAD_WIDTH
     value_end = key_end + HEAD_WIDTH
@@ -254,7 +379,7 @@
     tokens_f = tokens_placed.astype(jnp.float32)
     inv_first = lax.rsqrt(jnp.mean(tokens_f * tokens_f, axis=-1, keepdims=True) + epsilon)
     scaled_first = tokens_f * inv_first
-    normed = (scaled_first * attn_norm_gain).astype(jnp.bfloat16)
+    normed = (scaled_first * attn_gain_rel).astype(jnp.bfloat16)
     projected = matmul_low(normed, w_inputs)
     query_pre = projected[:, :query_end]
     key_before_rotary = projected[:, query_end:key_end]
@@ -264,8 +389,8 @@
     step_raw = projected[:, bc_end:step_end]
     query_rot = apply_rotary(query_pre, sequence_position, query_heads, 1.0).astype(jnp.bfloat16)
     key_rot = apply_rotary(key_before_rotary, sequence_position, 1, 1.0).astype(jnp.bfloat16)
-    key_value = lax.all_gather(
-        jnp.concatenate([key_rot, value_low], axis=1), "context", axis=0, tiled=True
+    key_value = gather_earlier(jnp.concatenate([key_rot, value_low], axis=1)).reshape(
+        group_row_list, 2 * HEAD_WIDTH
     )
     query_matrix = (
         query_rot.reshape(count_of_rows, query_heads, HEAD_WIDTH)
@@ -340,7 +465,6 @@
         .reshape(count_of_rows, query_end)
         .astype(jnp.bfloat16)
     )
-    attn_part = matmul_nt(attended, full_attn_out)
     halo_rows = passed_along(conv_in[count_of_rows - (KC - 1) :], "context", 1)
     extended = jnp.concatenate([halo_rows, conv_in], axis=0).astype(jnp.float32)
     conv_weight = jnp.concatenate([conv_ssm, conv_bc], axis=0)
@@ -371,20 +495,22 @@
     gated_inv = lax.rsqrt(square_sum / DI + epsilon)
     gated_norm = gated * gated_inv[:, None]
     mixed = (gated_norm * ssm_norm_gain).astype(jnp.bfloat16)
-    ssm_part = matmul_nt(mixed, full_ssm_out)
-    mixer = over_tensor(attn_part + ssm_part)
+    both = jnp.concatenate([attended, mixed], axis=1)
+    mixer = over_tensor(matmul_nt(both, full_out))
     resid = tokens_f + mixer
     inv_second = lax.rsqrt(jnp.mean(resid * resid, axis=-1, keepdims=True) + epsilon)
     scaled_second = resid * inv_second
-    normed_ff = (scaled_second * ff_norm_gain).astype(jnp.bfloat16)
-    gate_v = matmul_low(normed_ff, full_gate)
-    up_v = matmul_low(normed_ff, full_up)
+    normed_ff = (scaled_second * ff_gain_rel).astype(jnp.bfloat16)
+    gate_up = matmul_low(normed_ff, full_gate_up)
+    hidden_width = gate_up.shape[1] // 2
+    gate_v = gate_up[:, :hidden_width]
+    up_v = gate_up[:, hidden_width:]
     sig_gate = jax.nn.sigmoid(gate_v)
     silu_gate = gate_v * sig_gate
     hidden = (silu_gate * up_v).astype(jnp.bfloat16)
     ff_part = over_tensor(matmul_nt(hidden, full_down))
     final = resid + ff_part
-    output = final.astype(jnp.bfloat16)
+    output = relative(final.astype(jnp.bfloat16), shard, 1)
     grad_final = cot_placed.astype(jnp.float32)
     grad_ff = grad_final.astype(jnp.bfloat16)
     grad_hidden = matmul_low(grad_ff, full_down)
@@ -393,21 +519,23 @@
         jnp.bfloat16
     )
     grad_up = (grad_hidden * silu_gate).astype(jnp.bfloat16)
-    grad_normed_ff = over_tensor(matmul_nt(grad_gate, full_gate) + matmul_nt(grad_up, full_up))
-    grad_weight_gate = matmul_tn(normed_ff, grad_gate)
-    grad_weight_up = matmul_tn(normed_ff, grad_up)
+    grad_gate_up = jnp.concatenate([grad_gate, grad_up], axis=1)
+    grad_normed_ff = over_tensor(matmul_nt(grad_gate_up, full_gate_up))
+    grad_weight_ff = jnp.concatenate([matmul_tn(normed_ff, grad_gate_up).astype(jnp.bfloat16), grad_down.astype(jnp.bfloat16)], axis=1)
+    sum_ff = sum_context(scatter_sum(grad_weight_ff))
     grad_ff_gain = jnp.sum(grad_normed_ff * scaled_second, axis=0)
-    grad_second = grad_normed_ff * ff_norm_gain
+    grad_second = grad_normed_ff * ff_gain_rel
     grad_resid = (
         grad_final
         + inv_second * grad_second
         - resid * inv_second**3 * jnp.mean(grad_second * resid, axis=-1, keepdims=True)
     )
     grad_mixer = grad_resid.astype(jnp.bfloat16)
-    grad_attended = matmul_low(grad_mixer, full_attn_out).astype(jnp.bfloat16)
-    grad_attn_out = matmul_tn(grad_mixer, attended)
-    grad_mixed = matmul_low(grad_mixer, full_ssm_out)
-    grad_ssm_out = matmul_tn(grad_mixer, mixed)
+    grad_both = matmul_low(grad_mixer, full_out)
+    grad_attended = grad_both[:, :query_end].astype(jnp.bfloat16)
+    grad_mixed = grad_both[:, query_end:]
+    grad_weight_out = matmul_tn(grad_mixer, both).astype(jnp.bfloat16)
+    sum_out = sum_context(scatter_sum(grad_weight_out))
     grad_rows = (
         grad_attended.reshape(count_of_rows, query_heads, HEAD_WIDTH)
         .transpose(1, 0, 2)
@@ -437,12 +565,7 @@
     grad_query_rows, grad_kv_blocks = lax.scan(
         back_step, jnp.zeros((query_rows, HEAD_WIDTH), jnp.float32), block_ids
     )
-    grad_kv = lax.psum_scatter(
-        grad_kv_blocks.reshape(group_row_list, 2 * HEAD_WIDTH).astype(jnp.bfloat16),
-        "context",
-        scatter_dimension=0,
-        tiled=True,
-    ).astype(jnp.float32)
+    grad_kv = scatter_earlier(grad_kv_blocks.reshape(contexts, count_of_rows, 2 * HEAD_WIDTH))
     grad_query_rot = (
         grad_query_rows.reshape(query_heads, count_of_rows, HEAD_WIDTH)
         .transpose(1, 0, 2)
@@ -507,17 +630,39 @@
     )
     w_back = w_inputs * column_scale[None, :]
     grad_normed = over_tensor(matmul_nt(grad_inputs, w_back))
-    grad_inputs_weight = matmul_tn(normed, grad_inputs)
+    grad_inputs_weight = matmul_tn(normed, grad_inputs).astype(jnp.bfloat16)
+    sum_inputs = sum_context(scatter_sum(grad_inputs_weight))
     grad_attn_gain = jnp.sum(grad_normed * scaled_first, axis=0)
-    grad_first = grad_normed * attn_norm_gain
-    input_grad = (
+    grad_first = grad_normed * attn_gain_rel
+    input_grad = relative(
         grad_resid
         + inv_first * grad_first
-        - tokens_f * inv_first**3 * jnp.mean(grad_first * tokens_f, axis=-1, keepdims=True)
+        - tokens_f * inv_first**3 * jnp.mean(grad_first * tokens_f, axis=-1, keepdims=True),
+        shard,
+        1,
     )
     stats_part = jnp.stack(
         [jnp.sum(final * final), jnp.sum(mixer * mixer), jnp.sum(ff_part * ff_part)]
     )
+    small = [
+        stats_part,
+        relative(grad_attn_gain, shard, 0),
+        relative(grad_ff_gain, shard, 0),
+        grad_conv[:inner_width_local],
+        grad_conv_bc,
+        grad_bias,
+        grad_decay_log,
+        grad_skip,
+        grad_ssm_gain,
+    ]
+    flat = jnp.concatenate([item.reshape(-1) for item in small])
+    flat = jnp.pad(flat, (0, -flat.shape[0] % 1024)).reshape(-1, 128)
+    flat = sum_small(flat).reshape(-1)
+    summed = []
+    at = 0
+    for item in small:
+        summed.append(flat[at : at + item.size].reshape(item.shape))
+        at += item.size
     (
         stats_sum,
         sum_attn_gain,
@@ -528,130 +673,35 @@
         sum_decay_log,
         sum_skip,
         sum_ssm_gain,
-    ) = lax.psum(
-        (
-            stats_part,
-            grad_attn_gain,
-            grad_ff_gain,
-            grad_conv[:inner_width_local],
-            grad_conv_bc,
-            grad_bias,
-            grad_decay_log,
-            grad_skip,
-            grad_ssm_gain,
-        ),
-        ("fsdp", "context"),
-    )
+    ) = summed
     token_count = group_row_list * lax.axis_size("fsdp")
     rms_stats = jnp.sqrt(stats_sum / (token_count * D))
-    part_query = grad_inputs_weight[:, :query_end]
-    part_key = grad_inputs_weight[:, query_end:key_end]
-    part_value = grad_inputs_weight[:, key_end:value_end]
-    part_gate_z = grad_inputs_weight[:, value_end:gate_end]
-    part_ssm_in = grad_inputs_weight[:, gate_end:ssm_end]
-    part_bc = grad_inputs_weight[:, ssm_end:bc_end]
-    part_step = grad_inputs_weight[:, bc_end:step_end]
-    (
-        rows_query,
-        rows_key,
-        rows_value,
-        rows_attn_out,
-        rows_gate_z,
-        rows_ssm_in,
-        rows_bc,
-        rows_step,
-        rows_ssm_out,
-        rows_gate,
-        rows_up,
-        rows_down,
-    ) = (
-        lax.psum_scatter(
-            part_query.astype(jnp.bfloat16), "fsdp", scatter_dimension=0, tiled=True
-        ).astype(jnp.float32),
-        lax.psum_scatter(
-            part_key.astype(jnp.bfloat16), "fsdp", scatter_dimension=0, tiled=True
-        ).astype(jnp.float32),
-        lax.psum_scatter(
-            part_value.astype(jnp.bfloat16), "fsdp", scatter_dimension=0, tiled=True
-        ).astype(jnp.float32),
-        lax.psum_scatter(
-            grad_attn_out.astype(jnp.bfloat16), "fsdp", scatter_dimension=0, tiled=True
-        ).astype(jnp.float32),
-        lax.psum_scatter(
-            part_gate_z.astype(jnp.bfloat16), "fsdp", scatter_dimension=0, tiled=True
-        ).astype(jnp.float32),
-        lax.psum_scatter(
-            part_ssm_in.astype(jnp.bfloat16), "fsdp", scatter_dimension=0, tiled=True
-        ).astype(jnp.float32),
-        lax.psum_scatter(
-            part_bc.astype(jnp.bfloat16), "fsdp", scatter_dimension=0, tiled=True
-        ).astype(jnp.float32),
-        lax.psum_scatter(
-            part_step.astype(jnp.bfloat16), "fsdp", scatter_dimension=0, tiled=True
-        ).astype(jnp.float32),
-        lax.psum_scatter(
-            grad_ssm_out.astype(jnp.bfloat16), "fsdp", scatter_dimension=0, tiled=True
-        ).astype(jnp.float32),
-        lax.psum_scatter(
-            grad_weight_gate.astype(jnp.bfloat16), "fsdp", scatter_dimension=0, tiled=True
-        ).astype(jnp.float32),
-        lax.psum_scatter(
-            grad_weight_up.astype(jnp.bfloat16), "fsdp", scatter_dimension=0, tiled=True
-        ).astype(jnp.float32),
-        lax.psum_scatter(
-            grad_down.astype(jnp.bfloat16), "fsdp", scatter_dimension=0, tiled=True
-        ).astype(jnp.float32),
-    )
-    (
-        final_query,
-        final_key,
-        final_value,
-        final_attn_out,
-        final_gate_z,
-        final_ssm_in,
-        final_bc,
-        final_step,
-        final_ssm_out,
-        final_gate,
-        final_up,
-        final_down,
-    ) = (
-        lax.psum(rows_query.astype(jnp.bfloat16), "context").astype(jnp.float32),
-        lax.psum(rows_key.astype(jnp.bfloat16), "context").astype(jnp.float32),
-        lax.psum(rows_value.astype(jnp.bfloat16), "context").astype(jnp.float32),
-        lax.psum(rows_attn_out.astype(jnp.bfloat16), "context").astype(jnp.float32),
-        lax.psum(rows_gate_z.astype(jnp.bfloat16), "context").astype(jnp.float32),
-        lax.psum(rows_ssm_in.astype(jnp.bfloat16), "context").astype(jnp.float32),
-        lax.psum(rows_bc.astype(jnp.bfloat16), "context").astype(jnp.float32),
-        lax.psum(rows_step.astype(jnp.bfloat16), "context").astype(jnp.float32),
-        lax.psum(rows_ssm_out.astype(jnp.bfloat16), "context").astype(jnp.float32),
-        lax.psum(rows_gate.astype(jnp.bfloat16), "context").astype(jnp.float32),
-        lax.psum(rows_up.astype(jnp.bfloat16), "context").astype(jnp.float32),
-        lax.psum(rows_down.astype(jnp.bfloat16), "context").astype(jnp.float32),
-    )
+    sum_inputs = sum_inputs.astype(jnp.float32)
+    sum_out = sum_out.astype(jnp.float32)
+    sum_ff = sum_ff.astype(jnp.float32)
     return (
         output,
         input_grad,
         sum_attn_gain,
         sum_ff_gain,
-        final_query,
-        final_key,
-        final_value,
-        final_attn_out,
-        final_gate_z,
-        final_ssm_in,
-        final_bc,
-        final_step,
-        final_ssm_out,
+        sum_inputs[:, :query_end],
+        sum_inputs[:, query_end:key_end],
+        sum_inputs[:, key_end:value_end],
+        sum_out[:, :query_end],
+        sum_inputs[:, value_end:gate_end],
+        sum_inputs[:, gate_end:ssm_end],
+        sum_inputs[:, ssm_end:bc_end],
+        sum_inputs[:, bc_end:step_end],
+        sum_out[:, query_end:],
         sum_conv_ssm,
         sum_conv_bc,
         sum_bias,
         sum_decay_log,
         sum_skip,
         sum_ssm_gain,
-        final_gate,
-        final_up,
-        final_down,
+        sum_ff[:, :hidden_width],
+        sum_ff[:, hidden_width : 2 * hidden_width],
+        sum_ff[:, 2 * hidden_width :],
         rms_stats,
     )
 

time: 1090 us -> 630 us (0.58)
  waiting for transfers between devices: 599 us -> 233 us
  blocking collectives: 213 us -> 0 us
  local copies, waits for them, and re-layouts: 60.1 us -> 116 us
  starting transfers between devices: 27.5 us -> 75.9 us
  other arithmetic: 74.3 us -> 110 us
  matrix products: 76.1 us -> 62.2 us
  between operations: 19.6 us -> 7.73 us
    reduce_scatter x13 -> x0, waiting for transfers between devices: 372 us -> none  [the longest x1 38.2 us: per_device(): lax.psum_scatter(grad_down.astype(jnp.bfloat16), 'fsdp', scatter_dimensio...]
    ppermute x0 -> x57, waiting for transfers between devices: none -> 189 us  [swap(): return lax.ppermute(block, axis, route)]
    psum x3 -> x0, blocking collectives: 115 us -> none  [the longest x1 109 us: per_device(): lax.psum((stats_part, grad_attn_gain, grad_ff_gain, grad_conv[:inner_widt...]
    psum x6 -> x0, waiting for transfers between devices: 102 us -> none  [the longest x4 38.6 us: over_tensor(): return lax.psum(value_matrix, 'tensor')]
    all_gather x7 -> x0, blocking collectives: 79.2 us -> none  [the longest x1 15.3 us: per_device(): lax.all_gather(w_bc, 'fsdp', axis=0, tiled=True)]
    all_gather x6 -> x0, waiting for transfers between devices: 63 us -> none  [the longest x1 33.6 us: per_device(): lax.all_gather(w_up, 'fsdp', axis=0, tiled=True)]
    ppermute x0 -> x57, starting transfers between devices: none -> 47.5 us  [swap(): return lax.ppermute(block, axis, route)]
    unnamed x309 -> x441, local copies, waits for them, and re-layouts: 17.3 us -> 42.7 us
  transfers between devices with their start and end apart: 34 -> 69, of which waited for: 25 -> 29; matrix products, arithmetic and copies ran while one was open for 12% -> 42% of each run, Pallas kernels for 0% -> 0%
where the time goes in v1:
time: 630 us; the launch traced here: 619 us
  waiting for transfers between devices  233 us (37%)
  local copies, waits for them, and re-layouts  116 us (18%)
  other arithmetic  110 us (17%)
  starting transfers between devices  75.9 us (12%)
  matrix products  62.2 us (10%)
  loops' own time  14.3 us (2%)
  between operations  7.73 us (1%)
    ppermute x57, waiting for transfers between devices, swap(): return lax.ppermute(block, axis, route)  189 us
    ppermute x57, starting transfers between devices, swap(): return lax.ppermute(block, axis, route)  47.5 us
    ppermute x12, waiting for transfers between devices, passed_along(): return lax.ppermute(block, axis, route)  44 us
    unnamed x441, local copies, waits for them, and re-layouts  42.7 us
    ppermute x12, starting transfers between devices, passed_along(): return lax.ppermute(block, axis, route)  28.4 us
    dot_general x3, matrix products, ssd_local(): jnp.einsum('hts,shp->thp', within * intersection[None], scaled, precision...  13.7 us
    dot_general x7, matrix products, matmul_nt(): lax.dot_general(left, right, (((1,), (1,)), ((), ())), preferred_element_...  13.5 us
  transfers between devices with their start and end apart: 69, of which 29 were waited for; matrix products, arithmetic and copies ran while one was open for 42% of the time, Pallas kernels for 0%

profile of v1, /device:TPU:0, one launch (start us, length us, event | category | flops | bytes accessed | tf_op | source)
XLA Modules:
  0.0 618.6 jit_solution(9011785913009854180)
XLA Ops:
  49.1 6.4 %collective-permute-done.29 = bf16[64,1024]{1,0:T(8,128)(2,1)S(1)} collective-permute-done((bf16[64,1024]{1,0:T(8,128)(2,1)S(1)}, bf16[64,1024]{1,0:T(8,128)(2,1)S(1)}, u32[]{:S(2)}, u32[]{:S(2)}) %collective-permute-start.29) | collective-permute-done | bytes 131104 | tf_op jit(solution)/shard_map/ppermute | solution.py:151
  62.4 8.0 %collective-permute-done.14 = bf16[256,1024]{1,0:T(8,128)(2,1)S(1)} collective-permute-done((bf16[256,1024]{1,0:T(8,128)(2,1)S(1)}, bf16[256,1024]{1,0:T(8,128)(2,1)S(1)}, u32[]{:S(2)}, u32[]{:S(2)}) %collective-permute-start.14) | collective-permute-done | bytes 524320 | tf_op jit(solution)/shard_map/ppermute | solution.py:151
  74.4 17.8 %collective-permute-done.25 = bf16[128,1024]{1,0:T(8,128)(2,1)S(1)} collective-permute-done((bf16[128,1024]{1,0:T(8,128)(2,1)S(1)}, bf16[128,1024]{1,0:T(8,128)(2,1)S(1)}, u32[]{:S(2)}, u32[]{:S(2)}) %collective-permute-start.25) | collective-permute-done | bytes 262176 | tf_op jit(solution)/shard_map/ppermute | solution.py:151
  97.5 21.9 %collective-permute-done.17 = bf16[128,1024]{1,0:T(8,128)(2,1)S(1)} collective-permute-done((bf16[128,1024]{1,0:T(8,128)(2,1)S(1)}, bf16[128,1024]{1,0:T(8,128)(2,1)S(1)}, u32[]{:S(2)}, u32[]{:S(2)}) %collective-permute-start.17) | collective-permute-done | bytes 262176 | tf_op jit(solution)/shard_map/ppermute | solution.py:151
  125.0 8.7 %collective-permute-done.5 = bf16[128,2188]{0,1:T(8,128)(2,1)S(1)} collective-permute-done((bf16[128,2188]{0,1:T(8,128)(2,1)S(1)}, bf16[128,2188]{0,1:T(8,128)(2,1)S(1)}, u32[]{:S(2)}, u32[]{:S(2)}) %collective-permute-start.5) | collective-permute-done | bytes 560160 | tf_op jit(solution)/shard_map/ppermute | solution.py:151
  169.8 12.4 %while.66 = (s32[]{:T(128)}, f32[1024]{0:T(1024)S(1)}, f32[1024]{0:T(1024)}, s32[2]{0:T(128)}, s32[256]{0:T(256)S(1)}, /*index=5*/s32[256]{0:T(256)S(1)}, bf16[1...) while((s32[]{:T(128)}, f32[1024]{0:T(1024)S(1)}, ...), condition=%wide.region_8.9_spmd.clone.clone, body=%wide.region_3.8_spmd.clone.clone.sunk | while | flops 74451464 | bytes 4723089 | solution.py:442
  206.3 13.6 %while.67 = (s32[]{:T(128)}, f32[1024,64]{0,1:T(8,128)}, s32[2]{0:T(128)}, s32[256]{0:T(256)S(1)}, s32[256]{0:T(256)S(1)}, /*index=5*/bf16[1024,128]{1,0:T(8,128...) while((s32[]{:T(128)}, f32[1024,64]{0,1:T(8,128)}, ...), condition=%wide.region_12.13_spmd.clone.clone, body=%wide.region_9.12_spmd.clone.clone.sunk | while | flops 137953792 | bytes 962369 | solution.py:459
  231.5 10.7 %collective-permute-done.22 = bf16[128,2048]{1,0:T(8,128)(2,1)S(1)} collective-permute-done((bf16[128,2048]{1,0:T(8,128)(2,1)S(1)}, bf16[128,2048]{1,0:T(8,128)(2,1)S(1)}, u32[]{:S(2)}, u32[]{:S(2)}) %collective-permute-start.22) | collective-permute-done | bytes 524320 | tf_op jit(solution)/shard_map/ppermute | solution.py:151
  262.4 8.8 %collective-permute-done.61 = bf16[128,3072]{1,0:T(8,128)(2,1)} collective-permute-done((bf16[128,3072]{1,0:T(8,128)(2,1)}, bf16[128,3072]{1,0:T(8,128)(2,1)}, u32[]{:S(2)}, u32[]{:S(2)}) %collective-permute-start.61) | collective-permute-done | bytes 786464 | tf_op jit(solution)/shard_map/ppermute | solution.py:151
  285.4 18.2 %while.68 = (s32[]{:T(128)}, f32[1024,64]{0,1:T(8,128)}, f32[2,512,128]{2,1,0:T(8,128)}, s32[2]{0:T(128)}, s32[256]{0:T(256)S(1)}, /*index=5*/s32[256]{0:T(256)S...) while((s32[]{:T(128)}, f32[1024,64]{0,1:T(8,128)}, ...), condition=%wide.region_24.25_spmd.clone.clone, body=%wide.region_21.24_spmd.clone.clone.sunk | while | flops 341017088 | bytes 12892549 | solution.py:565
  289.7 7.8 %conditional.14 = (f32[1024,64]{0,1:T(8,128)}, f32[1,512,128]{1,2,0:T(8,128)S(1)}) conditional(s32[]{:T(128)} %convert_element_type.771, f32[1024,64]{0,1:T(8,128)} %get-tuple-element.1802, (s32[]{:T(128)}, s32[256]{0:T(256)S(1)}, s32[256]{0:T(256)S(1)}, bf16[1024,128]{1,0:T(8,128)(2,1)}, bf16[1024,64]{1,0:T(8,128)(2,1)}, ...), branch_computations={%region_22.22_spmd, %region_23.23_spmd} | conditional | flops 341017088 | bytes 11843678 | solution.py:563
  338.4 6.5 %fusion.50 = (f32[12,256]{1,0:T(8,128)}, f32[12,256]{1,0:T(8,128)}, f32[256,256]{1,0:T(8,128)}) fusion(f32[256,256]{1,0:T(8,128)} %fusion.161, f32[12,256]{1,0:T(8,128)} %bitcast.374, pred[256,256]{1,0:T(8,128)(4,1)} %fusion.128, f32[12,64,256]{2,1,0:T(8,128)} %bitcast.329, f32[256,12,64]{0,2,1:T(8,128)} %bitcast.326, f32[256,12]{0,1:T(8,128)S(1)} %copy-done.95), kind=kOutput, calls=%fused_computation.84 | convolution fusion | flops 611182592 | bytes 2211840 | tf_op jit(solution)/shard_map/transpose(jvp(hts,shp->thp))/dot_general | solution.py:103
  380.5 20.4 %collective-permute-done.37 = bf16[784,128]{1,0:T(8,128)(2,1)S(1)} collective-permute-done((bf16[784,128]{1,0:T(8,128)(2,1)S(1)}, bf16[784,128]{1,0:T(8,128)(2,1)S(1)}, u32[]{:S(2)}, u32[]{:S(2)}) %collective-permute-start.37) | collective-permute-done | bytes 200736 | tf_op jit(solution)/shard_map/ppermute | solution.py:25
  432.0 14.8 %collective-permute-done.39 = f32[3,1024]{0,1:T(8,128)} collective-permute-done((f32[3,1024]{0,1:T(8,128)}, f32[3,1024]{0,1:T(8,128)}, u32[]{:S(2)}, u32[]{:S(2)}) %collective-permute-start.39) | collective-permute-done | bytes 12320 | tf_op jit(solution)/shard_map/ppermute | solution.py:25
  457.2 6.3 %collective-permute-done.57 = bf16[128,1024]{1,0:T(8,128)(2,1)S(1)} collective-permute-done((bf16[128,1024]{1,0:T(8,128)(2,1)S(1)}, bf16[128,1024]{1,0:T(8,128)(2,1)S(1)}, u32[]{:S(2)}, u32[]{:S(2)}) %collective-permute-start.57) | collective-permute-done | bytes 262176 | tf_op jit(solution)/shard_map/ppermute | solution.py:151
  465.3 6.3 %collective-permute-done.58 = bf16[64,1024]{1,0:T(8,128)(2,1)S(1)} collective-permute-done((bf16[64,1024]{1,0:T(8,128)(2,1)S(1)}, bf16[64,1024]{1,0:T(8,128)(2,1)S(1)}, u32[]{:S(2)}, u32[]{:S(2)}) %collective-permute-start.58) | collective-permute-done | bytes 131104 | tf_op jit(solution)/shard_map/ppermute | solution.py:151
  483.1 6.2 %collective-permute-done.60 = bf16[128,1024]{1,0:T(8,128)(2,1)S(1)} collective-permute-done((bf16[128,1024]{1,0:T(8,128)(2,1)S(1)}, bf16[128,1024]{1,0:T(8,128)(2,1)S(1)}, u32[]{:S(2)}, u32[]{:S(2)}) %collective-permute-start.60) | collective-permute-done | bytes 262176 | tf_op jit(solution)/shard_map/ppermute | solution.py:151
  496.3 6.3 %collective-permute-done.41 = f32[56,128]{1,0:T(8,128)S(1)} collective-permute-done((f32[56,128]{1,0:T(8,128)S(1)}, f32[56,128]{1,0:T(8,128)S(1)}, u32[]{:S(2)}, u32[]{:S(2)}) %collective-permute-start.41) | collective-permute-done | bytes 28704 | tf_op jit(solution)/shard_map/ppermute | solution.py:151
  526.5 11.6 %collective-permute-done.66 = bf16[64,3072]{1,0:T(8,128)(2,1)S(1)} collective-permute-done((bf16[64,3072]{1,0:T(8,128)(2,1)S(1)}, bf16[64,3072]{1,0:T(8,128)(2,1)S(1)}, u32[]{:S(2)}, u32[]{:S(2)}) %collective-permute-start.66) | collective-permute-done | bytes 393248 | tf_op jit(solution)/shard_map/ppermute | solution.py:151
  538.4 7.0 %collective-permute-done.49 = bf16[128,2188]{0,1:T(8,128)(2,1)S(1)} collective-permute-done((bf16[128,2188]{0,1:T(8,128)(2,1)S(1)}, bf16[128,2188]{0,1:T(8,128)(2,1)S(1)}, u32[]{:S(2)}, u32[]{:S(2)}) %collective-permute-start.49) | collective-permute-done | bytes 560160 | tf_op jit(solution)/shard_map/ppermute | solution.py:151
  546.9 18.3 %collective-permute-done.67 = bf16[64,3072]{1,0:T(8,128)(2,1)} collective-permute-done((bf16[64,3072]{1,0:T(8,128)(2,1)S(1)}, bf16[64,3072]{1,0:T(8,128)(2,1)}, u32[]{:S(2)}, u32[]{:S(2)}) %collective-permute-start.67) | collective-permute-done | bytes 393248 | tf_op jit(solution)/shard_map/ppermute | solution.py:151
  575.0 11.5 %collective-permute-done.51 = bf16[64,2188]{1,0:T(8,128)(2,1)S(1)} collective-permute-done((bf16[64,2188]{1,0:T(8,128)(2,1)S(1)}, bf16[64,2188]{1,0:T(8,128)(2,1)S(1)}, u32[]{:S(2)}, u32[]{:S(2)}) %collective-permute-start.51) | collective-permute-done | bytes 280096 | tf_op jit(solution)/shard_map/ppermute | solution.py:151
  587.6 12.4 %collective-permute-done.68 = bf16[128,3072]{1,0:T(8,128)(2,1)} collective-permute-done((bf16[128,3072]{1,0:T(8,128)(2,1)}, bf16[128,3072]{1,0:T(8,128)(2,1)}, u32[]{:S(2)}, u32[]{:S(2)}) %collective-permute-start.68) | collective-permute-done | bytes 786464 | tf_op jit(solution)/shard_map/ppermute | solution.py:151
  603.9 6.5 %collective-permute-done.52 = bf16[128,2188]{0,1:T(8,128)(2,1)S(1)} collective-permute-done((bf16[128,2188]{0,1:T(8,128)(2,1)S(1)}, bf16[128,2188]{0,1:T(8,128)(2,1)S(1)}, u32[]{:S(2)}, u32[]{:S(2)}) %collective-permute-start.52) | collective-permute-done | bytes 560160 | tf_op jit(solution)/shard_map/ppermute | solution.py:151
  (893 shorter events, 388.4 us)
Async XLA Ops:
  0.8 57.8 %collective-permute-start.23 = (bf16[256,1024]{1,0:T(8,128)(2,1)}, bf16[256,1024]{1,0:T(8,128)(2,1)}, u32[]{:S(2)}, u32[]{:S(2)}) collective-permute-start(bf16[256,1024]{1,0:T(8,128)(2,1)} %param.74), channel_id=1, source_target_pairs={{0,8},{8,0},{16,24},{24,16},{1,9},{9,1},{17,25},{25,17},{2,10},{10... | collective-permute-start | bytes 1572872 | tf_op jit(solution)/shard_map/ppermute | solution.py:151
  3.8 56.4 %collective-permute-start.24 = (bf16[256,1024]{1,0:T(8,128)(2,1)}, bf16[256,1024]{1,0:T(8,128)(2,1)}, u32[]{:S(2)}, u32[]{:S(2)}) collective-permute-start(bf16[256,1024]{1,0:T(8,128)(2,1)} %param.74), channel_id=1, source_target_pairs={{0,16},{8,24},{16,0},{24,8},{1,17},{9,25},{17,1},{25,9},{2,18},{10... | collective-permute-start | bytes 1572872 | tf_op jit(solution)/shard_map/ppermute | solution.py:151
  7.1 35.3 %collective-permute-start.2 = (bf16[64,1024]{1,0:T(8,128)(2,1)}, bf16[64,1024]{1,0:T(8,128)(2,1)}, u32[]{:S(2)}, u32[]{:S(2)}) collective-permute-start(bf16[64,1024]{1,0:T(8,128)(2,1)} %get-tuple-element.1440), channel_id=1, source_target_pairs={{0,2},{2,0},{4,6},{6,4},{1,3},{3,1},{5,7},{7,5},{8,10},{10,8},{12,... | collective-permute-start | bytes 393224 | tf_op jit(solution)/shard_map/ppermute | solution.py:151
  8.7 34.5 %collective-permute-start.1 = (bf16[64,1024]{1,0:T(8,128)(2,1)}, bf16[64,1024]{1,0:T(8,128)(2,1)}, u32[]{:S(2)}, u32[]{:S(2)}) collective-permute-start(bf16[64,1024]{1,0:T(8,128)(2,1)} %get-tuple-element.1441), channel_id=1, source_target_pairs={{0,4},{2,6},{4,0},{6,2},{1,5},{3,7},{5,1},{7,3},{8,12},{10,14},{12... | collective-permute-start | bytes 393224 | tf_op jit(solution)/shard_map/ppermute | solution.py:151
  11.3 35.4 %collective-permute-start = (bf16[64,1024]{1,0:T(8,128)(2,1)}, bf16[64,1024]{1,0:T(8,128)(2,1)}, u32[]{:S(2)}, u32[]{:S(2)}) collective-permute-start(bf16[64,1024]{1,0:T(8,128)(2,1)} %get-tuple-element.1442), channel_id=1, source_target_pairs={{0,6},{2,4},{4,2},{6,0},{1,7},{3,5},{5,3},{7,1},{8,14},{10,12},{12... | collective-permute-start | bytes 393224 | tf_op jit(solution)/shard_map/ppermute | solution.py:151
  56.1 66.4 %collective-permute-start.4 = (bf16[256,2188]{0,1:T(8,128)(2,1)S(1)}, bf16[256,2188]{0,1:T(8,128)(2,1)S(1)}, u32[]{:S(2)}, u32[]{:S(2)}) collective-permute-start(bf16[256,2188]{0,1:T(8,128)(2,1)S(1)} %copy-done.149), channel_id=1, source_target_pairs={{0,16},{8,24},{16,0},{24,8},{1,17},{9,25},{17,1},{25,9},{2,18},{10... | collective-permute-start | bytes 3360776 | tf_op jit(solution)/shard_map/ppermute | solution.py:151
  58.5 65.6 %collective-permute-start.3 = (bf16[256,2188]{0,1:T(8,128)(2,1)S(1)}, bf16[256,2188]{0,1:T(8,128)(2,1)S(1)}, u32[]{:S(2)}, u32[]{:S(2)}) collective-permute-start(bf16[256,2188]{0,1:T(8,128)(2,1)S(1)} %copy-done.149), channel_id=1, source_target_pairs={{0,8},{8,0},{16,24},{24,16},{1,9},{9,1},{17,25},{25,17},{2,10},{10... | collective-permute-start | bytes 3360776 | tf_op jit(solution)/shard_map/ppermute | solution.py:151
  60.2 59.8 %collective-permute-start.19 = (bf16[256,2048]{1,0:T(8,128)(2,1)}, bf16[256,2048]{1,0:T(8,128)(2,1)S(1)}, u32[]{:S(2)}, u32[]{:S(2)}) collective-permute-start(bf16[256,2048]{1,0:T(8,128)(2,1)} %get-tuple-element.1432), channel_id=1, source_target_pairs={{0,8},{8,0},{16,24},{24,16},{1,9},{9,1},{17,25},{25,17},{2,10},{10... | collective-permute-start | bytes 3145736 | tf_op jit(solution)/shard_map/ppermute | solution.py:151
  92.2 27.3 %collective-permute-start.17 = (bf16[128,1024]{1,0:T(8,128)(2,1)S(1)}, bf16[128,1024]{1,0:T(8,128)(2,1)S(1)}, u32[]{:S(2)}, u32[]{:S(2)}) collective-permute-start(bf16[128,1024]{1,0:T(8,128)(2,1)S(1)} %slice.864), channel_id=1, source_target_pairs={{0,8},{8,0},{16,24},{24,16},{1,9},{9,1},{17,25},{25,17},{2,10},{10... | collective-permute-start | bytes 786440 | tf_op jit(solution)/shard_map/ppermute | solution.py:151
  97.0 129.9 %collective-permute-start.20 = (bf16[256,2048]{1,0:T(8,128)(2,1)}, bf16[256,2048]{1,0:T(8,128)(2,1)}, u32[]{:S(2)}, u32[]{:S(2)}) collective-permute-start(bf16[256,2048]{1,0:T(8,128)(2,1)} %get-tuple-element.1432), channel_id=1, source_target_pairs={{0,16},{8,24},{16,0},{24,8},{1,17},{9,25},{17,1},{25,9},{2,18},{10... | collective-permute-start | bytes 3145736 | tf_op jit(solution)/shard_map/ppermute | solution.py:151
  119.4 106.4 %collective-permute-start.26 = (bf16[128,1024]{1,0:T(8,128)(2,1)}, bf16[128,1024]{1,0:T(8,128)(2,1)}, u32[]{:S(2)}, u32[]{:S(2)}) collective-permute-start(bf16[128,1024]{1,0:T(8,128)(2,1)} %slice.870), channel_id=1, source_target_pairs={{0,8},{8,0},{16,24},{24,16},{1,9},{9,1},{17,25},{25,17},{2,10},{10... | collective-permute-start | bytes 786440 | tf_op jit(solution)/shard_map/ppermute | solution.py:151
  161.5 68.9 %collective-permute-start.21 = (bf16[128,2048]{1,0:T(8,128)(2,1)}, bf16[128,2048]{1,0:T(8,128)(2,1)}, u32[]{:S(2)}, u32[]{:S(2)}) collective-permute-start(bf16[128,2048]{1,0:T(8,128)(2,1)} %slice.865), channel_id=1, source_target_pairs={{0,16},{8,24},{16,0},{24,8},{1,17},{9,25},{17,1},{25,9},{2,18},{10... | collective-permute-start | bytes 1572872 | tf_op jit(solution)/shard_map/ppermute | solution.py:151
  275.8 199.1 %collective-permute-start.64 = (bf16[256,3072]{1,0:T(8,128)(2,1)}, bf16[256,3072]{1,0:T(8,128)(2,1)}, u32[]{:S(2)}, u32[]{:S(2)}) collective-permute-start(bf16[256,3072]{1,0:T(8,128)(2,1)} %pad_maximum_fusion.1), channel_id=1, source_target_pairs={{0,16},{8,24},{16,0},{24,8},{1,17},{9,25},{17,1},{25,9},{2,18},{10... | collective-permute-start | bytes 4718600 | tf_op jit(solution)/shard_map/ppermute | solution.py:151
  277.5 198.0 %collective-permute-start.62 = (bf16[256,3072]{1,0:T(8,128)(2,1)}, bf16[256,3072]{1,0:T(8,128)(2,1)}, u32[]{:S(2)}, u32[]{:S(2)}) collective-permute-start(bf16[256,3072]{1,0:T(8,128)(2,1)} %pad_maximum_fusion), channel_id=1, source_target_pairs={{0,8},{8,0},{16,24},{24,16},{1,9},{9,1},{17,25},{25,17},{2,10},{10... | collective-permute-start | bytes 4718600 | tf_op jit(solution)/shard_map/ppermute | solution.py:151
  322.4 35.3 %collective-permute-start.33 = (bf16[256,128]{0,1:T(8,128)(2,1)}, bf16[256,128]{0,1:T(8,128)(2,1)}, u32[]{:S(2)}, u32[]{:S(2)}) collective-permute-start(bf16[256,128]{0,1:T(8,128)(2,1)} %bitcast.381), channel_id=1, source_target_pairs={{4,0},{6,2},{5,1},{7,3},{12,8},{14,10},{13,9},{15,11},{20,16},{22,... | collective-permute-start | bytes 196616 | tf_op jit(solution)/shard_map/ppermute | solution.py:25
  323.8 35.5 %collective-permute-start.34 = (bf16[256,128]{0,1:T(8,128)(2,1)}, bf16[256,128]{0,1:T(8,128)(2,1)}, u32[]{:S(2)}, u32[]{:S(2)}) collective-permute-start(bf16[256,128]{0,1:T(8,128)(2,1)} %bitcast.380), channel_id=1, source_target_pairs={{6,0},{7,1},{14,8},{15,9},{22,16},{23,17},{30,24},{31,25}} | collective-permute-start | bytes 196616 | tf_op jit(solution)/shard_map/ppermute | solution.py:25
  330.3 30.6 %collective-permute-start.32 = (bf16[256,128]{0,1:T(8,128)(2,1)}, bf16[256,128]{0,1:T(8,128)(2,1)}, u32[]{:S(2)}, u32[]{:S(2)}) collective-permute-start(bf16[256,128]{0,1:T(8,128)(2,1)} %bitcast.56), channel_id=1, source_target_pairs={{2,0},{4,2},{6,4},{3,1},{5,3},{7,5},{10,8},{12,10},{14,12},{11,9},... | collective-permute-start | bytes 196616 | tf_op jit(solution)/shard_map/ppermute | solution.py:25
  378.7 73.9 %collective-permute-start.56 = (bf16[256,1024]{1,0:T(8,128)(2,1)}, bf16[256,1024]{1,0:T(8,128)(2,1)}, u32[]{:S(2)}, u32[]{:S(2)}) collective-permute-start(bf16[256,1024]{1,0:T(8,128)(2,1)} %pad_maximum_fusion.19), channel_id=1, source_target_pairs={{0,16},{8,24},{16,0},{24,8},{1,17},{9,25},{17,1},{25,9},{2,18},{10... | collective-permute-start | bytes 1572872 | tf_op jit(solution)/shard_map/ppermute | solution.py:151
  379.9 72.7 %collective-permute-start.54 = (bf16[256,1024]{1,0:T(8,128)(2,1)}, bf16[256,1024]{1,0:T(8,128)(2,1)}, u32[]{:S(2)}, u32[]{:S(2)}) collective-permute-start(bf16[256,1024]{1,0:T(8,128)(2,1)} %pad_maximum_fusion.18), channel_id=1, source_target_pairs={{0,8},{8,0},{16,24},{24,16},{1,9},{9,1},{17,25},{25,17},{2,10},{10... | collective-permute-start | bytes 1572872 | tf_op jit(solution)/shard_map/ppermute | solution.py:151
  473.3 50.6 %collective-permute-start.48 = (bf16[256,2188]{0,1:T(8,128)(2,1)}, bf16[256,2188]{0,1:T(8,128)(2,1)}, u32[]{:S(2)}, u32[]{:S(2)}) collective-permute-start(bf16[256,2188]{0,1:T(8,128)(2,1)} %pad_maximum_fusion.3), channel_id=1, source_target_pairs={{0,16},{8,24},{16,0},{24,8},{1,17},{9,25},{17,1},{25,9},{2,18},{10... | collective-permute-start | bytes 3360776 | tf_op jit(solution)/shard_map/ppermute | solution.py:151
  474.9 49.1 %collective-permute-start.46 = (bf16[256,2188]{0,1:T(8,128)(2,1)}, bf16[256,2188]{0,1:T(8,128)(2,1)}, u32[]{:S(2)}, u32[]{:S(2)}) collective-permute-start(bf16[256,2188]{0,1:T(8,128)(2,1)} %pad_maximum_fusion.2), channel_id=1, source_target_pairs={{0,8},{8,0},{16,24},{24,16},{1,9},{9,1},{17,25},{25,17},{2,10},{10... | collective-permute-start | bytes 3360776 | tf_op jit(solution)/shard_map/ppermute | solution.py:151
  481.1 38.8 %collective-permute-start.65 = (bf16[128,3072]{1,0:T(8,128)(2,1)}, bf16[128,3072]{1,0:T(8,128)(2,1)}, u32[]{:S(2)}, u32[]{:S(2)}) collective-permute-start(bf16[128,3072]{1,0:T(8,128)(2,1)} %broadcast_select_fusion.2), channel_id=1, source_target_pairs={{0,2},{2,0},{4,6},{6,4},{1,3},{3,1},{5,7},{7,5},{8,10},{10,8},{12,... | collective-permute-start | bytes 2359304 | tf_op jit(solution)/shard_map/ppermute | solution.py:151
  538.3 26.9 %collective-permute-start.67 = (bf16[64,3072]{1,0:T(8,128)(2,1)S(1)}, bf16[64,3072]{1,0:T(8,128)(2,1)}, u32[]{:S(2)}, u32[]{:S(2)}) collective-permute-start(bf16[64,3072]{1,0:T(8,128)(2,1)S(1)} %add_convert_fusion.10), channel_id=1, source_target_pairs={{0,4},{2,6},{4,0},{6,2},{1,5},{3,7},{5,1},{7,3},{8,12},{10,14},{12... | collective-permute-start | bytes 1179656 | tf_op jit(solution)/shard_map/ppermute | solution.py:151
  572.6 27.4 %collective-permute-start.68 = (bf16[128,3072]{1,0:T(8,128)(2,1)}, bf16[128,3072]{1,0:T(8,128)(2,1)}, u32[]{:S(2)}, u32[]{:S(2)}) collective-permute-start(bf16[128,3072]{1,0:T(8,128)(2,1)} %pad_maximum_fusion.7), channel_id=1, source_target_pairs={{0,2},{2,0},{4,6},{6,4},{1,3},{3,1},{5,7},{7,5},{8,10},{10,8},{12,... | collective-permute-start | bytes 2359304 | tf_op jit(solution)/shard_map/ppermute | solution.py:151
  (247 other events, 2947.8 us)

commit v2 on v1

v2 whole, which is shorter than its diff:
```python
import functools

import jax
import jax.numpy as jnp
from jax import lax
from jax.experimental import pallas as pl
from jax.experimental.pallas import tpu as pltpu
from jax.sharding import PartitionSpec as P

D = 1024
QUERY_HEADS = 8
HEAD_WIDTH = 64
SPACE_HEADS = 24
SPACE_HEAD_WIDTH = 64
STATE_WIDTH = 128
KC = 4
DI = 1536
SHARDS = 4
BLOCK = D // SHARDS
LANES = 128

epsilon = 1e-06
rope_base = 100000000000.0
masked_value = -1e30
highest = lax.Precision.HIGHEST
bf16 = jnp.bfloat16
f32 = jnp.float32


def dot(left, right, precision=None):
    return lax.dot_general(
        left, right, (((1,), (0,)), ((), ())), precision=precision, preferred_element_type=f32
    )


def dot_tn(left, right, precision=None):
    return lax.dot_general(
        left, right, (((0,), (0,)), ((), ())), precision=precision, preferred_element_type=f32
    )


def dot_nt(left, right, precision=None):
    return lax.dot_general(
        left, right, (((1,), (1,)), ((), ())), precision=precision, preferred_element_type=f32
    )


def sigmoid(value):
    return 1.0 / (1.0 + jnp.exp(-value))


def iota(shape, axis):
    return lax.broadcasted_iota(jnp.int32, shape, axis)


def starts_of(lens_ref, places):
    start = jnp.zeros_like(places)
    end = jnp.int32(0)
    for i in range(lens_ref.shape[1]):
        end = end + lens_ref[0, i]
        start = jnp.where(places >= end, end, start)
    return start


def first_place(rows):
    return lax.axis_index("context") * rows


def head_lanes(width):
    shape = (LANES, width)
    return (iota(shape, 1) // SPACE_HEAD_WIDTH == iota(shape, 0)).astype(f32)


def spread(per_head, width):
    return dot(per_head, head_lanes(width), highest)


def head_sums(value):
    return dot_nt(value, head_lanes(value.shape[1]), highest)


def turn(value, cosine, sine, sign):
    lane = iota(value.shape, 1)
    partner = jnp.where(
        lane % HEAD_WIDTH < HEAD_WIDTH // 2,
        -sign * pltpu.roll(value, LANES - HEAD_WIDTH // 2, 1),
        sign * pltpu.roll(value, HEAD_WIDTH // 2, 1),
    )
    return value * cosine + partner * sine


def put_columns(out_ref, value, rows=None):
    out_ref[...] = value


def run(body, outs, args, smem=(), scratch=(), flops=10**9, name=None):
    moved = sum(a.size * a.dtype.itemsize for a in args)
    moved += sum(o.size * o.dtype.itemsize for o in outs)
    result = pl.pallas_call(
        body,
        out_shape=tuple(outs),
        in_specs=[
            pl.BlockSpec(memory_space=pltpu.SMEM if i in smem else pltpu.VMEM)
            for i in range(len(args))
        ],
        out_specs=tuple(pl.BlockSpec(memory_space=pltpu.VMEM) for _ in outs),
        scratch_shapes=list(scratch),
        cost_estimate=pl.CostEstimate(flops=flops, bytes_accessed=moved, transcendentals=0),
        name=name,
    )(*args)
    return result


def arr(rows, columns, kind):
    return jax.ShapeDtypeStruct((rows, columns), kind)


def passed_along(block, axis, distance):
    devices = range(lax.axis_size(axis))
    route = [(i - distance, i) for i in devices if i - distance in devices]
    return lax.ppermute(block, axis, route)


def swap(block, axis, bit):
    route = [(i, i ^ bit) for i in range(lax.axis_size(axis))]
    return lax.ppermute(block, axis, route)


def gather_shards(own):
    half = own.shape[0] // 2
    from_x = swap(own, "fsdp", 1)
    from_y = swap(own, "fsdp", 2)
    top = swap(from_x[:half], "fsdp", 2)
    low = swap(from_y[half:], "fsdp", 1)
    return (own, from_x, from_y, top, low)


def piece_columns(pieces):
    at = 0
    spans = []
    for piece in pieces:
        spans.append((at, at + piece.shape[0]))
        at += piece.shape[0]
    return spans


def grad_shapes(columns):
    half = BLOCK // 2
    return [arr(BLOCK, columns, bf16)] + [arr(half, columns, bf16)] * 6


def store_grad(refs, columns, left, right):
    refs[0][:, columns] = dot_tn(left[:, :BLOCK], right).astype(bf16)
    for k in range(1, SHARDS):
        value = dot_tn(left[:, k * BLOCK : (k + 1) * BLOCK], right).astype(bf16)
        refs[2 * k - 1][:, columns] = value[: BLOCK // 2]
        refs[2 * k][:, columns] = value[BLOCK // 2 :]


def plus_kernel(a_ref, b_ref, out_ref):
    out_ref[...] = (a_ref[...].astype(f32) + b_ref[...].astype(f32)).astype(bf16)


def plus(left, right):
    return run(plus_kernel, [arr(*left.shape, bf16)], (left, right), flops=left.size, name="plus")[0]


def split_store(total, bit, kept_ref, sent_ref):
    half = total.shape[0] // 2
    upper = (lax.axis_index("context") & bit) != 0

    @pl.when(upper)
    def _():
        kept_ref[...] = total[half:]
        sent_ref[...] = total[:half]

    @pl.when(jnp.logical_not(upper))
    def _():
        kept_ref[...] = total[:half]
        sent_ref[...] = total[half:]


def own_kernel(bit, own_ref, x0_ref, x1_ref, y0_ref, y1_ref, *out_refs):
    half = own_ref.shape[0] // 2
    parts = []
    for k, (x_ref, y_ref) in enumerate(((x0_ref, y0_ref), (x1_ref, y1_ref))):
        parts.append(
            own_ref[k * half : (k + 1) * half].astype(f32)
            + x_ref[...].astype(f32)
            + y_ref[...].astype(f32)
        )
    total = jnp.concatenate(parts, axis=0).astype(bf16)
    if bit:
        split_store(total, bit, *out_refs)
    else:
        out_refs[0][...] = total


def halve_kernel(bit, kept_ref, got_ref, *out_refs):
    total = (kept_ref[...].astype(f32) + got_ref[...].astype(f32)).astype(bf16)
    if bit:
        split_store(total, bit, *out_refs)
    else:
        out_refs[0][...] = total


def join_kernel(bit, own_ref, other_ref, out_ref):
    upper = (lax.axis_index("context") & bit) != 0
    own, other = own_ref[...], other_ref[...]
    out_ref[...] = jnp.concatenate(
        [jnp.where(upper, other, own), jnp.where(upper, own, other)], axis=0
    )


def last_kernel(bit, widths, own_ref, other_ref, *out_refs):
    half = own_ref.shape[0]
    upper = (lax.axis_index("context") & bit) != 0
    own, other = own_ref[...].astype(f32), other_ref[...].astype(f32)
    low, high = jnp.where(upper, other, own), jnp.where(upper, own, other)
    at = 0
    for out_ref, width in zip(out_refs, widths, strict=True):
        out_ref[:half] = low[:, at : at + width]
        out_ref[half:] = high[:, at : at + width]
        at += width


def reduce_grad(blocks, widths):
    own, x0, x1, y0, y1, d0, d1 = blocks
    columns = own.shape[1]
    top = swap(d0, "fsdp", 2)
    low = swap(d1, "fsdp", 1)
    got_x1 = swap(x1, "fsdp", 1)
    got_y0 = swap(y0, "fsdp", 2)
    got_x0 = swap(plus(x0, top), "fsdp", 1)
    got_y1 = swap(plus(y1, low), "fsdp", 2)
    bits = []
    bit = 1
    while bit < lax.axis_size("context"):
        bits.append(bit)
        bit *= 2
    rows = own.shape[0]

    def outs_at(rows):
        return [arr(rows // 2, columns, bf16)] * 2

    kept, sent = run(
        functools.partial(own_kernel, bits[0]),
        outs_at(rows),
        (own, got_x0, got_x1, got_y0, got_y1),
        flops=own.size,
        name="own_sum",
    )
    for i, bit in enumerate(bits):
        got = swap(sent, "context", bit)
        rows //= 2
        if i + 1 < len(bits):
            kept, sent = run(
                functools.partial(halve_kernel, bits[i + 1]),
                outs_at(rows),
                (kept, got),
                flops=own.size,
                name="halve",
            )
        else:
            (total,) = run(
                functools.partial(halve_kernel, 0),
                [arr(rows, columns, bf16)],
                (kept, got),
                flops=own.size,
                name="halve",
            )
    for bit in reversed(bits[1:]):
        other = swap(total, "context", bit)
        rows *= 2
        (total,) = run(
            functools.partial(join_kernel, bit),
            [arr(rows, columns, bf16)],
            (total, other),
            flops=own.size,
            name="join",
        )
    other = swap(total, "context", bits[0])
    return run(
        functools.partial(last_kernel, bits[0], widths),
        [arr(2 * rows, width, f32) for width in widths],
        (total, other),
        flops=own.size,
        name="last",
    )


def sum_small(block):
    for axis in ("fsdp", "context"):
        bit = 1
        while bit < lax.axis_size(axis):
            block = block + swap(block, axis, bit)
            bit *= 2
    return block


def deal_rows(block, shift):
    contexts = lax.axis_size("context")
    pieces = block.reshape(contexts, block.shape[0] // contexts, block.shape[1])
    if contexts > 4:
        dealt = lax.all_to_all(pieces, "context", split_axis=0, concat_axis=0, tiled=True)
        return [jnp.roll(dealt, shift, axis=0).reshape(block.shape)]
    index = lax.axis_index("context")
    got = []
    for k in range(contexts):
        piece = lax.dynamic_index_in_dim(pieces, index ^ k, 0, keepdims=False)
        got.append(swap(piece, "context", k) if k else piece)
    return got


def place_rows(piece_refs, deal_ref, out_ref):
    shard = lax.axis_index("fsdp")
    contexts = len(piece_refs)
    rows = piece_refs[0].shape[0]
    index = lax.axis_index("context")
    shift = deal_ref[0, 0] // rows - index + contexts
    for q in range(contexts):
        source = lax.rem(q - shift + 2 * contexts, contexts) ^ index
        for k in range(contexts):

            @pl.when((source == k) if contexts > 1 else True)
            def _():
                for b in range(SHARDS):
                    at = pl.multiple_of((shard ^ b) * BLOCK, BLOCK)
                    out_ref[q * rows : (q + 1) * rows, b * BLOCK : (b + 1) * BLOCK] = piece_refs[
                        k
                    ][:, pl.ds(at, BLOCK)]


def unplace(out_ref, value):
    shard = lax.axis_index("fsdp")
    for b in range(SHARDS):
        at = pl.multiple_of((shard ^ b) * BLOCK, BLOCK)
        out_ref[:, pl.ds(at, BLOCK)] = value[:, b * BLOCK : (b + 1) * BLOCK]


def relative_row(ref):
    shard = lax.axis_index("fsdp")
    return jnp.concatenate(
        [ref[:, pl.ds(pl.multiple_of((shard ^ b) * BLOCK, BLOCK), BLOCK)] for b in range(SHARDS)],
        axis=1,
    )


GAIN_ROWS = 16


def pack_state(out_ref, state, gain_row):
    rows = state.shape[0]
    diagonal = (iota((GAIN_ROWS, LANES), 0) == iota((GAIN_ROWS, LANES), 1)).astype(f32) * gain_row
    gains = dot(diagonal, jnp.ones((LANES, LANES), f32), highest)
    high = gains.astype(bf16)
    out_ref[:rows] = state.astype(bf16)
    out_ref[rows : rows + GAIN_ROWS] = high
    out_ref[rows + GAIN_ROWS :] = (gains - high.astype(f32)).astype(bf16)


def gains_of(ref):
    rows = ref.shape[0] - 2 * GAIN_ROWS
    return ref[rows : rows + GAIN_ROWS].astype(f32) + ref[rows + GAIN_ROWS :].astype(f32)


def chain_state(near_ref, far_ref):
    rows = near_ref.shape[0] - 2 * GAIN_ROWS
    gains = gains_of(near_ref)
    parts = []
    for h in range(rows // SPACE_HEAD_WIDTH):
        at = slice(h * SPACE_HEAD_WIDTH, (h + 1) * SPACE_HEAD_WIDTH)
        parts.append(near_ref[at].astype(f32) + gains[h : h + 1] * far_ref[at].astype(f32))
    return jnp.concatenate(parts, axis=0)


def chain_kernel(near_ref, far_ref, out_ref):
    rows = near_ref.shape[0] - 2 * GAIN_ROWS
    out_ref[:rows] = chain_state(near_ref, far_ref).astype(bf16)
    gains = gains_of(near_ref) * gains_of(far_ref)
    high = gains.astype(bf16)
    out_ref[rows : rows + GAIN_ROWS] = high
    out_ref[rows + GAIN_ROWS :] = (gains - high.astype(f32)).astype(bf16)


def chain(near, far):
    return run(
        chain_kernel, [arr(*near.shape, bf16)], (near, far), flops=near.size, name="chain"
    )[0]


def relay(packed, direction):
    contexts = lax.axis_size("context")
    near = passed_along(packed, "context", direction)
    distance = 2
    whole = chain(packed, near) if contexts > 2 else packed
    while distance * 2 < contexts:
        far = passed_along(whole, "context", direction * distance)
        near = chain(near, far)
        whole = chain(whole, far)
        distance *= 2
    far = passed_along(whole, "context", direction * distance)
    return near, far


def place_kernel(count, deal_ref, *refs):
    place_rows(refs[:count], deal_ref, refs[count])


def project_kernel(counts, deal_ref, gain_ref, cos_ref, sin_ref, *refs):
    piece_count, shard_count, edges = counts
    piece_refs = refs[:piece_count]
    shard_refs = refs[piece_count : piece_count + shard_count]
    x_ref, normed_ref, q_ref, kv_ref, z_ref, conv_ref, step_ref = refs[piece_count + shard_count :]
    query_end, kv_end, z_end, conv_end, step_end = edges
    place_rows(piece_refs, deal_ref, x_ref)
    x = x_ref[...].astype(f32)
    inverse = lax.rsqrt(jnp.mean(x * x, axis=1, keepdims=True) + epsilon)
    normed_ref[...] = (x * inverse * relative_row(gain_ref)).astype(bf16)

    def product(low, high):
        at = 0
        total = None
        for ref in shard_refs:
            rows = ref.shape[0]
            term = dot(normed_ref[:, at : at + rows], ref[:, low:high])
            total = term if total is None else total + term
            at += rows
        return total

    cosine, sine = cos_ref[...], sin_ref[...]
    query = product(0, query_end)
    for at in range(0, query_end, LANES):
        q_ref[:, at : at + LANES] = turn(query[:, at : at + LANES], cosine, sine, 1.0).astype(bf16)
    kv = product(query_end, kv_end)
    lane = iota(kv.shape, 1)
    kv_ref[...] = jnp.where(lane < HEAD_WIDTH, turn(kv, cosine, sine, 1.0), kv).astype(bf16)
    z_ref[...] = product(kv_end, z_end)
    conv_ref[...] = product(z_end, conv_end).astype(bf16)
    step_ref[...] = jnp.zeros(step_ref.shape, f32)
    step_ref[:, : step_end - conv_end] = product(conv_end, step_end)


def convolve(lens_ref, ext_ref, taps_ref, rows):
    base = first_place(rows)
    places = base + iota((rows, 1), 0)
    offset = places - starts_of(lens_ref, places)
    total = None
    for j in range(KC):
        window = ext_ref[8 - (KC - 1) + j : 8 - (KC - 1) + j + rows]
        if j < KC - 1:
            window = jnp.where(offset >= KC - 1 - j, window, 0.0)
        term = window * taps_ref[j : j + 1]
        total = term if total is None else total + term
    return total


def decays(lens_ref, step_raw, params_ref, rows):
    base = first_place(rows)
    raw = step_raw + params_ref[0:1]
    step = jnp.maximum(raw, 0.0) + jnp.log(1.0 + jnp.exp(-jnp.abs(raw)))
    rate = -jnp.exp(params_ref[1:2])
    lower = (iota((rows, rows), 0) >= iota((rows, rows), 1)).astype(f32)
    cumulative = dot(lower, step * rate, highest)
    places = base + iota((rows, 1), 0)
    start = starts_of(lens_ref, places)
    carry = jnp.where(start < base, jnp.exp(cumulative), 0.0)
    last_start = starts_of(lens_ref, base + rows - 1)
    last = cumulative[rows - 1 : rows]
    tail = jnp.where(places >= last_start, jnp.exp(last - cumulative), 0.0)
    return raw, step, rate, cumulative, carry, tail


def joined_mask(lens_ref, rows):
    base = first_place(rows)
    start = starts_of(lens_ref, base + iota((rows, 1), 0)) - base
    key = iota((rows, rows), 1)
    return (key <= iota((rows, rows), 0)) & (key >= start)


def head_decay(h, cum_ref, cum_t_ref, masked):
    lane = iota(cum_ref.shape, 1)
    column = jnp.sum(jnp.where(lane == h, cum_ref[...], 0.0), axis=1, keepdims=True)
    return jnp.exp(column - cum_t_ref[pl.ds(h, 1), :] + masked)


def space_kernel(
    lens_ref,
    conv_ref,
    halo_ref,
    step_ref,
    taps_ref,
    params_ref,
    act_ref,
    y_ref,
    packed_ref,
    cum_ref,
    ext_ref,
    scaled_ref,
    cum_t_ref,
    inner_ref,
    mask_ref,
):
    rows, width = conv_ref.shape
    inner = width - 2 * STATE_WIDTH
    ext_ref[0:8] = halo_ref[...].astype(f32)
    ext_ref[8:] = conv_ref[...].astype(f32)
    before = convolve(lens_ref, ext_ref, taps_ref, rows)
    act_ref[...] = before * sigmoid(before)
    raw, step, rate, cumulative, carry, tail = decays(lens_ref, step_ref[...], params_ref, rows)
    cum_ref[...] = cumulative
    cum_t_ref[...] = jnp.transpose(cumulative)
    u = act_ref[:, :inner]
    scaled = u * spread(step, inner)
    scaled_ref[...] = scaled.astype(bf16)
    bmat = act_ref[:, inner : inner + STATE_WIDTH].astype(bf16)
    cmat = act_ref[:, inner + STATE_WIDTH :].astype(bf16)
    tailed = (scaled * spread(tail, inner)).astype(bf16)
    pack_state(packed_ref, dot_tn(tailed, bmat), carry[rows - 1 : rows])
    inner_ref[...] = dot_nt(cmat, bmat)
    mask_ref[...] = jnp.where(joined_mask(lens_ref, rows), 0.0, masked_value)
    y_ref[...] = spread(params_ref[...], inner)[2:3] * u

    def pair(p, carried):
        at = pl.multiple_of(p * LANES, LANES)
        block = scaled_ref[:, pl.ds(at, LANES)]
        outs = []
        for i in range(2):
            decay = head_decay(2 * p + i, cum_ref, cum_t_ref, mask_ref[...])
            outs.append(dot((decay * inner_ref[...]).astype(bf16), block))
        lane = iota((rows, LANES), 1)
        y_ref[:, pl.ds(at, LANES)] += jnp.where(lane < SPACE_HEAD_WIDTH, outs[0], outs[1])
        return carried

    lax.fori_loop(0, inner // LANES, pair, 0)


def gate_kernel(
    lens_ref, near_ref, far_ref, act_ref, y_ref, cum_ref, z_ref, state_ref, carried_ref, ssm_ref, square_ref
):
    rows, inner = y_ref.shape
    state = chain_state(near_ref, far_ref).astype(bf16)
    state_ref[...] = state
    cmat = act_ref[:, inner + STATE_WIDTH :].astype(bf16)
    carried = dot_nt(cmat, state)
    carried_ref[...] = carried
    base = first_place(rows)
    start = starts_of(lens_ref, base + iota((rows, 1), 0))
    carry = jnp.where(start < base, jnp.exp(cum_ref[...]), 0.0)
    ssm_y = y_ref[...] + spread(carry, inner) * carried
    ssm_ref[...] = ssm_y
    z = z_ref[...]
    gated = ssm_y * z * sigmoid(z)
    square_ref[...] = jnp.broadcast_to(jnp.sum(gated * gated, axis=1, keepdims=True), (rows, LANES))


def mix_kernel(
    attended_ref, ssm_ref, z_ref, square_ref, other_ref, gain_ref, *refs
):
    shard_refs, (both_ref, part_ref) = refs[:-2], refs[-2:]
    width = attended_ref.shape[1]
    z = z_ref[...]
    gated = ssm_ref[...] * z * sigmoid(z)
    inverse = lax.rsqrt((square_ref[:, :1] + other_ref[:, :1]) / DI + epsilon)
    both_ref[:, :width] = attended_ref[...]
    both_ref[:, width:] = (gated * inverse * gain_ref[...]).astype(bf16)
    at = 0
    for ref in shard_refs:
        part_ref[:, at : at + ref.shape[0]] = dot_nt(both_ref[...], ref[...])
        at += ref.shape[0]


def hidden_kernel(x_ref, part_ref, other_ref, gain_ref, *refs):
    shard_refs = refs[:-4]
    mixer_ref, normed_ref, gate_ref, up_ref = refs[-4:]
    mixer = part_ref[...] + other_ref[...]
    mixer_ref[...] = mixer
    resid = x_ref[...].astype(f32) + mixer
    inverse = lax.rsqrt(jnp.mean(resid * resid, axis=1, keepdims=True) + epsilon)
    normed_ref[...] = (resid * inverse * relative_row(gain_ref)).astype(bf16)
    width = gate_ref.shape[1]
    for out_ref, low in ((gate_ref, 0), (up_ref, width)):
        at = 0
        total = None
        for ref in shard_refs:
            rows = ref.shape[0]
            term = dot(normed_ref[:, at : at + rows], ref[:, low : low + width])
            total = term if total is None else total + term
            at += rows
        out_ref[...] = total


def down_kernel(counts, gate_ref, up_ref, cot_ref, *refs):
    count = counts
    gate_up_refs, down_refs = refs[:count], refs[count : 2 * count]
    hidden_ref, pair_ref, part_ref, back_ref = refs[2 * count :]
    width = gate_ref.shape[1]
    gate = gate_ref[...]
    up = up_ref[...]
    sig = sigmoid(gate)
    silu = gate * sig
    hidden_ref[...] = (silu * up).astype(bf16)
    at = 0
    grad_hidden = None
    for ref in down_refs:
        rows = ref.shape[0]
        term = dot(cot_ref[:, at : at + rows], ref[...])
        grad_hidden = term if grad_hidden is None else grad_hidden + term
        at += rows
    pair_ref[:, :width] = (grad_hidden * up * sig * (1.0 + gate * (1.0 - sig))).astype(bf16)
    pair_ref[:, width:] = (grad_hidden * silu).astype(bf16)
    at = 0
    for ref, down in zip(gate_up_refs, down_refs, strict=True):
        rows = ref.shape[0]
        back_ref[:, at : at + rows] = dot_nt(pair_ref[...], ref[...])
        part_ref[:, at : at + rows] = dot_nt(hidden_ref[...], down[...])
        at += rows


def final_kernel(x_ref, mixer_ref, part_ref, other_ref, out_ref, stats_ref):
    mixer = mixer_ref[...]
    ff_part = part_ref[...] + other_ref[...]
    final = x_ref[...].astype(f32) + mixer + ff_part
    unplace(out_ref, final.astype(bf16))
    lane = iota((8, LANES), 1)
    stats = jnp.zeros((8, LANES), f32)
    for i, value in enumerate((final, mixer, ff_part)):
        total = jnp.sum(jnp.sum(value * value, axis=0, keepdims=True), axis=1, keepdims=True)
        stats = jnp.where(lane == i, total, stats)
    stats_ref[...] = stats


def head_pair(ref, h, rows):
    at = h // 2 * LANES
    lane = iota((rows, LANES), 1)
    mine = (lane < HEAD_WIDTH) if h % 2 == 0 else (lane >= HEAD_WIDTH)
    value = ref[:, at : at + LANES]
    return jnp.where(mine, value, jnp.zeros_like(value))


def doubled(kv):
    lane = iota(kv.shape, 1)
    wide = kv.astype(f32)
    turned = pltpu.roll(wide, HEAD_WIDTH, 1)
    keys = jnp.where(lane < HEAD_WIDTH, wide, turned).astype(bf16)
    values = jnp.where(lane < HEAD_WIDTH, turned, wide).astype(bf16)
    return keys, values


def allowed_mask(lens_ref, rows, key_base):
    places = first_place(rows) + iota((rows, 1), 0)
    start = starts_of(lens_ref, places)
    key = key_base + iota((rows, rows), 1)
    return (key <= places) & (key >= start)


def over_blocks(lens_ref, rows, kv_refs, body, skipped):
    base = first_place(rows)
    first_start = starts_of(lens_ref, base)
    if len(kv_refs) == 1 and len(kv_refs[0].shape) == 3:

        def step(k, carried):
            key_base = k * rows
            seen = (key_base <= base) & (key_base + rows > first_start)

            @pl.when(seen)
            def _():
                body(k, kv_refs[0][k], key_base)

            @pl.when(jnp.logical_not(seen))
            def _():
                skipped(k)

            return carried

        lax.fori_loop(0, kv_refs[0].shape[0], step, 0)
        return
    for k, ref in enumerate(kv_refs):
        key_base = base - k * rows
        seen = (key_base >= 0) & (key_base + rows > first_start)

        @pl.when(seen)
        def _():
            body(k, ref[...], key_base)

        @pl.when(jnp.logical_not(seen))
        def _():
            skipped(k)


def attend_kernel(count, lens_ref, q_ref, *refs):
    kv_refs = refs[:count]
    out_ref, exact_ref, log_ref, max_ref, sum_ref, acc_ref = refs[count:]
    rows, width = q_ref.shape
    heads = width // HEAD_WIDTH
    max_ref[...] = jnp.full(max_ref.shape, masked_value, f32)
    sum_ref[...] = jnp.zeros(sum_ref.shape, f32)
    acc_ref[...] = jnp.zeros(acc_ref.shape, f32)

    def body(k, kv, key_base):
        keys, values = doubled(kv)
        allowed = allowed_mask(lens_ref, rows, key_base)
        for h in range(heads):
            scores = dot_nt(head_pair(q_ref, h, rows), keys) * HEAD_WIDTH**-0.5
            scores = jnp.where(allowed, scores, masked_value)
            old = max_ref[h]
            new = jnp.maximum(old, jnp.max(scores, axis=1, keepdims=True))
            weights = jnp.where(allowed, jnp.exp(scores - new[:, :1]), 0.0)
            scale = jnp.exp(old - new)
            max_ref[h] = new
            sum_ref[h] = sum_ref[h] * scale + jnp.sum(weights, axis=1, keepdims=True)
            acc_ref[h] = acc_ref[h] * scale + dot(weights.astype(bf16), values)

    over_blocks(lens_ref, rows, kv_refs, body, lambda k: None)
    lane = iota((rows, LANES), 1)
    for pair in range(heads // 2):
        halves = []
        for h in (2 * pair, 2 * pair + 1):
            log_ref[h] = max_ref[h] + jnp.log(sum_ref[h])
            halves.append(acc_ref[h] / sum_ref[h])
        value = jnp.where(lane < HEAD_WIDTH, halves[0], halves[1])
        exact_ref[:, pair * LANES : (pair + 1) * LANES] = value
        out_ref[:, pair * LANES : (pair + 1) * LANES] = value.astype(bf16)


def attend_back_kernel(count, lens_ref, q_ref, grad_ref, exact_ref, log_ref, cos_ref, sin_ref, *refs):
    kv_refs = refs[:count]
    query_ref = refs[count]
    kv_grad_refs = refs[count + 1 : -2]
    delta_ref, acc_ref = refs[-2:]
    rows, width = q_ref.shape
    heads = width // HEAD_WIDTH
    scale = HEAD_WIDTH**-0.5
    acc_ref[...] = jnp.zeros(acc_ref.shape, f32)
    lane = iota((rows, LANES), 1)
    for h in range(heads):
        at = h // 2 * LANES
        product = head_pair(grad_ref, h, rows).astype(f32) * exact_ref[:, at : at + LANES]
        delta_ref[h] = jnp.broadcast_to(jnp.sum(product, axis=1, keepdims=True), (rows, LANES))

    def store(k, value):
        if len(kv_grad_refs) == 1 and len(kv_grad_refs[0].shape) == 3:
            kv_grad_refs[0][k] = value.astype(kv_grad_refs[0].dtype)
        else:
            kv_grad_refs[k][...] = value.astype(kv_grad_refs[k].dtype)

    def body(k, kv, key_base):
        keys, values = doubled(kv)
        allowed = allowed_mask(lens_ref, rows, key_base)
        grad_keys = jnp.zeros((rows, LANES), f32)
        grad_values = jnp.zeros((rows, LANES), f32)
        for h in range(heads):
            query = head_pair(q_ref, h, rows)
            grad = head_pair(grad_ref, h, rows)
            scores = dot_nt(query, keys) * scale
            probs = jnp.where(allowed, jnp.exp(scores - log_ref[h][:, :1]), 0.0)
            grad_probs = dot_nt(grad, values)
            grad_scores = (probs * (grad_probs - delta_ref[h][:, :1])).astype(bf16)
            acc_ref[h] += dot(grad_scores, keys)
            grad_keys += dot_tn(grad_scores, query)
            grad_values += dot_tn(probs.astype(bf16), grad)
        grad_keys = (grad_keys + pltpu.roll(grad_keys, HEAD_WIDTH, 1)) * scale
        grad_values = grad_values + pltpu.roll(grad_values, HEAD_WIDTH, 1)
        store(k, jnp.where(lane < HEAD_WIDTH, grad_keys, grad_values))

    over_blocks(
        lens_ref, rows, kv_refs, body, lambda k: store(k, jnp.zeros((rows, LANES), f32))
    )
    for pair in range(heads // 2):
        value = jnp.where(lane < HEAD_WIDTH, acc_ref[2 * pair], acc_ref[2 * pair + 1]) * scale
        query_ref[:, pair * LANES : (pair + 1) * LANES] = turn(
            value, cos_ref[...], sin_ref[...], -1.0
        ).astype(bf16)


def norm_back(grad, value, inverse):
    return inverse * grad - value * (inverse * inverse * inverse) * jnp.mean(
        grad * value, axis=1, keepdims=True
    )


def resid_back_kernel(
    back_ref, other_ref, x_ref, mixer_ref, cot_ref, gain_ref, ssm_ref, z_ref, square_ref,
    square_other_ref, ssm_gain_ref, *refs
):
    shard_refs = refs[:-6]
    resid_ref, low_ref, attended_ref, mixed_ref, inner_ref, gains_ref = refs[-6:]
    rows = x_ref.shape[0]
    grad_normed = back_ref[...] + other_ref[...]
    resid = x_ref[...].astype(f32) + mixer_ref[...]
    inverse = lax.rsqrt(jnp.mean(resid * resid, axis=1, keepdims=True) + epsilon)
    ff_gain = jnp.sum(grad_normed * (resid * inverse), axis=0, keepdims=True)
    grad_resid = cot_ref[...].astype(f32) + norm_back(
        grad_normed * relative_row(gain_ref), resid, inverse
    )
    resid_ref[...] = grad_resid
    low_ref[...] = grad_resid.astype(bf16)
    width = attended_ref.shape[1]
    at = 0
    total = None
    for ref in shard_refs:
        count = ref.shape[0]
        term = dot(low_ref[:, at : at + count], ref[...])
        total = term if total is None else total + term
        at += count
    attended_ref[...] = total[:, :width].astype(bf16)
    grad_mixed = total[:, width:]
    mixed_ref[...] = grad_mixed
    z = z_ref[...]
    gated = ssm_ref[...] * z * sigmoid(z)
    gated_inverse = lax.rsqrt((square_ref[:, :1] + square_other_ref[:, :1]) / DI + epsilon)
    inner = jnp.sum(grad_mixed * ssm_gain_ref[...] * gated, axis=1, keepdims=True)
    inner_ref[...] = jnp.broadcast_to(inner, (rows, LANES))
    gains_ref[0:1] = ff_gain
    gains_ref[1:2, : grad_mixed.shape[1]] = jnp.sum(
        grad_mixed * (gated * gated_inverse), axis=0, keepdims=True
    )


def gate_back_kernel(
    lens_ref, mixed_ref, inner_ref, inner_other_ref, square_ref, square_other_ref, ssm_gain_ref,
    ssm_ref, z_ref, carried_ref, act_ref, cum_ref, state_ref,
    out_ref, z_grad_ref, packed_ref, cmat_ref, carry_ref,
):
    rows, inner = ssm_ref.shape
    z = z_ref[...]
    sig = sigmoid(z)
    ssm_y = ssm_ref[...]
    gated = ssm_y * z * sig
    inverse = lax.rsqrt((square_ref[:, :1] + square_other_ref[:, :1]) / DI + epsilon)
    total = (inner_ref[:, :1] + inner_other_ref[:, :1]) / DI
    grad_gated = inverse * (mixed_ref[...] * ssm_gain_ref[...]) - gated * (
        inverse * inverse * inverse * total
    )
    grad_out = grad_gated * (z * sig)
    out_ref[...] = grad_out
    z_grad_ref[...] = (grad_gated * ssm_y * sig * (1.0 + z * (1.0 - sig))).astype(bf16)
    base = first_place(rows)
    start = starts_of(lens_ref, base + iota((rows, 1), 0))
    carry = jnp.where(start < base, jnp.exp(cum_ref[...]), 0.0)
    weighted = (spread(carry, inner) * grad_out).astype(bf16)
    cmat = act_ref[:, inner + STATE_WIDTH :].astype(bf16)
    pack_state(packed_ref, dot_tn(weighted, cmat), carry[rows - 1 : rows])
    cmat_ref[...] = dot(weighted, state_ref[...])
    carry_ref[...] = head_sums(grad_out * carried_ref[...])


def space_back_kernel(
    lens_ref, grad_ref, act_ref, cum_ref, step_ref, params_ref, scaled_grad_ref, grad_inner_ref,
    scaled_ref, cum_t_ref, inner_ref, mask_ref, low_ref,
):
    rows, inner = grad_ref.shape
    raw = step_ref[...] + params_ref[0:1]
    step = jnp.maximum(raw, 0.0) + jnp.log(1.0 + jnp.exp(-jnp.abs(raw)))
    cum_t_ref[...] = jnp.transpose(cum_ref[...])
    scaled_ref[...] = (act_ref[:, :inner] * spread(step, inner)).astype(bf16)
    bmat = act_ref[:, inner : inner + STATE_WIDTH].astype(bf16)
    cmat = act_ref[:, inner + STATE_WIDTH :].astype(bf16)
    inner_ref[...] = dot_nt(cmat, bmat)
    mask_ref[...] = jnp.where(joined_mask(lens_ref, rows), 0.0, masked_value)
    low_ref[...] = grad_ref[...].astype(bf16)
    grad_inner_ref[...] = jnp.zeros(grad_inner_ref.shape, f32)

    def pair(p, carried):
        at = pl.multiple_of(p * LANES, LANES)
        block = scaled_ref[:, pl.ds(at, LANES)]
        grad = low_ref[:, pl.ds(at, LANES)]
        lane = iota((rows, LANES), 1)
        outs = []
        for i in range(2):
            decay = head_decay(2 * p + i, cum_ref, cum_t_ref, mask_ref[...])
            outs.append(dot_tn((decay * inner_ref[...]).astype(bf16), grad))
            mine = (lane < SPACE_HEAD_WIDTH) if i == 0 else (lane >= SPACE_HEAD_WIDTH)
            grad_inner_ref[...] += decay * dot_nt(
                jnp.where(mine, grad, jnp.zeros_like(grad)), block
            )
        scaled_grad_ref[:, pl.ds(at, LANES)] = jnp.where(
            lane < SPACE_HEAD_WIDTH, outs[0], outs[1]
        )
        return carried

    lax.fori_loop(0, inner // LANES, pair, 0)


def conv_back_kernel(
    lens_ref, near_ref, far_ref, grad_ref, scaled_grad_ref, grad_inner_ref, act_ref, y_ref, step_ref,
    conv_ref, halo_ref, taps_ref, params_ref, state_ref, cmat_grad_ref, carry_grad_ref,
    ssm_out_ref, bc_ref, halo_out_ref, halo_bc_ref, step_out_ref, tap_ref, small_ref,
    ext_ref, act_grad_ref,
):
    rows, inner = grad_ref.shape
    width = conv_ref.shape[1]
    base = first_place(rows)
    raw, step, rate, cumulative, carry, tail = decays(lens_ref, step_ref[...], params_ref, rows)
    state_grad = chain_state(near_ref, far_ref)
    low_state = state_grad.astype(bf16)
    bmat = act_ref[:, inner : inner + STATE_WIDTH].astype(bf16)
    cmat = act_ref[:, inner + STATE_WIDTH :].astype(bf16)
    u = act_ref[:, :inner]
    step_wide = spread(step, inner)
    tail_wide = spread(tail, inner)
    skip_wide = spread(params_ref[...], inner)[2:3]
    scaled = u * step_wide
    out_grad = grad_ref[...]
    from_state = dot_nt(bmat, low_state)
    scaled_local = scaled_grad_ref[...]
    scaled_grad = scaled_local + tail_wide * from_state
    tail_grad = head_sums(scaled * from_state) * tail
    grad_inner = grad_inner_ref[...].astype(bf16)
    act_grad_ref[8 : 8 + rows, :inner] = skip_wide * out_grad + scaled_grad * step_wide
    act_grad_ref[8 : 8 + rows, inner : inner + STATE_WIDTH] = dot_tn(grad_inner, cmat) + dot(
        (tail_wide * scaled).astype(bf16), low_state
    )
    act_grad_ref[8 : 8 + rows, inner + STATE_WIDTH :] = dot(grad_inner, bmat) + cmat_grad_ref[...]
    step_grad = head_sums(scaled_grad * u)
    local = y_ref[...] - skip_wide * u
    cum_grad = head_sums(
        out_grad.astype(bf16).astype(f32) * local - scaled.astype(bf16).astype(f32) * scaled_local
    )
    cum_grad = cum_grad + carry_grad_ref[...] * carry - tail_grad
    product = state_grad * state_ref[...].astype(f32)
    summed = dot_nt(jnp.ones((8, LANES), f32), product, highest)
    decay_grad = head_sums(summed)[0:1]
    ending = jnp.sum(tail_grad, axis=0, keepdims=True) + decay_grad * carry[rows - 1 : rows]
    upper = (iota((rows, rows), 0) <= iota((rows, rows), 1)).astype(f32)
    log_grad = dot(upper, cum_grad, highest) + ending
    step_grad = step_grad + log_grad * rate
    raw_grad = step_grad * sigmoid(raw)
    step_out_ref[...] = raw_grad.astype(bf16)
    small_ref[...] = jnp.zeros(small_ref.shape, f32)
    small_ref[0:1] = jnp.sum(raw_grad, axis=0, keepdims=True)
    small_ref[1:2] = jnp.sum(log_grad * step, axis=0, keepdims=True) * rate
    small_ref[2:3] = head_sums(jnp.broadcast_to(
        jnp.sum(out_grad * u, axis=0, keepdims=True), (8, inner)))[0:1]
    ext_ref[0:8] = halo_ref[...].astype(f32)
    ext_ref[8:] = conv_ref[...].astype(f32)
    before = convolve(lens_ref, ext_ref, taps_ref, rows)
    sig = sigmoid(before)
    inside = slice(8, 8 + rows)
    act_grad_ref[inside] = act_grad_ref[inside] * (sig * (1.0 + before * (1.0 - sig)))
    act_grad_ref[0:8] = jnp.zeros((8, width), f32)
    act_grad_ref[8 + rows :] = jnp.zeros((8, width), f32)
    tap_ref[...] = jnp.zeros(tap_ref.shape, f32)
    total = None
    for j in range(KC):
        back = KC - 1 - j
        places = base + iota((rows + 8, 1), 0) - 8 + back
        seen = places - starts_of(lens_ref, places) >= back
        window = jnp.where(seen, act_grad_ref[back : back + rows + 8], 0.0)
        term = window * taps_ref[j : j + 1]
        total = term if total is None else total + term
        tap_ref[j : j + 1] = jnp.sum(
            jnp.where(
                (base + iota((rows, 1), 0)) - starts_of(lens_ref, base + iota((rows, 1), 0)) >= back,
                act_grad_ref[inside],
                0.0,
            )
            * ext_ref[8 - back : 8 - back + rows],
            axis=0,
            keepdims=True,
        )
    ssm_out_ref[...] = total[8:, :inner]
    bc_ref[:rows] = total[8:, inner:]
    bc_ref[rows:] = tap_ref[:, inner:]
    halo_out_ref[...] = total[:8]
    halo_bc_ref[...] = total[:8, inner:]


def inputs_back_kernel(
    counts, ssm_ref, bc_ref, bc_other_ref, halo_ref, halo_bc_ref, step_ref, query_ref, z_ref,
    cos_ref, sin_ref, tap_ref, *refs
):
    kv_count, shard_count, edges = counts
    kv_refs = refs[:kv_count]
    shard_refs = refs[kv_count : kv_count + shard_count]
    early_ref, late_ref, back_ref, taps_ref = refs[kv_count + shard_count :]
    query_end, kv_end, z_end, conv_end, step_end = edges
    rows, inner = ssm_ref.shape
    kv = kv_refs[0][...].astype(f32)
    for ref in kv_refs[1:]:
        kv = kv + ref[...].astype(f32)
    lane = iota(kv.shape, 1)
    early_ref[:, :query_end] = query_ref[...]
    early_ref[:, query_end:kv_end] = jnp.where(
        lane < HEAD_WIDTH, turn(kv, cos_ref[...], sin_ref[...], -1.0), kv
    ).astype(bf16)
    early_ref[:, kv_end:] = z_ref[...]
    pad = jnp.zeros((rows - 8, inner), f32)
    late_ref[:, :inner] = (
        ssm_ref[...] + jnp.concatenate([pad, halo_ref[:, :inner]], axis=0)
    ).astype(bf16)
    bc = bc_ref[:rows] + bc_other_ref[:rows]
    pad = jnp.zeros((rows - 8, 2 * STATE_WIDTH), f32)
    bc_low = (
        bc + jnp.concatenate([pad, halo_ref[:, inner:] + halo_bc_ref[...]], axis=0)
    ).astype(bf16)
    late_ref[:, inner : inner + 2 * STATE_WIDTH] = bc_low
    late_ref[:, inner + 2 * STATE_WIDTH :] = step_ref[:, : step_end - conv_end]
    taps_ref[:, :inner] = tap_ref[:, :inner]
    taps_ref[:, inner:] = bc_ref[rows:] + bc_other_ref[rows:]
    half_bc = (bc_low.astype(f32) * 0.5).astype(bf16)
    at = 0
    for ref in shard_refs:
        count = ref.shape[0]
        total = dot_nt(early_ref[...], ref[:, :z_end])
        total = total + dot_nt(late_ref[:, :inner], ref[:, z_end : z_end + inner])
        total = total + dot_nt(half_bc, ref[:, z_end + inner : conv_end])
        total = total + dot_nt(late_ref[:, inner + 2 * STATE_WIDTH :], ref[:, conv_end:step_end])
        back_ref[:, at : at + count] = total
        at += count


def first_back_kernel(
    x_ref, resid_ref, back_ref, other_ref, gain_ref, gains_ref, taps_ref, small_ref, stats_ref,
    out_ref, sums_ref,
):
    x = x_ref[...].astype(f32)
    inverse = lax.rsqrt(jnp.mean(x * x, axis=1, keepdims=True) + epsilon)
    grad_normed = back_ref[...] + other_ref[...]
    unplace(
        out_ref,
        resid_ref[...] + norm_back(grad_normed * relative_row(gain_ref), x, inverse),
    )
    attn_gain = jnp.sum(grad_normed * (x * inverse), axis=0, keepdims=True)
    sums_ref[...] = jnp.zeros(sums_ref.shape, f32)
    unplace(sums_ref.at[0:1], attn_gain)
    unplace(sums_ref.at[1:2], gains_ref[0:1])
    inner = sums_ref.shape[1] - 2 * STATE_WIDTH
    sums_ref[2 : 2 + KC] = taps_ref[0:KC]
    sums_ref[6:7, :inner] = gains_ref[1:2, :inner]
    sums_ref[6:7, inner : inner + LANES] = small_ref[0:1]
    sums_ref[6:7, inner + LANES :] = small_ref[1:2]
    sums_ref[7:8, :LANES] = small_ref[2:3]
    sums_ref[7:8, LANES : 2 * LANES] = stats_ref[0:1]


def ff_grad_kernel(normed_ref, pair_ref, cot_ref, hidden_ref, *out_refs):
    width = pair_ref.shape[1]
    store_grad(out_refs, slice(0, width), normed_ref[...], pair_ref[...])
    store_grad(
        out_refs, slice(width, width + hidden_ref.shape[1]), cot_ref[...], hidden_ref[...]
    )


def weight_grad_kernel(left_ref, right_ref, *out_refs):
    store_grad(out_refs, slice(0, right_ref.shape[1]), left_ref[...], right_ref[...])


def per_device(
    tokens, lengths, deal, attn_norm_gain, ff_norm_gain, w_query, w_key, w_value, w_attn_out,
    w_gate_z, w_ssm_in, w_bc, w_step, w_ssm_out, conv_ssm, conv_bc, step_bias, decay_log,
    skip_gain, ssm_norm_gain, w_gate, w_up, w_down, cotangent,
):
    rows = tokens.shape[0]
    contexts = lax.axis_size("context")
    tensors = lax.axis_size("tensor")
    query_width = w_query.shape[1]
    inner = w_ssm_in.shape[1]
    heads = inner // SPACE_HEAD_WIDTH
    ff_width = w_gate.shape[1]
    query_end = query_width
    kv_end = query_end + 2 * HEAD_WIDTH
    z_end = kv_end + inner
    conv_end = z_end + inner + 2 * STATE_WIDTH
    step_end = conv_end + heads
    edges = (query_end, kv_end, z_end, conv_end, step_end)
    conv_width = inner + 2 * STATE_WIDTH

    shift = (deal[0, 0] // (rows // contexts) - lax.axis_index("context")) % contexts
    own_inputs = jnp.concatenate(
        [w_query, w_key, w_value, w_gate_z, w_ssm_in, w_bc, w_step], axis=1
    )
    in_shards = gather_shards(own_inputs)
    token_pieces = deal_rows(tokens, shift)
    cot_pieces = deal_rows(cotangent, shift)
    out_shards = gather_shards(jnp.concatenate([w_attn_out, w_ssm_out], axis=1))
    gate_up_shards = gather_shards(jnp.concatenate([w_gate, w_up], axis=1))
    down_shards = gather_shards(w_down)
    attn_gain = attn_norm_gain.reshape(1, D)
    ff_gain = ff_norm_gain.reshape(1, D)
    ssm_gain = ssm_norm_gain.reshape(1, inner)
    taps = jnp.concatenate([conv_ssm, conv_bc], axis=0).T
    params = jnp.pad(jnp.stack([step_bias, decay_log, skip_gain]), ((0, 5), (0, LANES - heads)))

    places = lax.axis_index("context") * rows + jnp.arange(rows, dtype=jnp.int32)
    ends = jnp.cumsum(lengths[0])
    starts = jnp.max(jnp.where(ends[None, :] <= places[:, None], ends[None, :], 0), axis=1)
    half = HEAD_WIDTH // 2
    freqs = rope_base ** (-(jnp.arange(LANES) % half).astype(f32) / half)
    angles = (places - starts).astype(f32)[:, None] * freqs[None, :]
    cosine, sine = jnp.cos(angles), jnp.sin(angles)

    x, normed, query, kv, z, conv_in, step_raw = run(
        functools.partial(project_kernel, (len(token_pieces), len(in_shards), edges)),
        [
            arr(rows, D, bf16), arr(rows, D, bf16), arr(rows, query_width, bf16),
            arr(rows, LANES, bf16), arr(rows, inner, f32), arr(rows, conv_width, bf16),
            arr(rows, LANES, f32),
        ],
        (deal, attn_gain, cosine, sine, *token_pieces, *in_shards),
        smem=(0,), flops=10**9, name="project",
    )
    halo = passed_along(conv_in[rows - 8 :], "context", 1)
    if contexts > 4:
        kv_blocks = [lax.all_gather(kv, "context", axis=0)]
    else:
        kv_blocks = [kv] + [passed_along(kv, "context", k) for k in range(1, contexts)]

    act, y_local, packed, cumulative = run(
        space_kernel,
        [
            arr(rows, conv_width, f32), arr(rows, inner, f32),
            arr(inner + 2 * GAIN_ROWS, LANES, bf16), arr(rows, LANES, f32),
        ],
        (lengths, conv_in, halo, step_raw, taps, params),
        smem=(0,), flops=10**9, name="space",
        scratch=[
            pltpu.VMEM((rows + 8, conv_width), f32), pltpu.VMEM((rows, inner), bf16),
            pltpu.VMEM((LANES, rows), f32), pltpu.VMEM((rows, rows), f32),
            pltpu.VMEM((rows, rows), f32),
        ],
    )
    near, far = relay(packed, 1)
    query_heads = query_width // HEAD_WIDTH
    per_head = jax.ShapeDtypeStruct((query_heads, rows, LANES), f32)
    attended, attended_exact, log_sum = run(
        functools.partial(attend_kernel, len(kv_blocks)),
        [arr(rows, query_width, bf16), arr(rows, query_width, f32), per_head],
        (lengths, query, *kv_blocks),
        smem=(0,), flops=10**9, name="attend",
        scratch=[pltpu.VMEM((query_heads, rows, LANES), f32)] * 3,
    )
    state, carried, ssm_y, square = run(
        gate_kernel,
        [arr(inner, LANES, bf16), arr(rows, inner, f32), arr(rows, inner, f32), arr(rows, LANES, f32)],
        (lengths, near, far, act, y_local, cumulative, z),
        smem=(0,), flops=10**8, name="gate",
    )
    square_other = swap(square, "tensor", 1)
    both, mix_part = run(
        mix_kernel,
        [arr(rows, query_width + inner, bf16), arr(rows, D, f32)],
        (attended, ssm_y, z, square, square_other, ssm_gain, *out_shards),
        flops=10**9, name="mix",
    )
    mix_other = swap(mix_part, "tensor", 1)
    mixer, normed_ff, gate, up = run(
        hidden_kernel,
        [arr(rows, D, f32), arr(rows, D, bf16), arr(rows, ff_width, f32), arr(rows, ff_width, f32)],
        (x, mix_part, mix_other, ff_gain, *gate_up_shards),
        flops=10**9, name="hidden",
    )
    (cot,) = run(
        functools.partial(place_kernel, len(cot_pieces)),
        [arr(rows, D, bf16)],
        (deal, *cot_pieces),
        smem=(0,), flops=10**6, name="place",
    )
    hidden, pair, ff_part, back = run(
        functools.partial(down_kernel, len(down_shards)),
        [
            arr(rows, ff_width, bf16), arr(rows, 2 * ff_width, bf16), arr(rows, D, f32),
            arr(rows, D, f32),
        ],
        (gate, up, cot, *gate_up_shards, *down_shards),
        flops=2 * 10**9, name="down",
    )
    back_other = swap(back, "tensor", 1)
    ff_other = swap(ff_part, "tensor", 1)
    ff_grads = run(
        ff_grad_kernel, grad_shapes(3 * ff_width), (normed_ff, pair, cot, hidden),
        flops=2 * 10**9, name="ff_grad",
    )
    grad_gate, grad_up, grad_down = reduce_grad(ff_grads, [ff_width] * 3)
    output, stats = run(
        final_kernel,
        [arr(rows, D, bf16), arr(8, LANES, f32)],
        (x, mixer, ff_part, ff_other),
        flops=10**7, name="final",
    )

    grad_resid, grad_low, grad_attended, grad_mixed, inner_sum, gain_sums = run(
        resid_back_kernel,
        [
            arr(rows, D, f32), arr(rows, D, bf16), arr(rows, query_width, bf16),
            arr(rows, inner, f32), arr(rows, LANES, f32), arr(8, D, f32),
        ],
        (back, back_other, x, mixer, cot, ff_gain, ssm_y, z, square, square_other, ssm_gain,
         *out_shards),
        flops=10**9, name="resid_back",
    )
    inner_other = swap(inner_sum, "tensor", 1)
    out_grads = run(
        weight_grad_kernel, grad_shapes(query_width + inner), (grad_low, both),
        flops=10**9, name="out_grad",
    )
    grad_attn_out, grad_ssm_out = reduce_grad(out_grads, [query_width, inner])
    out_grad, z_grad, back_packed, cmat_grad, carry_grad = run(
        gate_back_kernel,
        [
            arr(rows, inner, f32), arr(rows, inner, bf16),
            arr(inner + 2 * GAIN_ROWS, LANES, bf16), arr(rows, LANES, f32), arr(rows, LANES, f32),
        ],
        (lengths, grad_mixed, inner_sum, inner_other, square, square_other, ssm_gain, ssm_y, z,
         carried, act, cumulative, state),
        smem=(0,), flops=10**9, name="gate_back",
    )
    near, far = relay(back_packed, -1)
    if contexts > 4:
        kv_grad_shapes = [jax.ShapeDtypeStruct((contexts, rows, LANES), bf16)]
    else:
        kv_grad_shapes = [arr(rows, LANES, f32)] + [arr(rows, LANES, bf16)] * (contexts - 1)
    query_grad, *kv_grads = run(
        functools.partial(attend_back_kernel, len(kv_blocks)),
        [arr(rows, query_width, bf16), *kv_grad_shapes],
        (lengths, query, grad_attended, attended_exact, log_sum, cosine, sine, *kv_blocks),
        smem=(0,), flops=10**9, name="attend_back",
        scratch=[pltpu.VMEM((query_heads, rows, LANES), f32)] * 2,
    )
    if contexts > 4:
        kv_grads = [
            lax.psum_scatter(kv_grads[0], "context", scatter_dimension=0, tiled=False)
        ]
    else:
        kv_grads = [kv_grads[0]] + [
            passed_along(kv_grads[k], "context", -k) for k in range(1, contexts)
        ]
    scaled_grad, grad_inner = run(
        space_back_kernel,
        [arr(rows, inner, f32), arr(rows, rows, f32)],
        (lengths, out_grad, act, cumulative, step_raw, params),
        smem=(0,), flops=10**9, name="space_back",
        scratch=[
            pltpu.VMEM((rows, inner), bf16), pltpu.VMEM((LANES, rows), f32),
            pltpu.VMEM((rows, rows), f32), pltpu.VMEM((rows, rows), f32),
            pltpu.VMEM((rows, inner), bf16),
        ],
    )
    ssm_grad, bc_grad, halo_grad, halo_bc, step_grad, tap_grad, small = run(
        conv_back_kernel,
        [
            arr(rows, inner, f32), arr(rows + 8, 2 * STATE_WIDTH, f32), arr(8, conv_width, f32),
            arr(8, 2 * STATE_WIDTH, f32), arr(rows, LANES, bf16), arr(8, conv_width, f32),
            arr(8, LANES, f32),
        ],
        (lengths, near, far, out_grad, scaled_grad, grad_inner, act, y_local, step_raw, conv_in,
         halo, taps, params, state, cmat_grad, carry_grad),
        smem=(0,), flops=10**9, name="conv_back",
        scratch=[
            pltpu.VMEM((rows + 8, conv_width), f32), pltpu.VMEM((rows + 16, conv_width), f32),
        ],
    )
    bc_other = swap(bc_grad, "tensor", 1)
    halo_next = passed_along(halo_grad, "context", -1)
    cross = [
        ((c + 1) * tensors + t, c * tensors + (t ^ 1))
        for c in range(contexts - 1)
        for t in range(tensors)
    ]
    halo_bc_next = lax.ppermute(halo_bc, ("context", "tensor"), cross)
    early, late, first_part, tap_sums = run(
        functools.partial(inputs_back_kernel, (len(kv_grads), len(in_shards), edges)),
        [
            arr(rows, z_end, bf16), arr(rows, step_end - z_end, bf16), arr(rows, D, f32),
            arr(8, conv_width, f32),
        ],
        (ssm_grad, bc_grad, bc_other, halo_next, halo_bc_next, step_grad, query_grad, z_grad,
         cosine, sine, tap_grad, *kv_grads, *in_shards),
        flops=10**9, name="inputs_back",
    )
    first_other = swap(first_part, "tensor", 1)
    late_grads = run(
        weight_grad_kernel, grad_shapes(step_end - z_end), (normed, late),
        flops=10**9, name="late_grad",
    )
    early_grads = run(
        weight_grad_kernel, grad_shapes(z_end), (normed, early), flops=10**9, name="early_grad",
    )
    grad_query, grad_key, grad_value, grad_z = reduce_grad(
        early_grads, [query_width, HEAD_WIDTH, HEAD_WIDTH, inner]
    )
    grad_ssm_in, grad_bc, grad_step = reduce_grad(late_grads, [inner, 2 * STATE_WIDTH, heads])
    input_grad, sums = run(
        first_back_kernel,
        [arr(rows, D, f32), arr(8, conv_width, f32)],
        (x, grad_resid, first_part, first_other, attn_gain, gain_sums, tap_sums, small, stats),
        flops=10**7, name="first_back",
    )
    sums = sum_small(sums)
    token_count = rows * contexts * lax.axis_size("fsdp")
    rms_stats = jnp.sqrt(sums[7, LANES : LANES + 3] / (token_count * D))
    tap_sums = sums[2 : 2 + KC].T
    return (
        output,
        input_grad,
        sums[0],
        sums[1],
        grad_query,
        grad_key,
        grad_value,
        grad_attn_out,
        grad_z,
        grad_ssm_in,
        grad_bc,
        grad_step,
        grad_ssm_out,
        tap_sums[:inner],
        tap_sums[inner:],
        sums[6, inner : inner + heads],
        sums[6, inner + LANES : inner + LANES + heads],
        sums[7, :heads],
        sums[6, :inner],
        grad_gate,
        grad_up,
        grad_down,
        rms_stats,
    )


def solution(mesh):
    rows = P(("fsdp", "context"), None)
    weight = P("fsdp", "tensor")
    return jax.shard_map(
        per_device,
        mesh=mesh,
        in_specs=(
            rows, P("fsdp", None), P("fsdp", "context"), P(), P(), weight, weight, weight, weight,
            weight, weight, P("fsdp", None), weight, weight, P("tensor", None), P(), P("tensor"),
            P("tensor"), P("tensor"), P("tensor"), weight, weight, weight, rows,
        ),
        out_specs=(
            rows, rows, P(), P(), weight, weight, weight, weight, weight, weight, P("fsdp", None),
            weight, weight, P("tensor", None), P(), P("tensor"), P("tensor"), P("tensor"),
            P("tensor"), weight, weight, weight, P(),
        ),
        check_vma=False,
    )
```

time: 630 us -> 472 us (0.75); the launches traced: 619 us -> 468 us
  Pallas kernels: 0 us -> 176 us
  waiting for transfers between devices: 233 us -> 116 us
  other arithmetic: 110 us -> 4.68 us
  local copies, waits for them, and re-layouts: 116 us -> 49.6 us
  matrix products: 62.2 us -> 0 us
  starting transfers between devices: 75.9 us -> 120 us
  loops' own time: 14.3 us -> 0 us
    pallas_call x0 -> x50, Pallas kernels: none -> 176 us  [run(): pl.pallas_call(body, out_shape=tuple(outs), in_specs=[pl.BlockSpec(memory...]
    ppermute x57 -> x73, waiting for transfers between devices: 189 us -> 102 us  [swap(): return lax.ppermute(block, axis, route)]
    dot_general x31 -> x0, matrix products: 62.2 us -> none  [the longest x3 13.7 us: ssd_local(): jnp.einsum('hts,shp->thp', within * intersection[None], scaled, precision...]
    ppermute x57 -> x73, starting transfers between devices: 47.5 us -> 90.1 us  [swap(): return lax.ppermute(block, axis, route)]
    ppermute x12, waiting for transfers between devices: 44 us -> 14.4 us  [passed_along(): return lax.ppermute(block, axis, route)]
    convert_element_type x31 -> x1, other arithmetic: 27.9 us -> 0.01 us  [per_device(): angles = (places - starts).astype(f32)[:, None] * freqs[None, :]]
    unnamed x441 -> x136, local copies, waits for them, and re-layouts: 42.7 us -> 21.3 us
    reduce_sum x16 -> x0, other arithmetic: 19.9 us -> none  [the longest x2 4.71 us: ssd_local(): local_out = local_out + skip_gain[None, :, None] * scan_inputs]
  transfers between devices with their start and end apart: 69 -> 86, of which waited for: 29 -> 25; matrix products, arithmetic and copies ran while one was open for 42% -> 7% of each run, Pallas kernels for 0% -> 35%
where the time goes in v2:
time: 472 us; the launch traced here: 468 us
  Pallas kernels  176 us (37%)
  starting transfers between devices  120 us (25%)
  waiting for transfers between devices  116 us (25%)
  local copies, waits for them, and re-layouts  49.6 us (11%)
    pallas_call x50, Pallas kernels, run(): pl.pallas_call(body, out_shape=tuple(outs), in_specs=[pl.BlockSpec(memory...  176 us
    ppermute x73, waiting for transfers between devices, swap(): return lax.ppermute(block, axis, route)  102 us
    ppermute x73, starting transfers between devices, swap(): return lax.ppermute(block, axis, route)  90.1 us
    ppermute x12, starting transfers between devices, passed_along(): return lax.ppermute(block, axis, route)  28.7 us
    unnamed x136, local copies, waits for them, and re-layouts  21.3 us
    ppermute x12, waiting for transfers between devices, passed_along(): return lax.ppermute(block, axis, route)  14.4 us
  transfers between devices with their start and end apart: 86, of which 25 were waited for; matrix products, arithmetic and copies ran while one was open for 7% of the time, Pallas kernels for 35%

profile of v2, /device:TPU:0, one launch (start us, length us, event | category | flops | bytes accessed | tf_op | source)
XLA Modules:
  0.0 468.1 jit_solution(6555383403031839612)
XLA Ops:
  21.3 13.8 %collective-permute-done.4 = bf16[256,2188]{0,1:T(8,128)(2,1)S(1)} collective-permute-done((bf16[256,2188]{0,1:T(8,128)(2,1)}, bf16[256,2188]{0,1:T(8,128)(2,1)S(1)}, u32[]{:S(2)}, u32[]{:S(2)}) %collective-permute-start.4) | collective-permute-done | bytes 1120288 | tf_op jit(solution)/shard_map/ppermute | solution.py:126
  45.0 5.1 %collective-permute-done.6 = bf16[128,2188]{0,1:T(8,128)(2,1)} collective-permute-done((bf16[128,2188]{0,1:T(8,128)(2,1)}, bf16[128,2188]{0,1:T(8,128)(2,1)}, u32[]{:S(2)}, u32[]{:S(2)}) %collective-permute-start.6) | collective-permute-done | bytes 560160 | tf_op jit(solution)/shard_map/ppermute | solution.py:126
  57.9 5.6 %project.1 = (bf16[256,1024]{1,0:T(8,128)(2,1)}, bf16[256,1024]{1,0:T(8,128)(2,1)}, bf16[256,256]{1,0:T(8,128)(2,1)}, bf16[256,128]{1,0:T(8,128)(2,1)}, f32[256,...) custom-call(s32[1,256]{1,0:T(1,128)} %deal_ref.3, f32[1,1024]{1,0:T(1,128)} %bitcast.43, ...), custom_call_target="tpu_custom_call" | custom-call | flops 1000000000 | bytes 7959552 | tf_op jit(solution)/shard_map/project/pallas_call | solution.py:99
  69.8 6.6 %space.1 = (f32[256,1024]{1,0:T(8,128)}, f32[256,768]{1,0:T(8,128)}, bf16[800,128]{1,0:T(8,128)(2,1)}, f32[256,128]{1,0:T(8,128)}) custom-call(s32[1,4]{1,0:T(1,128)} %lens_ref.13, bf16[256,1024]{1,0:T(8,128)(2,1)} %get-tuple-element.144.conv_ref, bf16[8,1024]{1,0:T(8,128)(2,1)} %copy-done.52, f32[256,128]{1,0:T(8,128)} %get-tuple-element.145.step_ref, ...), custom_call_target="tpu_custom_call" | custom-call | flops 1000000000 | bytes 2863120 | tf_op jit(solution)/shard_map/space/pallas_call | solution.py:99
  86.6 6.0 %collective-permute-start.12 = (bf16[800,128]{1,0:T(8,128)(2,1)}, bf16[800,128]{1,0:T(8,128)(2,1)}, u32[]{:S(2)}, u32[]{:S(2)}) collective-permute-start(bf16[800,128]{1,0:T(8,128)(2,1)} %chain.2), channel_id=1, source_target_pairs={{0,4},{2,6},{1,5},{3,7},{8,12},{10,14},{9,13},{11,15},{16,20},{18,... | collective-permute-start | bytes 614408 | tf_op jit(solution)/shard_map/ppermute | solution.py:121
  109.5 15.6 %attend.1 = (bf16[256,256]{1,0:T(8,128)(2,1)}, f32[256,256]{1,0:T(8,128)}, f32[4,256,128]{2,1,0:T(8,128)}) custom-call(s32[1,4]{1,0:T(1,128)} %lens_ref.13, bf16[256,256]{1,0:T(8,128)(2,1)} %get-tuple-element.141.q_ref, bf16[256,128]{1,0:T(8,128)(2,1)} %get-tuple-element.142.refs_0_, bf16[256,128]{1,0:T(8,128)(2,1)} %copy-done.62, ...), custom_call_target="tpu_custom_call" | custom-call | flops 1000000000 | bytes 1310736 | tf_op jit(solution)/shard_map/attend/pallas_call | solution.py:99
  134.8 7.6 %collective-permute-start.25 = (bf16[64,1024]{1,0:T(8,128)(2,1)S(1)}, bf16[64,1024]{1,0:T(8,128)(2,1)S(1)}, u32[]{:S(2)}, u32[]{:S(2)}) collective-permute-start(bf16[64,1024]{1,0:T(8,128)(2,1)S(1)} %get-tuple-element.326), channel_id=1, source_target_pairs={{0,6},{2,4},{4,2},{6,0},{1,7},{3,5},{5,3},{7,1},{8,14},{10,12},{12... | collective-permute-start | bytes 393224 | tf_op jit(solution)/shard_map/ppermute | solution.py:126
  146.1 5.6 %collective-permute-start.24 = (bf16[64,1024]{1,0:T(8,128)(2,1)S(1)}, bf16[64,1024]{1,0:T(8,128)(2,1)S(1)}, u32[]{:S(2)}, u32[]{:S(2)}) collective-permute-start(bf16[64,1024]{1,0:T(8,128)(2,1)S(1)} %get-tuple-element.327), channel_id=1, source_target_pairs={{0,4},{2,6},{4,0},{6,2},{1,5},{3,7},{5,1},{7,3},{8,12},{10,14},{12... | collective-permute-start | bytes 393224 | tf_op jit(solution)/shard_map/ppermute | solution.py:126
  161.4 5.6 %hidden.1 = (f32[256,1024]{1,0:T(8,128)}, bf16[256,1024]{1,0:T(8,128)(2,1)}, f32[256,1024]{1,0:T(8,128)}, f32[256,1024]{1,0:T(8,128)}) custom-call(bf16[256,1024]{1,0:T(8,128)(2,1)} %get-tuple-element.140.x_ref, f32[256,1024]{1,0:T(8,128)} %get-tuple-element.153.part_ref, f32[256,1024]{1,0:T(8,128)} %collective-permute-done.18.other_ref, ...), custom_call_target="tpu_custom_call" | custom-call | flops 1000000000 | bytes 10489856 | tf_op jit(solution)/shard_map/hidden/pallas_call | solution.py:99
  167.9 8.0 %down.1 = (bf16[256,1024]{1,0:T(8,128)(2,1)}, bf16[256,2048]{1,0:T(8,128)(2,1)}, f32[256,1024]{1,0:T(8,128)}, f32[256,1024]{1,0:T(8,128)}) custom-call(f32[256,1024]{1,0:T(8,128)} %get-tuple-element.155.gate_ref, f32[256,1024]{1,0:T(8,128)} %get-tuple-element.156.up_ref, bf16[256,1024]{1,0:T(8,128)(2,1)} %place.1.cot_ref, bf16[256,2048]{1,0:T(8,128)(2,1)} %copy-done.3, ...), custom_call_target="tpu_custom_call" | custom-call | flops 2000000000 | bytes 12582912 | tf_op jit(solution)/shard_map/down/pallas_call | solution.py:99
  175.8 5.8 %ff_grad.1 = (bf16[256,3072]{1,0:T(8,128)(2,1)}, bf16[128,3072]{1,0:T(8,128)(2,1)}, bf16[128,3072]{1,0:T(8,128)(2,1)}, bf16[128,3072]{1,0:T(8,128)(2,1)}, bf16[1...) custom-call(bf16[256,1024]{1,0:T(8,128)(2,1)} %get-tuple-element.240.normed_ref, ...), custom_call_target="tpu_custom_call" | custom-call | flops 2000000000 | bytes 8912896 | tf_op jit(solution)/shard_map/ff_grad/pallas_call | solution.py:99
  185.7 16.6 %collective-permute-done.76.b_ref = bf16[128,3072]{1,0:T(8,128)(2,1)S(1)} collective-permute-done((bf16[128,3072]{1,0:T(8,128)(2,1)}, bf16[128,3072]{1,0:T(8,128)(2,1)S(1)}, u32[]{:S(2)}, u32[]{:S(2)}) %collective-permute-start.76) | collective-permute-done | bytes 786464 | tf_op jit(solution)/shard_map/ppermute | solution.py:126
  211.0 5.8 %resid_back.1 = (f32[256,1024]{1,0:T(8,128)}, bf16[256,1024]{1,0:T(8,128)(2,1)}, bf16[256,256]{1,0:T(8,128)(2,1)}, f32[256,768]{1,0:T(8,128)}, f32[256,128]{1,0:T(8,128)}, /*index=5*/f32[8,1024]{1,0:T(8,128)}) custom-call(f32[256,1024]{1,0:T(8,128)} %get-tuple-element.159.back_ref, f32[256,1024]{1,0:T(8,128)} %copy-done.12, ...), custom_call_target="tpu_custom_call" | custom-call | flops 1000000000 | bytes 10787840 | tf_op jit(solution)/shard_map/resid_back/pallas_call | solution.py:99
  225.4 5.4 %gate_back.1 = (f32[256,768]{1,0:T(8,128)}, bf16[256,768]{1,0:T(8,128)(2,1)}, bf16[800,128]{1,0:T(8,128)(2,1)}, f32[256,128]{1,0:T(8,128)}, f32[256,128]{1,0:T(8,128)}) custom-call(s32[1,4]{1,0:T(1,128)} %lens_ref.13, f32[256,768]{1,0:T(8,128)} %get-tuple-element.161.mixed_ref, f32[256,128]{1,0:T(8,128)} %get-tuple-element.162.inner_ref, ...), custom_call_target="tpu_custom_call" | custom-call | flops 1000000000 | bytes 6695952 | tf_op jit(solution)/shard_map/gate_back/pallas_call | solution.py:99
  234.3 8.5 %collective-permute-done.33.far_ref.near_ref = bf16[800,128]{1,0:T(8,128)(2,1)S(1)} collective-permute-done((bf16[800,128]{1,0:T(8,128)(2,1)}, bf16[800,128]{1,0:T(8,128)(2,1)S(1)}, u32[]{:S(2)}, u32[]{:S(2)}) %collective-permute-start.33) | collective-permute-done | bytes 204832 | tf_op jit(solution)/shard_map/ppermute | solution.py:121
  248.1 6.2 %space_back.1 = (f32[256,768]{1,0:T(8,128)}, f32[256,256]{1,0:T(8,128)}) custom-call(s32[1,4]{1,0:T(1,128)} %lens_ref.13, f32[256,768]{1,0:T(8,128)} %get-tuple-element.166.grad_ref, f32[256,1024]{1,0:T(8,128)} %get-tuple-element.147.act_ref, f32[256,128]{1,0:T(8,128)} %get-tuple-element.149.cum_ref, f32[256,128]{1,0:T(8,128)} %get-tuple-element.145.step_ref, ...), custom_call_target="tpu_custom_call" | custom-call | flops 1000000000 | bytes 3149840 | tf_op jit(solution)/shard_map/space_back/pallas_call | solution.py:99
  262.9 11.0 %conv_back.1 = (f32[256,768]{1,0:T(8,128)}, f32[264,256]{1,0:T(8,128)}, f32[8,1024]{1,0:T(8,128)}, f32[8,256]{1,0:T(8,128)}, bf16[256,128]{1,0:T(8,128)(2,1)}, /*index=5*/f32[8,1024]{1,0:T(8,128)}, f32[8,128]{1,0:T(8,128)}) custom-call(s32[1,4]{1,0:T(1,128)} %lens_ref.13, bf16[800,128]{1,0:T(8,128)(2,1)} %copy-done.14, bf16[800,128]{1,0:T(8,128)(2,1)} %copy-done.40, ...), custom_call_target="tpu_custom_call" | custom-call | flops 1000000000 | bytes 6430736 | tf_op jit(solution)/shard_map/conv_back/pallas_call | solution.py:99
  290.7 6.0 %inputs_back.1 = (bf16[256,1152]{1,0:T(8,128)(2,1)}, bf16[256,1036]{1,0:T(8,128)(2,1)}, f32[256,1024]{1,0:T(8,128)}, f32[8,1024]{1,0:T(8,128)}) custom-call(f32[256,768]{1,0:T(8,128)} %get-tuple-element.171.ssm_ref, f32[264,256]{1,0:T(8,128)} %get-tuple-element.172.bc_ref, f32[264,256]{1,0:T(8,128)} %copy-done.32, f32[8,1024]{1,0:T(8,128)} %copy-done.51, ...), custom_call_target="tpu_custom_call" | custom-call | flops 1000000000 | bytes 9263104 | tf_op jit(solution)/shard_map/inputs_back/pallas_call | solution.py:99
  306.1 7.5 %collective-permute-done.62.got_ref = bf16[128,1024]{1,0:T(8,128)(2,1)S(1)} collective-permute-done((bf16[128,1024]{1,0:T(8,128)(2,1)}, bf16[128,1024]{1,0:T(8,128)(2,1)S(1)}, u32[]{:S(2)}, u32[]{:S(2)}) %collective-permute-start.62) | collective-permute-done | bytes 262176 | tf_op jit(solution)/shard_map/ppermute | solution.py:126
  326.7 4.7 collective-permute-done.48.x1_ref
  331.3 6.4 %collective-permute-done.50.b_ref = bf16[128,1152]{1,0:T(8,128)(2,1)} collective-permute-done((bf16[128,1152]{1,0:T(8,128)(2,1)}, bf16[128,1152]{1,0:T(8,128)(2,1)}, u32[]{:S(2)}, u32[]{:S(2)}) %collective-permute-start.50) | collective-permute-done | bytes 294944 | tf_op jit(solution)/shard_map/ppermute | solution.py:126
  372.7 6.2 %collective-permute-done.72.got_ref = bf16[128,1036]{1,0:T(8,128)(2,1)} collective-permute-done((bf16[128,1036]{1,0:T(8,128)(2,1)}, bf16[128,1036]{1,0:T(8,128)(2,1)}, u32[]{:S(2)}, u32[]{:S(2)}) %collective-permute-start.72) | collective-permute-done | bytes 265248 | tf_op jit(solution)/shard_map/ppermute | solution.py:126
  383.9 6.8 %collective-permute-done.64.other_ref = bf16[64,1024]{1,0:T(8,128)(2,1)} collective-permute-done((bf16[64,1024]{1,0:T(8,128)(2,1)}, bf16[64,1024]{1,0:T(8,128)(2,1)}, u32[]{:S(2)}, u32[]{:S(2)}) %collective-permute-start.64) | collective-permute-done | bytes 131104 | tf_op jit(solution)/shard_map/ppermute | solution.py:126
  455.7 8.2 %collective-permute-done.85.other_ref = bf16[128,3072]{1,0:T(8,128)(2,1)S(1)} collective-permute-done((bf16[128,3072]{1,0:T(8,128)(2,1)}, bf16[128,3072]{1,0:T(8,128)(2,1)S(1)}, u32[]{:S(2)}, u32[]{:S(2)}) %collective-permute-start.85) | collective-permute-done | bytes 786464 | tf_op jit(solution)/shard_map/ppermute | solution.py:126
  (373 shorter events, 281.9 us)
Async XLA Ops:
  7.1 27.9 %collective-permute-start.4 = (bf16[256,2188]{0,1:T(8,128)(2,1)}, bf16[256,2188]{0,1:T(8,128)(2,1)S(1)}, u32[]{:S(2)}, u32[]{:S(2)}) collective-permute-start(bf16[256,2188]{0,1:T(8,128)(2,1)} %copy.72), channel_id=1, source_target_pairs={{0,16},{8,24},{16,0},{24,8},{1,17},{9,25},{17,1},{25,9},{2,18},{10... | collective-permute-start | bytes 3360776 | tf_op jit(solution)/shard_map/ppermute | solution.py:126
  10.1 27.5 %collective-permute-start.3 = (bf16[256,2188]{0,1:T(8,128)(2,1)}, bf16[256,2188]{0,1:T(8,128)(2,1)S(1)}, u32[]{:S(2)}, u32[]{:S(2)}) collective-permute-start(bf16[256,2188]{0,1:T(8,128)(2,1)} %copy.72), channel_id=1, source_target_pairs={{0,8},{8,0},{16,24},{24,16},{1,9},{9,1},{17,25},{25,17},{2,10},{10... | collective-permute-start | bytes 3360776 | tf_op jit(solution)/shard_map/ppermute | solution.py:126
  13.5 43.8 %collective-permute-start.2 = (bf16[64,1024]{1,0:T(8,128)(2,1)}, bf16[64,1024]{1,0:T(8,128)(2,1)S(1)}, u32[]{:S(2)}, u32[]{:S(2)}) collective-permute-start(bf16[64,1024]{1,0:T(8,128)(2,1)} %get-tuple-element.330), channel_id=1, source_target_pairs={{0,6},{2,4},{4,2},{6,0},{1,7},{3,5},{5,3},{7,1},{8,14},{10,12},{12... | collective-permute-start | bytes 393224 | tf_op jit(solution)/shard_map/ppermute | solution.py:126
  17.1 40.2 %collective-permute-start.1 = (bf16[64,1024]{1,0:T(8,128)(2,1)}, bf16[64,1024]{1,0:T(8,128)(2,1)}, u32[]{:S(2)}, u32[]{:S(2)}) collective-permute-start(bf16[64,1024]{1,0:T(8,128)(2,1)} %get-tuple-element.331), channel_id=1, source_target_pairs={{0,4},{2,6},{4,0},{6,2},{1,5},{3,7},{5,1},{7,3},{8,12},{10,14},{12... | collective-permute-start | bytes 393224 | tf_op jit(solution)/shard_map/ppermute | solution.py:126
  17.1 40.2 %collective-permute-start = (bf16[64,1024]{1,0:T(8,128)(2,1)}, bf16[64,1024]{1,0:T(8,128)(2,1)}, u32[]{:S(2)}, u32[]{:S(2)}) collective-permute-start(bf16[64,1024]{1,0:T(8,128)(2,1)} %get-tuple-element.332), channel_id=1, source_target_pairs={{0,2},{2,0},{4,6},{6,4},{1,3},{3,1},{5,7},{7,5},{8,10},{10,8},{12,... | collective-permute-start | bytes 393224 | tf_op jit(solution)/shard_map/ppermute | solution.py:126
  50.1 42.5 %collective-permute-start.15 = (bf16[256,1024]{1,0:T(8,128)(2,1)}, bf16[256,1024]{1,0:T(8,128)(2,1)}, u32[]{:S(2)}, u32[]{:S(2)}) collective-permute-start(bf16[256,1024]{1,0:T(8,128)(2,1)} %constant_dynamic-update-slice_fusion.refs_0_), channel_id=1, source_target_pairs={{0,16},{8,24},{16,0},{24,8},{1,17},{9,25},{17,1},{25,9},{2,18},{10... | collective-permute-start | bytes 1572872 | tf_op jit(solution)/shard_map/ppermute | solution.py:126
  53.7 40.6 %collective-permute-start.14 = (bf16[256,1024]{1,0:T(8,128)(2,1)}, bf16[256,1024]{1,0:T(8,128)(2,1)}, u32[]{:S(2)}, u32[]{:S(2)}) collective-permute-start(bf16[256,1024]{1,0:T(8,128)(2,1)} %constant_dynamic-update-slice_fusion.refs_0_), channel_id=1, source_target_pairs={{0,8},{8,0},{16,24},{24,16},{1,9},{9,1},{17,25},{25,17},{2,10},{10... | collective-permute-start | bytes 1572872 | tf_op jit(solution)/shard_map/ppermute | solution.py:126
  80.7 54.1 %collective-permute-start.20 = (bf16[256,2048]{1,0:T(8,128)(2,1)S(1)}, bf16[256,2048]{1,0:T(8,128)(2,1)S(1)}, u32[]{:S(2)}, u32[]{:S(2)}) collective-permute-start(bf16[256,2048]{1,0:T(8,128)(2,1)S(1)} %constant_dynamic-update-slice_fusion.2.refs_0_), channel_id=1, source_target_pairs={{0,16},{8,24},{16,0},{24,8},{1,17},{9,25},{17,1},{25,9},{2,18},{10... | collective-permute-start | bytes 3145736 | tf_op jit(solution)/shard_map/ppermute | solution.py:126
  81.2 62.0 %collective-permute-start.19 = (bf16[256,2048]{1,0:T(8,128)(2,1)S(1)}, bf16[256,2048]{1,0:T(8,128)(2,1)S(1)}, u32[]{:S(2)}, u32[]{:S(2)}) collective-permute-start(bf16[256,2048]{1,0:T(8,128)(2,1)S(1)} %constant_dynamic-update-slice_fusion.2.refs_0_), channel_id=1, source_target_pairs={{0,8},{8,0},{16,24},{24,16},{1,9},{9,1},{17,25},{25,17},{2,10},{10... | collective-permute-start | bytes 3145736 | tf_op jit(solution)/shard_map/ppermute | solution.py:126
  98.9 26.2 %collective-permute-start.17 = (bf16[128,1024]{1,0:T(8,128)(2,1)}, bf16[128,1024]{1,0:T(8,128)(2,1)S(1)}, u32[]{:S(2)}, u32[]{:S(2)}) collective-permute-start(bf16[128,1024]{1,0:T(8,128)(2,1)} %slice.79), channel_id=1, source_target_pairs={{0,8},{8,0},{16,24},{24,16},{1,9},{9,1},{17,25},{25,17},{2,10},{10... | collective-permute-start | bytes 786440 | tf_op jit(solution)/shard_map/ppermute | solution.py:126
  130.0 30.6 %collective-permute-start.18 = (f32[256,1024]{1,0:T(8,128)}, f32[256,1024]{1,0:T(8,128)}, u32[]{:S(2)}, u32[]{:S(2)}) collective-permute-start(f32[256,1024]{1,0:T(8,128)} %get-tuple-element.153.part_ref), channel_id=1, source_target_pairs={{0,1},{1,0},{2,3},{3,2},{4,5},{5,4},{6,7},{7,6},{8,9},{9,8},{10,11... | collective-permute-start | bytes 3145736 | tf_op jit(solution)/shard_map/ppermute | solution.py:126
  175.8 34.2 %collective-permute-start.31 = (f32[256,1024]{1,0:T(8,128)}, f32[256,1024]{1,0:T(8,128)S(1)}, u32[]{:S(2)}, u32[]{:S(2)}) collective-permute-start(f32[256,1024]{1,0:T(8,128)} %get-tuple-element.159.back_ref), channel_id=1, source_target_pairs={{0,1},{1,0},{2,3},{3,2},{4,5},{5,4},{6,7},{7,6},{8,9},{9,8},{10,11... | collective-permute-start | bytes 3145736 | tf_op jit(solution)/shard_map/ppermute | solution.py:126
  183.6 47.2 %collective-permute-start.78 = (bf16[128,3072]{1,0:T(8,128)(2,1)}, bf16[128,3072]{1,0:T(8,128)(2,1)S(1)}, u32[]{:S(2)}, u32[]{:S(2)}) collective-permute-start(bf16[128,3072]{1,0:T(8,128)(2,1)} %get-tuple-element.246), channel_id=1, source_target_pairs={{0,8},{8,0},{16,24},{24,16},{1,9},{9,1},{17,25},{25,17},{2,10},{10... | collective-permute-start | bytes 2359304 | tf_op jit(solution)/shard_map/ppermute | solution.py:126
  184.6 47.6 %collective-permute-start.79 = (bf16[128,3072]{1,0:T(8,128)(2,1)}, bf16[128,3072]{1,0:T(8,128)(2,1)S(1)}, u32[]{:S(2)}, u32[]{:S(2)}) collective-permute-start(bf16[128,3072]{1,0:T(8,128)(2,1)} %get-tuple-element.247), channel_id=1, source_target_pairs={{0,16},{8,24},{16,0},{24,8},{1,17},{9,25},{17,1},{25,9},{2,18},{10... | collective-permute-start | bytes 2359304 | tf_op jit(solution)/shard_map/ppermute | solution.py:126
  205.6 68.4 %collective-permute-start.77 = (bf16[128,3072]{1,0:T(8,128)(2,1)}, bf16[128,3072]{1,0:T(8,128)(2,1)S(1)}, u32[]{:S(2)}, u32[]{:S(2)}) collective-permute-start(bf16[128,3072]{1,0:T(8,128)(2,1)} %plus.14), channel_id=1, source_target_pairs={{0,8},{8,0},{16,24},{24,16},{1,9},{9,1},{17,25},{25,17},{2,10},{10... | collective-permute-start | bytes 2359304 | tf_op jit(solution)/shard_map/ppermute | solution.py:126
  209.2 66.1 %collective-permute-start.81 = (bf16[128,3072]{1,0:T(8,128)(2,1)}, bf16[128,3072]{1,0:T(8,128)(2,1)}, u32[]{:S(2)}, u32[]{:S(2)}) collective-permute-start(bf16[128,3072]{1,0:T(8,128)(2,1)} %plus.15), channel_id=1, source_target_pairs={{0,16},{8,24},{16,0},{24,8},{1,17},{9,25},{17,1},{25,9},{2,18},{10... | collective-permute-start | bytes 2359304 | tf_op jit(solution)/shard_map/ppermute | solution.py:126
  247.3 26.6 %collective-permute-start.59 = (bf16[128,1024]{1,0:T(8,128)(2,1)}, bf16[128,1024]{1,0:T(8,128)(2,1)}, u32[]{:S(2)}, u32[]{:S(2)}) collective-permute-start(bf16[128,1024]{1,0:T(8,128)(2,1)} %get-tuple-element.215), channel_id=1, source_target_pairs={{0,16},{8,24},{16,0},{24,8},{1,17},{9,25},{17,1},{25,9},{2,18},{10... | collective-permute-start | bytes 786440 | tf_op jit(solution)/shard_map/ppermute | solution.py:126
  286.5 55.7 %collective-permute-start.82 = (bf16[128,3072]{1,0:T(8,128)(2,1)}, bf16[128,3072]{1,0:T(8,128)(2,1)}, u32[]{:S(2)}, u32[]{:S(2)}) collective-permute-start(bf16[128,3072]{1,0:T(8,128)(2,1)} %get-tuple-element.251), channel_id=1, source_target_pairs={{0,2},{2,0},{4,6},{6,4},{1,3},{3,1},{5,7},{7,5},{8,10},{10,8},{12,... | collective-permute-start | bytes 2359304 | tf_op jit(solution)/shard_map/ppermute | solution.py:126
  331.3 73.7 %collective-permute-start.30 = (f32[256,1024]{1,0:T(8,128)S(1)}, f32[256,1024]{1,0:T(8,128)}, u32[]{:S(2)}, u32[]{:S(2)}) collective-permute-start(f32[256,1024]{1,0:T(8,128)S(1)} %copy-done.9), channel_id=1, source_target_pairs={{0,1},{1,0},{2,3},{3,2},{4,5},{5,4},{6,7},{7,6},{8,9},{9,8},{10,11... | collective-permute-start | bytes 3145736 | tf_op jit(solution)/shard_map/ppermute | solution.py:126
  337.8 73.7 %collective-permute-start.41 = (f32[256,1024]{1,0:T(8,128)S(1)}, f32[256,1024]{1,0:T(8,128)S(1)}, u32[]{:S(2)}, u32[]{:S(2)}) collective-permute-start(f32[256,1024]{1,0:T(8,128)S(1)} %copy-done.10), channel_id=1, source_target_pairs={{0,1},{1,0},{2,3},{3,2},{4,5},{5,4},{6,7},{7,6},{8,9},{9,8},{10,11... | collective-permute-start | bytes 3145736 | tf_op jit(solution)/shard_map/ppermute | solution.py:126
  359.7 32.7 %collective-permute-start.83 = (bf16[64,3072]{1,0:T(8,128)(2,1)}, bf16[64,3072]{1,0:T(8,128)(2,1)S(1)}, u32[]{:S(2)}, u32[]{:S(2)}) collective-permute-start(bf16[64,3072]{1,0:T(8,128)(2,1)} %get-tuple-element.253), channel_id=1, source_target_pairs={{0,4},{2,6},{4,0},{6,2},{1,5},{3,7},{5,1},{7,3},{8,12},{10,14},{12... | collective-permute-start | bytes 1179656 | tf_op jit(solution)/shard_map/ppermute | solution.py:126
  392.4 36.4 %collective-permute-start.65 = (bf16[128,1024]{1,0:T(8,128)(2,1)}, bf16[128,1024]{1,0:T(8,128)(2,1)}, u32[]{:S(2)}, u32[]{:S(2)}) collective-permute-start(bf16[128,1024]{1,0:T(8,128)(2,1)} %join.5.own_ref), channel_id=1, source_target_pairs={{0,2},{2,0},{4,6},{6,4},{1,3},{3,1},{5,7},{7,5},{8,10},{10,8},{12,... | collective-permute-start | bytes 786440 | tf_op jit(solution)/shard_map/ppermute | solution.py:126
  395.4 42.1 %collective-permute-start.84 = (bf16[64,3072]{1,0:T(8,128)(2,1)}, bf16[64,3072]{1,0:T(8,128)(2,1)S(1)}, u32[]{:S(2)}, u32[]{:S(2)}) collective-permute-start(bf16[64,3072]{1,0:T(8,128)(2,1)} %halve.15.own_ref), channel_id=1, source_target_pairs={{0,4},{2,6},{4,0},{6,2},{1,5},{3,7},{5,1},{7,3},{8,12},{10,14},{12... | collective-permute-start | bytes 1179656 | tf_op jit(solution)/shard_map/ppermute | solution.py:126
  403.4 30.2 %collective-permute-start.54 = (bf16[64,1152]{1,0:T(8,128)(2,1)}, bf16[64,1152]{1,0:T(8,128)(2,1)}, u32[]{:S(2)}, u32[]{:S(2)}) collective-permute-start(bf16[64,1152]{1,0:T(8,128)(2,1)} %halve.9.own_ref), channel_id=1, source_target_pairs={{0,4},{2,6},{4,0},{6,2},{1,5},{3,7},{5,1},{7,3},{8,12},{10,14},{12... | collective-permute-start | bytes 442376 | tf_op jit(solution)/shard_map/ppermute | solution.py:126
  (126 other events, 1435.3 us)
